TPU v7x, 512 devices: a whole 4x8x8 slice. The times are simulated.
512 devices in a mesh: section: 16 (over y, z_lo), expert: 32 (over z_hi, x, core).
Axes of the slice: x: 4, y: 8, z: 8 (z_hi: 4, z_lo: 2; z = z_hi * 2 + z_lo), core: 2. Of those that a mesh axis runs over, the one named last changes fastest.
Arguments:
- pre_gate_a: bfloat16 [16, 512, 4096], P('section', None, 'expert'), may hold values from -6 to 6
- pre_gate_b: bfloat16 [16, 512, 4096], P('section', None, 'expert'), may hold values from -6 to 6
- pre_up_a: bfloat16 [16, 512, 4096], P('section', None, 'expert'), may hold values from -6 to 6
- pre_up_b: bfloat16 [16, 512, 4096], P('section', None, 'expert'), may hold values from -6 to 6
- grads_a: bfloat16 [16, 2048, 3584], P('section', 'expert'), may hold values from -2 to 2
- grads_b: bfloat16 [16, 2048, 3584], P('section', 'expert'), may hold values from -2 to 2
- route_a: int32 [16, 2048, 1], P('section', 'expert'), may hold values from 0 to 3; in each aligned block of 64 rows (0 to 63, 64 to 127, ..., all dimensions but the last counted through in order) at most 16 rows name the same one
- route_b: int32 [16, 2048, 1], P('section', 'expert'), may hold values from 0 to 3; in each aligned block of 64 rows (0 to 63, 64 to 127, ..., all dimensions but the last counted through in order) at most 16 rows name the same one
- probs_a: float32 [16, 2048, 1], P('section', 'expert'), may hold values from 0.1 to 1
- probs_b: float32 [16, 2048, 1], P('section', 'expert'), may hold values from 0.1 to 1
- w_gate: bfloat16 [16, 3584, 4096], P('section', None, 'expert'), may hold values from -0.09375 to 0.09375
- w_up: bfloat16 [16, 3584, 4096], P('section', None, 'expert'), may hold values from -0.09375 to 0.09375
- w_down: bfloat16 [16, 4096, 3584], P('section', 'expert'), may hold values from -0.1875 to 0.1875
Outputs:
- dx_a: bfloat16 [16, 2048, 3584], P('section', 'expert')
- dx_b: bfloat16 [16, 2048, 3584], P('section', 'expert')
- dprob_a: float32 [16, 2048, 1], P('section', 'expert')
- dprob_b: float32 [16, 2048, 1], P('section', 'expert')
Inputs may be any that keep to these rules, and one draw needn't show every extreme that they name: `route_a`: each token names one expert; among the 64 tokens of one device's block every expert is named exactly 16 times. `route_b`: as for route_a.
All inputs are finite; a program needn't handle non-finite values.
Results may differ from a plain program's by a relative error of at most 0.0085.
Values may be sent and summed in bfloat16 or wider, within the bound.
No kernel may reach another device: no remote copies, remote signals or barrier semaphores. Data moves between devices by JAX's collectives and lax.ppermute only.
A program may use at most 64 MiB of HBM per device.

v0:
```python
import jax
import jax.numpy as jnp
from jax import lax
from jax.experimental import pallas as pl
from jax.experimental.pallas import tpu as pltpu
from jax.sharding import PartitionSpec as P

EXPERTS = 4
CAP = 16
NX = 4
NC = 2
PAD = 128
TILE = 512


def place(z, x, c):
    return z * NX * NC + x * NC + c


def weight_partner(x, c):
    return (((x + c) ^ 1) + NX - c) % NX


def token_partner(x, c):
    return weight_partner(x, 1 - c)


def moved(value, rule):
    pairs = []
    for z in range(EXPERTS):
        for x in range(NX):
            for c in range(NC):
                to_x, to_c = rule(x, c)
                pairs.append((place(z, x, c), place(z, to_x, to_c)))
    return lax.ppermute(value, "expert", pairs)


def to_weight_partner(value):
    return moved(value, lambda x, c: (weight_partner(x, c), c))


def to_sibling(value):
    return moved(value, lambda x, c: (x, 1 - c))


def over_z(value):
    columns = [[place(z, x, c) for z in range(EXPERTS)] for x in range(NX) for c in range(NC)]
    return lax.all_to_all(
        value, "expert", split_axis=0, concat_axis=0, axis_index_groups=columns, tiled=True
    )


def passed_along(value, steps):
    count = lax.axis_size("section")
    pairs = [(source, (source + steps) % count) for source in range(count)]
    return lax.ppermute(value, "section", pairs)


def slots_of(route):
    onehot = (route == jnp.arange(EXPERTS, dtype=jnp.int32)[None, :]).astype(jnp.float32)
    size = onehot.shape[0]
    before = jnp.tril(jnp.ones((size, size), jnp.float32), -1)
    rank = jnp.dot(before, onehot)
    slot = jnp.sum(rank * onehot, axis=-1, keepdims=True).astype(jnp.int32)
    return route * CAP + slot


def table(place_of):
    lanes = jnp.arange(EXPERTS * CAP, dtype=jnp.int32)[None, :]
    return (place_of == lanes).astype(jnp.bfloat16)


def nt(a, b):
    return lax.dot_general(a, b, (((1,), (1,)), ((), ())), preferred_element_type=jnp.float32)


def expert_kernel(
    pos, own, sib, same, cross,
    gate_own, up_own, gate_mate, up_mate,
    wd_own, wd_mate, wg_own, wg_mate, wu_own, wu_mate,
    p_own, p_sib, p_same, p_cross,
    v_rows, v_gate_own, v_up_own, v_gate_mate, v_up_mate, v_wd, v_w, v_out, s_in, s_w, s_out,
):
    x, c, tp = pos[0], pos[1], pos[2]
    n, wide = own.shape
    unit = wd_own.shape[0]
    loads = []
    for k, ref in enumerate((own, sib, same, cross)):
        loads.append((ref, v_rows.at[pl.ds(k * n, n)]))
    loads.append((wd_own, v_wd.at[pl.ds(0, unit)]))
    loads.append((wd_mate, v_wd.at[pl.ds(unit, unit)]))
    loads += [(gate_own, v_gate_own), (up_own, v_up_own), (gate_mate, v_gate_mate), (up_mate, v_up_mate)]
    first = [pltpu.make_async_copy(a, b, s_in.at[k]) for k, (a, b) in enumerate(loads)]
    later = [
        pltpu.make_async_copy(ref, v_w.at[k], s_w.at[k])
        for k, ref in enumerate((wg_own, wg_mate, wu_own, wu_mate))
    ]
    for copy in first + later:
        copy.start()
    for copy in first:
        copy.wait()
    dh = None
    for d in range(0, wide, TILE):
        cut = slice(d, d + TILE)
        term = nt(v_rows[:, cut], v_wd[:, cut])
        dh = term if dh is None else dh + term

    def saved(mine, mate):
        blocks = []
        for slot, xs in ((0, x), (1, tp)):
            for cs in (c, 1 - c):
                for z in range(EXPERTS):
                    blocks.append(
                        jnp.concatenate(
                            [
                                mine[z * NX * NC + xs * NC + cs],
                                mate[(slot * EXPERTS + z) * NC + cs],
                            ],
                            axis=-1,
                        )
                    )
        return jnp.concatenate(blocks, axis=0).astype(jnp.float32)

    gate = saved(v_gate_own, v_gate_mate)
    up = saved(v_up_own, v_up_mate)
    sig = jax.nn.sigmoid(gate)
    act = gate * sig
    slope = sig * (1.0 + gate * (1.0 - sig))
    q = jnp.sum(dh * (act * up), axis=-1, keepdims=True)
    dg = (dh * up * slope).astype(jnp.bfloat16)
    du = (dh * act).astype(jnp.bfloat16)
    both = jnp.concatenate([dg, du], axis=-1)
    v_out[:, wide:] = jnp.broadcast_to(q, (q.shape[0], PAD)).astype(jnp.bfloat16)
    for copy in later:
        copy.wait()
    for d in range(0, wide, TILE):
        cut = slice(d, d + TILE)
        w = jnp.concatenate([v_w[k, cut] for k in range(4)], axis=-1)
        v_out[:, cut] = nt(both, w).astype(jnp.bfloat16)
    stores = [
        pltpu.make_async_copy(v_out.at[pl.ds(k * n, n)], out, s_out.at[k])
        for k, out in enumerate((p_own, p_sib, p_same, p_cross))
    ]
    for copy in stores:
        copy.start()
    for copy in stores:
        copy.wait()


def expert_work(pos, pieces, saved, weights):
    count, wide = pieces[0].shape
    unit = weights[0].shape[0]
    shape = jax.ShapeDtypeStruct((count, wide + PAD), jnp.bfloat16)
    anywhere = pl.BlockSpec(memory_space=pl.ANY)
    bf16 = jnp.bfloat16
    return pl.pallas_call(
        expert_kernel,
        in_specs=[pl.BlockSpec(memory_space=pltpu.SMEM)] + [anywhere] * 14,
        out_specs=[anywhere] * 4,
        out_shape=[shape] * 4,
        scratch_shapes=[
            pltpu.VMEM((4 * count, wide), bf16),
            *[pltpu.VMEM(v.shape, bf16) for v in saved],
            pltpu.VMEM((2 * unit, wide), bf16),
            pltpu.VMEM((4, wide, unit), bf16),
            pltpu.VMEM((4 * count, wide + PAD), bf16),
            pltpu.SemaphoreType.DMA((10,)),
            pltpu.SemaphoreType.DMA((4,)),
            pltpu.SemaphoreType.DMA((4,)),
        ],
        compiler_params=pltpu.CompilerParams(vmem_limit_bytes=32 << 20),
        name="expert_work",
    )(pos, *pieces, *saved, *weights)


def gather_rows(own):
    same = moved(own, lambda x, c: (token_partner(x, c), c))
    cross = moved(own, lambda x, c: (token_partner(x, 1 - c), 1 - c))
    sib = to_sibling(own)
    return own, sib, same, cross


def reduce_rows(p_own, p_sib, p_same, p_cross):
    same = moved(p_same, lambda x, c: (token_partner(x, c), c))
    cross = moved(p_cross, lambda x, c: (token_partner(x, c), 1 - c))
    sib = to_sibling(p_sib)
    total = p_own.astype(jnp.float32) + sib.astype(jnp.float32)
    total = total + same.astype(jnp.float32) + cross.astype(jnp.float32)
    return total.astype(jnp.bfloat16)


def on_device(
    pre_gate_a, pre_gate_b, pre_up_a, pre_up_b, grads_a, grads_b,
    route_a, route_b, probs_a, probs_b, w_gate, w_up, w_down,
):
    upper = passed_along(grads_a[0], -1)
    lower = passed_along(grads_b[0], 1)
    me = lax.axis_index("expert")
    core = me % NC
    x = (me // NC) % NX
    mate = weight_partner(x, core)
    pos = jnp.stack([x, core, token_partner(x, core)]).astype(jnp.int32)
    pre = [v[0].reshape(-1, CAP, v.shape[-1]) for v in (pre_gate_a, pre_up_a, pre_gate_b, pre_up_b)]

    def wanted(v):
        grid = v.reshape(EXPERTS, NX, NC, CAP, v.shape[-1])
        pair = [lax.dynamic_index_in_dim(grid, k, 1, False) for k in (mate, (x + 2) % NX)]
        return jnp.stack(pair)

    weights = []
    for w in (w_down[0], w_gate[0], w_up[0]):
        weights += [w, to_weight_partner(w)]
    far = to_weight_partner(jnp.stack([wanted(v) for v in pre]))
    far = far.reshape(len(pre), -1, CAP, far.shape[-1])

    def handle(arrived, route, probs, saved):
        chosen = table(slots_of(route))
        send = lax.dot_general(
            chosen, arrived, (((0,), (0,)), ((), ())), preferred_element_type=jnp.float32
        ).astype(jnp.bfloat16)
        wide = send.shape[-1]
        own = over_z(send.reshape(EXPERTS, CAP, wide)).reshape(EXPERTS * CAP, wide)
        pieces = gather_rows(own)
        parts = expert_work(pos, pieces, saved, weights)
        total = reduce_rows(*parts)
        back = over_z(total.reshape(EXPERTS, CAP, -1)).reshape(EXPERTS * CAP, -1)
        picked = jnp.dot(chosen, back, preferred_element_type=jnp.float32)
        grad_x = (probs * picked[:, :wide]).astype(jnp.bfloat16)
        return grad_x[None], picked[None, :, wide:wide + 1]

    dx_a, dprob_a = handle(upper, route_a[0], probs_a[0], (pre[0], pre[1], far[0], far[1]))
    dx_b, dprob_b = handle(lower, route_b[0], probs_b[0], (pre[2], pre[3], far[2], far[3]))
    return (dx_a, dx_b, dprob_a, dprob_b)


def solution(mesh):
    hidden = P("section", None, "expert")
    tokens = P("section", "expert", None)

    return jax.shard_map(
        on_device,
        mesh=mesh,
        in_specs=(hidden,) * 4 + (tokens,) * 6 + (hidden, hidden, tokens),
        out_specs=(tokens,) * 4,
        check_vma=False,
    )
```

profile of v0, /device:TPU:24, one launch (start us, length us, event | category | flops | bytes accessed | tf_op | source)
XLA Modules:
  0.0 174.5 jit_solution(7784936329157552307)
XLA Ops:
  0.6 4.4 %collective-permute-start.11 = (bf16[64,3584]{1,0:T(8,128)(2,1)}, bf16[64,3584]{1,0:T(8,128)(2,1)S(1)}, u32[]{:S(2)}, u32[]{:S(2)}) collective-permute-start(bf16[64,3584]{1,0:T(8,128)(2,1)} %bitcast.103), channel_id=1, source_target_pairs={{0,32},{32,64},{64,96},{96,128},{128,160},{160,192},{192,224},{224... | collective-permute-start | bytes 1376264 | tf_op jit(solution)/shard_map/ppermute | solution.py:56
  5.1 3.4 %collective-permute-start.5 = (bf16[128,3584]{1,0:T(8,128)(2,1)}, bf16[128,3584]{1,0:T(8,128)(2,1)}, u32[]{:S(2)}, u32[]{:S(2)}) collective-permute-start(bf16[128,3584]{1,0:T(8,128)(2,1)} %bitcast.68), channel_id=1, source_target_pairs={{0,2},{1,7},{2,0},{3,5},{4,6},{5,3},{6,4},{7,1},{8,10},{9,15},{10,... | collective-permute-start | bytes 2752520 | tf_op jit(solution)/shard_map/ppermute | solution.py:35
  8.5 2.4 %collective-permute-start.6 = (bf16[3584,128]{1,0:T(8,128)(2,1)}, bf16[3584,128]{1,0:T(8,128)(2,1)}, u32[]{:S(2)}, u32[]{:S(2)}) collective-permute-start(bf16[3584,128]{1,0:T(8,128)(2,1)} %bitcast.71), channel_id=1, source_target_pairs={{0,2},{1,7},{2,0},{3,5},{4,6},{5,3},{6,4},{7,1},{8,10},{9,15},{10,... | collective-permute-start | bytes 2752520 | tf_op jit(solution)/shard_map/ppermute | solution.py:35
  10.9 3.4 %collective-permute-start.7 = (bf16[3584,128]{1,0:T(8,128)(2,1)}, bf16[3584,128]{1,0:T(8,128)(2,1)}, u32[]{:S(2)}, u32[]{:S(2)}) collective-permute-start(bf16[3584,128]{1,0:T(8,128)(2,1)} %bitcast.74), channel_id=1, source_target_pairs={{0,2},{1,7},{2,0},{3,5},{4,6},{5,3},{6,4},{7,1},{8,10},{9,15},{10,... | collective-permute-start | bytes 2752520 | tf_op jit(solution)/shard_map/ppermute | solution.py:35
  14.3 2.5 %collective-permute-start = (bf16[64,3584]{1,0:T(8,128)(2,1)}, bf16[64,3584]{1,0:T(8,128)(2,1)S(1)}, u32[]{:S(2)}, u32[]{:S(2)}) collective-permute-start(bf16[64,3584]{1,0:T(8,128)(2,1)} %bitcast.104), channel_id=1, source_target_pairs={{0,480},{32,0},{64,32},{96,64},{128,96},{160,128},{192,160},{224,1... | collective-permute-start | bytes 1376264 | tf_op jit(solution)/shard_map/ppermute | solution.py:56
  16.8 0.9 fusion.1
  17.8 1.4 dynamic-slice_bitcast_fusion.5
  19.9 1.2 convolution_convert_fusion
  21.0 10.4 %all-to-all-start.2 = ((bf16[4,16,3584]{2,1,0:T(8,128)(2,1)}), bf16[4,16,3584]{2,1,0:T(8,128)(2,1)S(1)}, u32[]{:S(2)}, u32[]{:S(2)}) async-start(bf16[4,16,3584]{2,1,0:T(8,128)(2,1)} %bitcast.37), calls=%async_computation.2 | async-start | bytes 917504 | tf_op jit(solution)/shard_map/all_to_all | solution.py:48
  31.5 0.7 copy-done.16
  32.3 0.7 dynamic-slice_bitcast_fusion.1
  33.0 1.2 convolution_convert_fusion.1
  34.2 16.5 %all-to-all-done.2 = bf16[4,16,3584]{2,1,0:T(8,128)(2,1)S(1)} async-done(((bf16[4,16,3584]{2,1,0:T(8,128)(2,1)}), bf16[4,16,3584]{2,1,0:T(8,128)(2,1)S(1)}, u32[]{:S(2)}, u32[]{:S(2)}) %all-to-all-start.2) | async-done | bytes 458784 | tf_op jit(solution)/shard_map/all_to_all | solution.py:48
  50.7 0.8 copy-done.3
  51.4 3.6 %all-to-all-start = ((bf16[4,16,3584]{2,1,0:T(8,128)(2,1)}), bf16[4,16,3584]{2,1,0:T(8,128)(2,1)S(1)}, u32[]{:S(2)}, u32[]{:S(2)}) async-start(bf16[4,16,3584]{2,1,0:T(8,128)(2,1)} %bitcast.6), calls=%async_computation | async-start | bytes 917504 | tf_op jit(solution)/shard_map/all_to_all | solution.py:48
  55.0 0.9 maximum_bitcast_fusion.1
  55.9 0.8 maximum_bitcast_fusion.2
  56.7 0.8 maximum_bitcast_fusion.3
  57.5 1.9 %collective-permute-start.4 = (bf16[4,2,4,2,16,128]{5,4,3,2,1,0:T(8,128)(2,1)S(1)}, bf16[4,2,4,2,16,128]{5,4,3,2,1,0:T(8,128)(2,1)S(1)}, u32[]{:S(2)}, u32[]{:S(2)}) collective-permute-start(bf16[4,2,4,2,16,128]{5,4,3,2,1,0:T(8,128)(2,1)S(1)} %pad_maximum_fusion), channel_id=1, source_target_pairs={{0,2},{1,7},{2,0},{3,5},{4,6},{5,3},{6,4},{7,1},{8,10},{9,15},{10,... | collective-permute-start | bytes 786440 | tf_op jit(solution)/shard_map/ppermute | solution.py:35
  59.4 2.3 %collective-permute-start.12 = (bf16[64,3584]{1,0:T(8,128)(2,1)}, bf16[64,3584]{1,0:T(8,128)(2,1)}, u32[]{:S(2)}, u32[]{:S(2)}) collective-permute-start(bf16[64,3584]{1,0:T(8,128)(2,1)} %bitcast.81), channel_id=1, source_target_pairs={{0,1},{1,0},{2,3},{3,2},{4,5},{5,4},{6,7},{7,6},{8,9},{9,8},{10,11... | collective-permute-start | bytes 1376264 | tf_op jit(solution)/shard_map/ppermute | solution.py:35
  61.8 4.0 %collective-permute-done.4 = bf16[4,2,4,2,16,128]{5,4,3,2,1,0:T(8,128)(2,1)S(1)} collective-permute-done((bf16[4,2,4,2,16,128]{5,4,3,2,1,0:T(8,128)(2,1)S(1)}, bf16[4,2,4,2,16,128]{5,4,3,2,1,0:T(8,128)(2,1)S(1)}, u32[]{:S(2)}, u32[]{:S(2)}) %collective-permute-start.4) | collective-permute-done | bytes 262176 | tf_op jit(solution)/shard_map/ppermute | solution.py:35
  65.8 2.6 %collective-permute-start.13 = (bf16[64,3584]{1,0:T(8,128)(2,1)}, bf16[64,3584]{1,0:T(8,128)(2,1)}, u32[]{:S(2)}, u32[]{:S(2)}) collective-permute-start(bf16[64,3584]{1,0:T(8,128)(2,1)} %bitcast.82), channel_id=1, source_target_pairs={{0,6},{1,3},{2,4},{3,1},{4,2},{5,7},{6,0},{7,5},{8,14},{9,11},{10,... | collective-permute-start | bytes 1376264 | tf_op jit(solution)/shard_map/ppermute | solution.py:35
  68.4 2.7 %collective-permute-start.14 = (bf16[64,3584]{1,0:T(8,128)(2,1)}, bf16[64,3584]{1,0:T(8,128)(2,1)}, u32[]{:S(2)}, u32[]{:S(2)}) collective-permute-start(bf16[64,3584]{1,0:T(8,128)(2,1)} %bitcast.83), channel_id=1, source_target_pairs={{0,3},{1,6},{2,1},{3,4},{4,7},{5,2},{6,5},{7,0},{8,11},{9,14},{10,... | collective-permute-start | bytes 1376264 | tf_op jit(solution)/shard_map/ppermute | solution.py:35
  71.1 3.8 %collective-permute-start.1 = (bf16[64,3584]{1,0:T(8,128)(2,1)S(1)}, bf16[64,3584]{1,0:T(8,128)(2,1)}, u32[]{:S(2)}, u32[]{:S(2)}) collective-permute-start(bf16[64,3584]{1,0:T(8,128)(2,1)S(1)} %bitcast.77), channel_id=1, source_target_pairs={{0,1},{1,0},{2,3},{3,2},{4,5},{5,4},{6,7},{7,6},{8,9},{9,8},{10,11... | collective-permute-start | bytes 1376264 | tf_op jit(solution)/shard_map/ppermute | solution.py:35
  75.0 1.0 fusion.26
  76.0 4.5 %collective-permute-done.13.same = bf16[64,3584]{1,0:T(8,128)(2,1)} collective-permute-done((bf16[64,3584]{1,0:T(8,128)(2,1)}, bf16[64,3584]{1,0:T(8,128)(2,1)}, u32[]{:S(2)}, u32[]{:S(2)}) %collective-permute-start.13) | collective-permute-done | bytes 458784 | tf_op jit(solution)/shard_map/ppermute | solution.py:35
  80.5 2.1 %collective-permute-done.14.cross = bf16[64,3584]{1,0:T(8,128)(2,1)} collective-permute-done((bf16[64,3584]{1,0:T(8,128)(2,1)}, bf16[64,3584]{1,0:T(8,128)(2,1)}, u32[]{:S(2)}, u32[]{:S(2)}) %collective-permute-start.14) | collective-permute-done | bytes 458784 | tf_op jit(solution)/shard_map/ppermute | solution.py:35
  82.6 6.7 %expert_work.3 = (bf16[64,3712]{1,0:T(8,128)(2,1)S(1)}, bf16[64,3712]{1,0:T(8,128)(2,1)S(1)}, bf16[64,3712]{1,0:T(8,128)(2,1)S(1)}, bf16[64,3712]{1,0:T(8,128)(2,1)S(1)}) custom-call(s32[3]{0:T(128)S(1)} %pad_add_fusion.pos, bf16[64,3584]{1,0:T(8,128)(2,1)S(1)} %bitcast.84, bf16[64,3584]{1,0:T(8,128)(2,1)} %collective-permute-done.12.sib, ...), custom_call_target="tpu_custom_call" | custom-call | tf_op jit(solution)/shard_map/expert_work/pallas_call | solution.py:156
  89.4 1.9 %collective-permute-start.15 = (bf16[64,3712]{1,0:T(8,128)(2,1)S(1)}, bf16[64,3712]{1,0:T(8,128)(2,1)S(1)}, u32[]{:S(2)}, u32[]{:S(2)}) collective-permute-start(bf16[64,3712]{1,0:T(8,128)(2,1)S(1)} %get-tuple-element.17), channel_id=1, source_target_pairs={{0,1},{1,0},{2,3},{3,2},{4,5},{5,4},{6,7},{7,6},{8,9},{9,8},{10,11... | collective-permute-start | bytes 1425416 | tf_op jit(solution)/shard_map/ppermute | solution.py:35
  91.3 2.6 %collective-permute-start.16 = (bf16[64,3712]{1,0:T(8,128)(2,1)S(1)}, bf16[64,3712]{1,0:T(8,128)(2,1)S(1)}, u32[]{:S(2)}, u32[]{:S(2)}) collective-permute-start(bf16[64,3712]{1,0:T(8,128)(2,1)S(1)} %get-tuple-element.18), channel_id=1, source_target_pairs={{0,6},{1,3},{2,4},{3,1},{4,2},{5,7},{6,0},{7,5},{8,14},{9,11},{10,... | collective-permute-start | bytes 1425416 | tf_op jit(solution)/shard_map/ppermute | solution.py:35
  93.9 2.0 %collective-permute-start.17 = (bf16[64,3712]{1,0:T(8,128)(2,1)S(1)}, bf16[64,3712]{1,0:T(8,128)(2,1)S(1)}, u32[]{:S(2)}, u32[]{:S(2)}) collective-permute-start(bf16[64,3712]{1,0:T(8,128)(2,1)S(1)} %get-tuple-element.19), channel_id=1, source_target_pairs={{0,7},{1,2},{2,5},{3,0},{4,3},{5,6},{6,1},{7,4},{8,15},{9,10},{10,... | collective-permute-start | bytes 1425416 | tf_op jit(solution)/shard_map/ppermute | solution.py:35
  95.9 4.4 %collective-permute-start.2 = (bf16[64,3584]{1,0:T(8,128)(2,1)S(1)}, bf16[64,3584]{1,0:T(8,128)(2,1)S(1)}, u32[]{:S(2)}, u32[]{:S(2)}) collective-permute-start(bf16[64,3584]{1,0:T(8,128)(2,1)S(1)} %bitcast.78), channel_id=1, source_target_pairs={{0,6},{1,3},{2,4},{3,1},{4,2},{5,7},{6,0},{7,5},{8,14},{9,11},{10,... | collective-permute-start | bytes 1376264 | tf_op jit(solution)/shard_map/ppermute | solution.py:35
  100.4 1.9 %collective-permute-start.3 = (bf16[64,3584]{1,0:T(8,128)(2,1)S(1)}, bf16[64,3584]{1,0:T(8,128)(2,1)S(1)}, u32[]{:S(2)}, u32[]{:S(2)}) collective-permute-start(bf16[64,3584]{1,0:T(8,128)(2,1)S(1)} %bitcast.79), channel_id=1, source_target_pairs={{0,3},{1,6},{2,1},{3,4},{4,7},{5,2},{6,5},{7,0},{8,11},{9,14},{10,... | collective-permute-start | bytes 1376264 | tf_op jit(solution)/shard_map/ppermute | solution.py:35
  102.3 15.6 %collective-permute-done.2.same = bf16[64,3584]{1,0:T(8,128)(2,1)S(1)} collective-permute-done((bf16[64,3584]{1,0:T(8,128)(2,1)S(1)}, bf16[64,3584]{1,0:T(8,128)(2,1)S(1)}, u32[]{:S(2)}, u32[]{:S(2)}) %collective-permute-start.2) | collective-permute-done | bytes 458784 | tf_op jit(solution)/shard_map/ppermute | solution.py:35
  118.0 7.1 %expert_work.2 = (bf16[64,3712]{1,0:T(8,128)(2,1)S(1)}, bf16[64,3712]{1,0:T(8,128)(2,1)}, bf16[64,3712]{1,0:T(8,128)(2,1)}, bf16[64,3712]{1,0:T(8,128)(2,1)}) custom-call(s32[3]{0:T(128)S(1)} %pad_add_fusion.pos, bf16[64,3584]{1,0:T(8,128)(2,1)S(1)} %bitcast.80, bf16[64,3584]{1,0:T(8,128)(2,1)} %collective-permute-done.1.sib, ...), custom_call_target="tpu_custom_call" | custom-call | tf_op jit(solution)/shard_map/expert_work/pallas_call | solution.py:156
  125.1 1.9 %collective-permute-start.10 = (bf16[64,3712]{1,0:T(8,128)(2,1)}, bf16[64,3712]{1,0:T(8,128)(2,1)S(1)}, u32[]{:S(2)}, u32[]{:S(2)}) collective-permute-start(bf16[64,3712]{1,0:T(8,128)(2,1)} %get-tuple-element.15), channel_id=1, source_target_pairs={{0,7},{1,2},{2,5},{3,0},{4,3},{5,6},{6,1},{7,4},{8,15},{9,10},{10,... | collective-permute-start | bytes 1425416 | tf_op jit(solution)/shard_map/ppermute | solution.py:35
  127.1 1.9 %collective-permute-start.8 = (bf16[64,3712]{1,0:T(8,128)(2,1)}, bf16[64,3712]{1,0:T(8,128)(2,1)S(1)}, u32[]{:S(2)}, u32[]{:S(2)}) collective-permute-start(bf16[64,3712]{1,0:T(8,128)(2,1)} %get-tuple-element.13), channel_id=1, source_target_pairs={{0,1},{1,0},{2,3},{3,2},{4,5},{5,4},{6,7},{7,6},{8,9},{9,8},{10,11... | collective-permute-start | bytes 1425416 | tf_op jit(solution)/shard_map/ppermute | solution.py:35
  129.0 3.2 %collective-permute-start.9 = (bf16[64,3712]{1,0:T(8,128)(2,1)}, bf16[64,3712]{1,0:T(8,128)(2,1)S(1)}, u32[]{:S(2)}, u32[]{:S(2)}) collective-permute-start(bf16[64,3712]{1,0:T(8,128)(2,1)} %get-tuple-element.14), channel_id=1, source_target_pairs={{0,6},{1,3},{2,4},{3,1},{4,2},{5,7},{6,0},{7,5},{8,14},{9,11},{10,... | collective-permute-start | bytes 1425416 | tf_op jit(solution)/shard_map/ppermute | solution.py:35
  132.2 1.0 add_convert_fusion
  133.2 7.3 %all-to-all-start.3 = ((bf16[4,16,3712]{2,1,0:T(8,128)(2,1)}), bf16[4,16,3712]{2,1,0:T(8,128)(2,1)S(1)}, u32[]{:S(2)}, u32[]{:S(2)}) async-start(bf16[4,16,3712]{2,1,0:T(8,128)(2,1)} %bitcast.43), calls=%async_computation.3 | async-start | bytes 950272 | tf_op jit(solution)/shard_map/all_to_all | solution.py:48
  141.0 1.0 add_convert_fusion.1
  142.0 13.2 %all-to-all-done.3 = bf16[4,16,3712]{2,1,0:T(8,128)(2,1)S(1)} async-done(((bf16[4,16,3712]{2,1,0:T(8,128)(2,1)}), bf16[4,16,3712]{2,1,0:T(8,128)(2,1)S(1)}, u32[]{:S(2)}, u32[]{:S(2)}) %all-to-all-start.3) | async-done | bytes 475168 | tf_op jit(solution)/shard_map/all_to_all | solution.py:48
  155.2 4.0 %all-to-all-start.1 = ((bf16[4,16,3712]{2,1,0:T(8,128)(2,1)}), bf16[4,16,3712]{2,1,0:T(8,128)(2,1)S(1)}, u32[]{:S(2)}, u32[]{:S(2)}) async-start(bf16[4,16,3712]{2,1,0:T(8,128)(2,1)} %bitcast.31), calls=%async_computation.1 | async-start | bytes 950272 | tf_op jit(solution)/shard_map/all_to_all | solution.py:48
  160.2 0.7 copy-done.13
  160.8 0.9 fusion.5
  161.7 10.3 %all-to-all-done.1 = bf16[4,16,3712]{2,1,0:T(8,128)(2,1)S(1)} async-done(((bf16[4,16,3712]{2,1,0:T(8,128)(2,1)}), bf16[4,16,3712]{2,1,0:T(8,128)(2,1)S(1)}, u32[]{:S(2)}, u32[]{:S(2)}) %all-to-all-start.1) | async-done | bytes 475168 | tf_op jit(solution)/shard_map/all_to_all | solution.py:48
  173.0 0.7 copy-done.14
  173.6 0.9 fusion.4
  (56 shorter events, 3.5 us)
Async XLA Ops:
  0.6 17.1 %copy-start.9 = (bf16[1,512,128]{2,1,0:T(8,128)(2,1)S(1)}, bf16[1,512,128]{2,1,0:T(8,128)(2,1)}, u32[]{:S(2)}) copy-start(bf16[1,512,128]{2,1,0:T(8,128)(2,1)} %param.13) | copy-start | bytes 393220
  0.6 19.2 %collective-permute-start.11 = (bf16[64,3584]{1,0:T(8,128)(2,1)}, bf16[64,3584]{1,0:T(8,128)(2,1)S(1)}, u32[]{:S(2)}, u32[]{:S(2)}) collective-permute-start(bf16[64,3584]{1,0:T(8,128)(2,1)} %bitcast.103), channel_id=1, source_target_pairs={{0,32},{32,64},{64,96},{96,128},{128,160},{160,192},{192,224},{224... | collective-permute-start | bytes 1376264 | tf_op jit(solution)/shard_map/ppermute | solution.py:56
  5.1 63.3 %collective-permute-start.5 = (bf16[128,3584]{1,0:T(8,128)(2,1)}, bf16[128,3584]{1,0:T(8,128)(2,1)}, u32[]{:S(2)}, u32[]{:S(2)}) collective-permute-start(bf16[128,3584]{1,0:T(8,128)(2,1)} %bitcast.68), channel_id=1, source_target_pairs={{0,2},{1,7},{2,0},{3,5},{4,6},{5,3},{6,4},{7,1},{8,10},{9,15},{10,... | collective-permute-start | bytes 2752520 | tf_op jit(solution)/shard_map/ppermute | solution.py:35
  8.5 62.6 %collective-permute-start.6 = (bf16[3584,128]{1,0:T(8,128)(2,1)}, bf16[3584,128]{1,0:T(8,128)(2,1)}, u32[]{:S(2)}, u32[]{:S(2)}) collective-permute-start(bf16[3584,128]{1,0:T(8,128)(2,1)} %bitcast.71), channel_id=1, source_target_pairs={{0,2},{1,7},{2,0},{3,5},{4,6},{5,3},{6,4},{7,1},{8,10},{9,15},{10,... | collective-permute-start | bytes 2752520 | tf_op jit(solution)/shard_map/ppermute | solution.py:35
  10.9 65.1 %collective-permute-start.7 = (bf16[3584,128]{1,0:T(8,128)(2,1)}, bf16[3584,128]{1,0:T(8,128)(2,1)}, u32[]{:S(2)}, u32[]{:S(2)}) collective-permute-start(bf16[3584,128]{1,0:T(8,128)(2,1)} %bitcast.74), channel_id=1, source_target_pairs={{0,2},{1,7},{2,0},{3,5},{4,6},{5,3},{6,4},{7,1},{8,10},{9,15},{10,... | collective-permute-start | bytes 2752520 | tf_op jit(solution)/shard_map/ppermute | solution.py:35
  14.3 18.7 %collective-permute-start = (bf16[64,3584]{1,0:T(8,128)(2,1)}, bf16[64,3584]{1,0:T(8,128)(2,1)S(1)}, u32[]{:S(2)}, u32[]{:S(2)}) collective-permute-start(bf16[64,3584]{1,0:T(8,128)(2,1)} %bitcast.104), channel_id=1, source_target_pairs={{0,480},{32,0},{64,32},{96,64},{128,96},{160,128},{192,160},{224,1... | collective-permute-start | bytes 1376264 | tf_op jit(solution)/shard_map/ppermute | solution.py:56
  19.2 0.7 copy-start.15
  21.0 11.3 %copy-start.7 = (bf16[1,512,128]{2,1,0:T(8,128)(2,1)S(1)}, bf16[1,512,128]{2,1,0:T(8,128)(2,1)}, u32[]{:S(2)}) copy-start(bf16[1,512,128]{2,1,0:T(8,128)(2,1)} %param.16) | copy-start | bytes 393220
  21.0 11.3 %copy-start.8 = (bf16[1,512,128]{2,1,0:T(8,128)(2,1)S(1)}, bf16[1,512,128]{2,1,0:T(8,128)(2,1)}, u32[]{:S(2)}) copy-start(bf16[1,512,128]{2,1,0:T(8,128)(2,1)} %param.14) | copy-start | bytes 393220
  21.0 29.6 %all-to-all-start.2 = ((bf16[4,16,3584]{2,1,0:T(8,128)(2,1)}), bf16[4,16,3584]{2,1,0:T(8,128)(2,1)S(1)}, u32[]{:S(2)}, u32[]{:S(2)}) async-start(bf16[4,16,3584]{2,1,0:T(8,128)(2,1)} %bitcast.37), calls=%async_computation.2 | async-start | bytes 917504 | tf_op jit(solution)/shard_map/all_to_all | solution.py:48
  31.5 0.7 copy-start.16
  33.0 49.6 %copy-start.2 = (bf16[1,3584,128]{2,1,0:T(8,128)(2,1)S(1)}, bf16[1,3584,128]{2,1,0:T(8,128)(2,1)}, u32[]{:S(2)}) copy-start(bf16[1,3584,128]{2,1,0:T(8,128)(2,1)} %param.24) | copy-start | bytes 2752516
  50.7 0.8 copy-start.3
  51.4 31.2 %copy-start.1 = (bf16[1,3584,128]{2,1,0:T(8,128)(2,1)S(1)}, bf16[1,3584,128]{2,1,0:T(8,128)(2,1)}, u32[]{:S(2)}) copy-start(bf16[1,3584,128]{2,1,0:T(8,128)(2,1)} %param.23) | copy-start | bytes 2752516
  51.4 19.7 %all-to-all-start = ((bf16[4,16,3584]{2,1,0:T(8,128)(2,1)}), bf16[4,16,3584]{2,1,0:T(8,128)(2,1)S(1)}, u32[]{:S(2)}, u32[]{:S(2)}) async-start(bf16[4,16,3584]{2,1,0:T(8,128)(2,1)} %bitcast.6), calls=%async_computation | async-start | bytes 917504 | tf_op jit(solution)/shard_map/all_to_all | solution.py:48
  55.0 27.6 %copy-start = (bf16[1,128,3584]{2,1,0:T(8,128)(2,1)S(1)}, bf16[1,128,3584]{2,1,0:T(8,128)(2,1)}, u32[]{:S(2)}) copy-start(bf16[1,128,3584]{2,1,0:T(8,128)(2,1)} %param.25) | copy-start | bytes 2752516
  57.5 8.3 %collective-permute-start.4 = (bf16[4,2,4,2,16,128]{5,4,3,2,1,0:T(8,128)(2,1)S(1)}, bf16[4,2,4,2,16,128]{5,4,3,2,1,0:T(8,128)(2,1)S(1)}, u32[]{:S(2)}, u32[]{:S(2)}) collective-permute-start(bf16[4,2,4,2,16,128]{5,4,3,2,1,0:T(8,128)(2,1)S(1)} %pad_maximum_fusion), channel_id=1, source_target_pairs={{0,2},{1,7},{2,0},{3,5},{4,6},{5,3},{6,4},{7,1},{8,10},{9,15},{10,... | collective-permute-start | bytes 786440 | tf_op jit(solution)/shard_map/ppermute | solution.py:35
  59.4 16.6 %collective-permute-start.12 = (bf16[64,3584]{1,0:T(8,128)(2,1)}, bf16[64,3584]{1,0:T(8,128)(2,1)}, u32[]{:S(2)}, u32[]{:S(2)}) collective-permute-start(bf16[64,3584]{1,0:T(8,128)(2,1)} %bitcast.81), channel_id=1, source_target_pairs={{0,1},{1,0},{2,3},{3,2},{4,5},{5,4},{6,7},{7,6},{8,9},{9,8},{10,11... | collective-permute-start | bytes 1376264 | tf_op jit(solution)/shard_map/ppermute | solution.py:35
  65.8 5.3 %copy-start.12 = (bf16[4,2,4,2,16,128]{5,4,3,2,1,0:T(8,128)(2,1)}, bf16[4,2,4,2,16,128]{5,4,3,2,1,0:T(8,128)(2,1)S(1)}, u32[]{:S(2)}) copy-start(bf16[4,2,4,2,16,128]{5,4,3,2,1,0:T(8,128)(2,1)S(1)} %collective-permute-done.4) | copy-start | bytes 786436
  65.8 14.7 %collective-permute-start.13 = (bf16[64,3584]{1,0:T(8,128)(2,1)}, bf16[64,3584]{1,0:T(8,128)(2,1)}, u32[]{:S(2)}, u32[]{:S(2)}) collective-permute-start(bf16[64,3584]{1,0:T(8,128)(2,1)} %bitcast.82), channel_id=1, source_target_pairs={{0,6},{1,3},{2,4},{3,1},{4,2},{5,7},{6,0},{7,5},{8,14},{9,11},{10,... | collective-permute-start | bytes 1376264 | tf_op jit(solution)/shard_map/ppermute | solution.py:35
  68.4 14.2 %collective-permute-start.14 = (bf16[64,3584]{1,0:T(8,128)(2,1)}, bf16[64,3584]{1,0:T(8,128)(2,1)}, u32[]{:S(2)}, u32[]{:S(2)}) collective-permute-start(bf16[64,3584]{1,0:T(8,128)(2,1)} %bitcast.83), channel_id=1, source_target_pairs={{0,3},{1,6},{2,1},{3,4},{4,7},{5,2},{6,5},{7,0},{8,11},{9,14},{10,... | collective-permute-start | bytes 1376264 | tf_op jit(solution)/shard_map/ppermute | solution.py:35
  71.1 29.3 %collective-permute-start.1 = (bf16[64,3584]{1,0:T(8,128)(2,1)S(1)}, bf16[64,3584]{1,0:T(8,128)(2,1)}, u32[]{:S(2)}, u32[]{:S(2)}) collective-permute-start(bf16[64,3584]{1,0:T(8,128)(2,1)S(1)} %bitcast.77), channel_id=1, source_target_pairs={{0,1},{1,0},{2,3},{3,2},{4,5},{5,4},{6,7},{7,6},{8,9},{9,8},{10,11... | collective-permute-start | bytes 1376264 | tf_op jit(solution)/shard_map/ppermute | solution.py:35
  74.9 7.7 %copy-start.4 = (bf16[4,16,3584]{2,1,0:T(8,128)(2,1)S(1)}, bf16[4,16,3584]{2,1,0:T(8,128)(2,1)}, u32[]{:S(2)}) copy-start(bf16[4,16,3584]{2,1,0:T(8,128)(2,1)} %copy-done.3) | copy-start | bytes 1376260
  82.6 35.4 %copy-start.10 = (bf16[1,512,128]{2,1,0:T(8,128)(2,1)S(1)}, bf16[1,512,128]{2,1,0:T(8,128)(2,1)}, u32[]{:S(2)}) copy-start(bf16[1,512,128]{2,1,0:T(8,128)(2,1)} %param.13) | copy-start | bytes 393220
  82.6 35.4 %copy-start.11 = (bf16[1,512,128]{2,1,0:T(8,128)(2,1)S(1)}, bf16[1,512,128]{2,1,0:T(8,128)(2,1)}, u32[]{:S(2)}) copy-start(bf16[1,512,128]{2,1,0:T(8,128)(2,1)} %param.15) | copy-start | bytes 393220
  89.4 39.6 %collective-permute-start.15 = (bf16[64,3712]{1,0:T(8,128)(2,1)S(1)}, bf16[64,3712]{1,0:T(8,128)(2,1)S(1)}, u32[]{:S(2)}, u32[]{:S(2)}) collective-permute-start(bf16[64,3712]{1,0:T(8,128)(2,1)S(1)} %get-tuple-element.17), channel_id=1, source_target_pairs={{0,1},{1,0},{2,3},{3,2},{4,5},{5,4},{6,7},{7,6},{8,9},{9,8},{10,11... | collective-permute-start | bytes 1425416 | tf_op jit(solution)/shard_map/ppermute | solution.py:35
  91.3 40.9 %collective-permute-start.16 = (bf16[64,3712]{1,0:T(8,128)(2,1)S(1)}, bf16[64,3712]{1,0:T(8,128)(2,1)S(1)}, u32[]{:S(2)}, u32[]{:S(2)}) collective-permute-start(bf16[64,3712]{1,0:T(8,128)(2,1)S(1)} %get-tuple-element.18), channel_id=1, source_target_pairs={{0,6},{1,3},{2,4},{3,1},{4,2},{5,7},{6,0},{7,5},{8,14},{9,11},{10,... | collective-permute-start | bytes 1425416 | tf_op jit(solution)/shard_map/ppermute | solution.py:35
  93.9 38.3 %collective-permute-start.17 = (bf16[64,3712]{1,0:T(8,128)(2,1)S(1)}, bf16[64,3712]{1,0:T(8,128)(2,1)S(1)}, u32[]{:S(2)}, u32[]{:S(2)}) collective-permute-start(bf16[64,3712]{1,0:T(8,128)(2,1)S(1)} %get-tuple-element.19), channel_id=1, source_target_pairs={{0,7},{1,2},{2,5},{3,0},{4,3},{5,6},{6,1},{7,4},{8,15},{9,10},{10,... | collective-permute-start | bytes 1425416 | tf_op jit(solution)/shard_map/ppermute | solution.py:35
  95.9 22.0 %collective-permute-start.2 = (bf16[64,3584]{1,0:T(8,128)(2,1)S(1)}, bf16[64,3584]{1,0:T(8,128)(2,1)S(1)}, u32[]{:S(2)}, u32[]{:S(2)}) collective-permute-start(bf16[64,3584]{1,0:T(8,128)(2,1)S(1)} %bitcast.78), channel_id=1, source_target_pairs={{0,6},{1,3},{2,4},{3,1},{4,2},{5,7},{6,0},{7,5},{8,14},{9,11},{10,... | collective-permute-start | bytes 1376264 | tf_op jit(solution)/shard_map/ppermute | solution.py:35
  100.4 17.6 %collective-permute-start.3 = (bf16[64,3584]{1,0:T(8,128)(2,1)S(1)}, bf16[64,3584]{1,0:T(8,128)(2,1)S(1)}, u32[]{:S(2)}, u32[]{:S(2)}) collective-permute-start(bf16[64,3584]{1,0:T(8,128)(2,1)S(1)} %bitcast.79), channel_id=1, source_target_pairs={{0,3},{1,6},{2,1},{3,4},{4,7},{5,2},{6,5},{7,0},{8,11},{9,14},{10,... | collective-permute-start | bytes 1376264 | tf_op jit(solution)/shard_map/ppermute | solution.py:35
  125.1 8.1 %copy-start.5 = (bf16[64,3712]{1,0:T(8,128)(2,1)}, bf16[64,3712]{1,0:T(8,128)(2,1)S(1)}, u32[]{:S(2)}) copy-start(bf16[64,3712]{1,0:T(8,128)(2,1)S(1)} %get-tuple-element.12) | copy-start | bytes 1425412
  125.1 15.4 %collective-permute-start.10 = (bf16[64,3712]{1,0:T(8,128)(2,1)}, bf16[64,3712]{1,0:T(8,128)(2,1)S(1)}, u32[]{:S(2)}, u32[]{:S(2)}) collective-permute-start(bf16[64,3712]{1,0:T(8,128)(2,1)} %get-tuple-element.15), channel_id=1, source_target_pairs={{0,7},{1,2},{2,5},{3,0},{4,3},{5,6},{6,1},{7,4},{8,15},{9,10},{10,... | collective-permute-start | bytes 1425416 | tf_op jit(solution)/shard_map/ppermute | solution.py:35
  127.1 13.4 %collective-permute-start.8 = (bf16[64,3712]{1,0:T(8,128)(2,1)}, bf16[64,3712]{1,0:T(8,128)(2,1)S(1)}, u32[]{:S(2)}, u32[]{:S(2)}) collective-permute-start(bf16[64,3712]{1,0:T(8,128)(2,1)} %get-tuple-element.13), channel_id=1, source_target_pairs={{0,1},{1,0},{2,3},{3,2},{4,5},{5,4},{6,7},{7,6},{8,9},{9,8},{10,11... | collective-permute-start | bytes 1425416 | tf_op jit(solution)/shard_map/ppermute | solution.py:35
  129.0 12.0 %collective-permute-start.9 = (bf16[64,3712]{1,0:T(8,128)(2,1)}, bf16[64,3712]{1,0:T(8,128)(2,1)S(1)}, u32[]{:S(2)}, u32[]{:S(2)}) collective-permute-start(bf16[64,3712]{1,0:T(8,128)(2,1)} %get-tuple-element.14), channel_id=1, source_target_pairs={{0,6},{1,3},{2,4},{3,1},{4,2},{5,7},{6,0},{7,5},{8,14},{9,11},{10,... | collective-permute-start | bytes 1425416 | tf_op jit(solution)/shard_map/ppermute | solution.py:35
  133.2 7.8 %copy-start.6 = (bf16[64,3712]{1,0:T(8,128)(2,1)S(1)}, bf16[64,3712]{1,0:T(8,128)(2,1)}, u32[]{:S(2)}) copy-start(bf16[64,3712]{1,0:T(8,128)(2,1)} %copy-done.5) | copy-start | bytes 1425412
  133.2 21.9 %all-to-all-start.3 = ((bf16[4,16,3712]{2,1,0:T(8,128)(2,1)}), bf16[4,16,3712]{2,1,0:T(8,128)(2,1)S(1)}, u32[]{:S(2)}, u32[]{:S(2)}) async-start(bf16[4,16,3712]{2,1,0:T(8,128)(2,1)} %bitcast.43), calls=%async_computation.3 | async-start | bytes 950272 | tf_op jit(solution)/shard_map/all_to_all | solution.py:48
  155.2 16.9 %all-to-all-start.1 = ((bf16[4,16,3712]{2,1,0:T(8,128)(2,1)}), bf16[4,16,3712]{2,1,0:T(8,128)(2,1)S(1)}, u32[]{:S(2)}, u32[]{:S(2)}) async-start(bf16[4,16,3712]{2,1,0:T(8,128)(2,1)} %bitcast.31), calls=%async_computation.1 | async-start | bytes 950272 | tf_op jit(solution)/shard_map/all_to_all | solution.py:48
  160.2 0.7 copy-start.13
  173.0 0.7 copy-start.14
where the time goes:
time: 176 us; the launch traced here: 175 us
  starting transfers between devices  74.7 us (42%)
  waiting for transfers between devices  66.6 us (38%)
  Pallas kernels  13.9 us (8%)
  local copies, waits for them, and re-layouts  7.79 us (4%)
  other arithmetic  6.36 us (4%)
  matrix products  4.13 us (2%)
    ppermute x16, starting transfers between devices, moved(): return lax.ppermute(value, 'expert', pairs)  42.5 us
    all_to_all x4, waiting for transfers between devices, over_z(): lax.all_to_all(value, 'expert', split_axis=0, concat_axis=0, axis_index_g...  39.9 us
    ppermute x16, waiting for transfers between devices, moved(): return lax.ppermute(value, 'expert', pairs)  26.7 us
    all_to_all x4, starting transfers between devices, over_z(): lax.all_to_all(value, 'expert', split_axis=0, concat_axis=0, axis_index_g...  25.4 us
    pallas_call x2, Pallas kernels, expert_work(): pl.pallas_call(expert_kernel, in_specs=[pl.BlockSpec(memory_space=pltpu.S...  13.9 us
    ppermute x2, starting transfers between devices, passed_along(): return lax.ppermute(value, 'section', pairs)  6.87 us
  transfers between devices with their start and end apart: 22, of which 8 were waited for; matrix products, arithmetic and copies ran while one was open for 7% of the time, Pallas kernels for 8%

commit v1 on v0

--- a/solution.py
+++ b/solution.py
@@ -1,3 +1,5 @@
+import functools
+
 import jax
 import jax.numpy as jnp
 from jax import lax
@@ -74,55 +76,68 @@
     return lax.dot_general(a, b, (((1,), (1,)), ((), ())), preferred_element_type=jnp.float32)
 
 
+CUTS = (0, 1024, 2048, 3072, 3584)
+
+
+def cuts_of(wide):
+    return [c for c in CUTS if c < wide] + [wide]
+
+
 def expert_kernel(
-    pos, own, sib, same, cross,
-    gate_own, up_own, gate_mate, up_mate,
+    pos, own, sib, same, cross, gate_own, up_own, far,
     wd_own, wd_mate, wg_own, wg_mate, wu_own, wu_mate,
     p_own, p_sib, p_same, p_cross,
-    v_rows, v_gate_own, v_up_own, v_gate_mate, v_up_mate, v_wd, v_w, v_out, s_in, s_w, s_out,
+    v_rows, v_near, v_far, v_wd, v_w, v_out, s_in, s_saved, s_w, s_out, *, which,
 ):
     x, c, tp = pos[0], pos[1], pos[2]
     n, wide = own.shape
     unit = wd_own.shape[0]
-    loads = []
-    for k, ref in enumerate((own, sib, same, cross)):
-        loads.append((ref, v_rows.at[pl.ds(k * n, n)]))
-    loads.append((wd_own, v_wd.at[pl.ds(0, unit)]))
-    loads.append((wd_mate, v_wd.at[pl.ds(unit, unit)]))
-    loads += [(gate_own, v_gate_own), (up_own, v_up_own), (gate_mate, v_gate_mate), (up_mate, v_up_mate)]
-    first = [pltpu.make_async_copy(a, b, s_in.at[k]) for k, (a, b) in enumerate(loads)]
-    later = [
-        pltpu.make_async_copy(ref, v_w.at[k], s_w.at[k])
-        for k, ref in enumerate((wg_own, wg_mate, wu_own, wu_mate))
-    ]
-    for copy in first + later:
-        copy.start()
-    for copy in first:
+    cuts = cuts_of(wide)
+    spans = [pl.ds(lo, hi - lo) for lo, hi in zip(cuts, cuts[1:])]
+    incoming, later = [], []
+    for i, span in enumerate(spans):
+        group = []
+        for k, ref in enumerate((own, sib, same, cross)):
+            group.append((ref.at[:, span], v_rows.at[pl.ds(k * n, n), span]))
+        for k, ref in enumerate((wd_own, wd_mate)):
+            group.append((ref.at[:, span], v_wd.at[pl.ds(k * unit, unit), span]))
+        incoming.append([pltpu.make_async_copy(a, b, s_in.at[i, k]) for k, (a, b) in enumerate(group)])
+    keep = [(gate_own, v_near.at[0]), (up_own, v_near.at[1])]
+    keep.append((far.at[pl.ds(2 * which, 2)], v_far))
+    keep = [pltpu.make_async_copy(a, b, s_saved.at[k]) for k, (a, b) in enumerate(keep)]
+    for i, span in enumerate(spans):
+        later.append(
+            [
+                pltpu.make_async_copy(ref.at[span], v_w.at[k, span], s_w.at[i, k])
+                for k, ref in enumerate((wg_own, wg_mate, wu_own, wu_mate))
+            ]
+        )
+    for group in incoming + [keep] + later:
+        for copy in group:
+            copy.start()
+    dh = None
+    for i, (lo, hi) in enumerate(zip(cuts, cuts[1:])):
+        for copy in incoming[i]:
+            copy.wait()
+        for d in range(lo, hi, TILE):
+            cut = slice(d, d + TILE)
+            term = nt(v_rows[:, cut], v_wd[:, cut])
+            dh = term if dh is None else dh + term
+    for copy in keep:
         copy.wait()
-    dh = None
-    for d in range(0, wide, TILE):
-        cut = slice(d, d + TILE)
-        term = nt(v_rows[:, cut], v_wd[:, cut])
-        dh = term if dh is None else dh + term
-
-    def saved(mine, mate):
+
+    def saved(k):
         blocks = []
         for slot, xs in ((0, x), (1, tp)):
             for cs in (c, 1 - c):
                 for z in range(EXPERTS):
-                    blocks.append(
-                        jnp.concatenate(
-                            [
-                                mine[z * NX * NC + xs * NC + cs],
-                                mate[(slot * EXPERTS + z) * NC + cs],
-                            ],
-                            axis=-1,
-                        )
-                    )
+                    near = v_near[k, z * NX * NC + xs * NC + cs]
+                    away = v_far[k, (slot * EXPERTS + z) * NC + cs]
+                    blocks.append(jnp.concatenate([near, away], axis=-1))
         return jnp.concatenate(blocks, axis=0).astype(jnp.float32)
 
-    gate = saved(v_gate_own, v_gate_mate)
-    up = saved(v_up_own, v_up_mate)
+    gate = saved(0)
+    up = saved(1)
     sig = jax.nn.sigmoid(gate)
     act = gate * sig
     slope = sig * (1.0 + gate * (1.0 - sig))
@@ -131,46 +146,77 @@
     du = (dh * act).astype(jnp.bfloat16)
     both = jnp.concatenate([dg, du], axis=-1)
     v_out[:, wide:] = jnp.broadcast_to(q, (q.shape[0], PAD)).astype(jnp.bfloat16)
-    for copy in later:
-        copy.wait()
-    for d in range(0, wide, TILE):
-        cut = slice(d, d + TILE)
-        w = jnp.concatenate([v_w[k, cut] for k in range(4)], axis=-1)
-        v_out[:, cut] = nt(both, w).astype(jnp.bfloat16)
-    stores = [
-        pltpu.make_async_copy(v_out.at[pl.ds(k * n, n)], out, s_out.at[k])
-        for k, out in enumerate((p_own, p_sib, p_same, p_cross))
-    ]
-    for copy in stores:
-        copy.start()
+    stores = []
+    for i, (lo, hi) in enumerate(zip(cuts, cuts[1:])):
+        for copy in later[i]:
+            copy.wait()
+        for d in range(lo, hi, TILE):
+            cut = slice(d, d + TILE)
+            w = jnp.concatenate([v_w[k, cut] for k in range(4)], axis=-1)
+            v_out[:, cut] = nt(both, w).astype(jnp.bfloat16)
+        size = hi - lo + (PAD if hi == wide else 0)
+        for k, out in enumerate((p_same, p_cross, p_sib, p_own)):
+            row = (2, 3, 1, 0)[k] * n
+            copy = pltpu.make_async_copy(
+                v_out.at[pl.ds(row, n), pl.ds(lo, size)], out.at[:, pl.ds(lo, size)], s_out.at[i, k]
+            )
+            copy.start()
+            stores.append(copy)
     for copy in stores:
         copy.wait()
 
 
-def expert_work(pos, pieces, saved, weights):
+def expert_work(pos, pieces, near, far, weights, which):
     count, wide = pieces[0].shape
     unit = weights[0].shape[0]
     shape = jax.ShapeDtypeStruct((count, wide + PAD), jnp.bfloat16)
     anywhere = pl.BlockSpec(memory_space=pl.ANY)
     bf16 = jnp.bfloat16
+    steps = len(cuts_of(wide)) - 1
     return pl.pallas_call(
-        expert_kernel,
-        in_specs=[pl.BlockSpec(memory_space=pltpu.SMEM)] + [anywhere] * 14,
+        functools.partial(expert_kernel, which=which),
+        in_specs=[pl.BlockSpec(memory_space=pltpu.SMEM)] + [anywhere] * 13,
         out_specs=[anywhere] * 4,
         out_shape=[shape] * 4,
         scratch_shapes=[
             pltpu.VMEM((4 * count, wide), bf16),
-            *[pltpu.VMEM(v.shape, bf16) for v in saved],
+            pltpu.VMEM((2,) + near[0].shape, bf16),
+            pltpu.VMEM((2,) + far.shape[1:], bf16),
             pltpu.VMEM((2 * unit, wide), bf16),
             pltpu.VMEM((4, wide, unit), bf16),
             pltpu.VMEM((4 * count, wide + PAD), bf16),
-            pltpu.SemaphoreType.DMA((10,)),
-            pltpu.SemaphoreType.DMA((4,)),
-            pltpu.SemaphoreType.DMA((4,)),
+            pltpu.SemaphoreType.DMA((steps, 6)),
+            pltpu.SemaphoreType.DMA((3,)),
+            pltpu.SemaphoreType.DMA((steps, 4)),
+            pltpu.SemaphoreType.DMA((steps, 4)),
         ],
         compiler_params=pltpu.CompilerParams(vmem_limit_bytes=32 << 20),
         name="expert_work",
-    )(pos, *pieces, *saved, *weights)
+    )(pos, *pieces, *near, far, *weights)
+
+
+def unpack_kernel(chosen, back, probs, grad_x, grad_p):
+    wide = grad_x.shape[-1]
+    picked = jnp.dot(chosen[...], back[:, :wide], preferred_element_type=jnp.float32)
+    grad_x[...] = (probs[...] * picked).astype(jnp.bfloat16)
+    shares = back[:, wide:].astype(jnp.float32).T.astype(jnp.bfloat16)
+    grad_p[...] = nt(shares, chosen[...])[:1]
+
+
+def unpack(chosen, back, probs):
+    count = chosen.shape[0]
+    vmem = pl.BlockSpec(memory_space=pltpu.VMEM)
+    return pl.pallas_call(
+        unpack_kernel,
+        in_specs=[vmem] * 3,
+        out_specs=[vmem] * 2,
+        out_shape=[
+            jax.ShapeDtypeStruct((count, back.shape[-1] - PAD), jnp.bfloat16),
+            jax.ShapeDtypeStruct((1, count), jnp.float32),
+        ],
+        compiler_params=pltpu.CompilerParams(vmem_limit_bytes=8 << 20),
+        name="unpack",
+    )(chosen, back, probs)
 
 
 def gather_rows(own):
@@ -213,7 +259,7 @@
     far = to_weight_partner(jnp.stack([wanted(v) for v in pre]))
     far = far.reshape(len(pre), -1, CAP, far.shape[-1])
 
-    def handle(arrived, route, probs, saved):
+    def handle(arrived, route, probs, near, which):
         chosen = table(slots_of(route))
         send = lax.dot_general(
             chosen, arrived, (((0,), (0,)), ((), ())), preferred_element_type=jnp.float32
@@ -221,15 +267,14 @@
         wide = send.shape[-1]
         own = over_z(send.reshape(EXPERTS, CAP, wide)).reshape(EXPERTS * CAP, wide)
         pieces = gather_rows(own)
-        parts = expert_work(pos, pieces, saved, weights)
+        parts = expert_work(pos, pieces, near, far, weights, which)
         total = reduce_rows(*parts)
         back = over_z(total.reshape(EXPERTS, CAP, -1)).reshape(EXPERTS * CAP, -1)
-        picked = jnp.dot(chosen, back, preferred_element_type=jnp.float32)
-        grad_x = (probs * picked[:, :wide]).astype(jnp.bfloat16)
-        return grad_x[None], picked[None, :, wide:wide + 1]
-
-    dx_a, dprob_a = handle(upper, route_a[0], probs_a[0], (pre[0], pre[1], far[0], far[1]))
-    dx_b, dprob_b = handle(lower, route_b[0], probs_b[0], (pre[2], pre[3], far[2], far[3]))
+        grad_x, grad_p = unpack(chosen, back, probs)
+        return grad_x[None], grad_p[..., None]
+
+    dx_a, dprob_a = handle(upper, route_a[0], probs_a[0], (pre[0], pre[1]), 0)
+    dx_b, dprob_b = handle(lower, route_b[0], probs_b[0], (pre[2], pre[3]), 1)
     return (dx_a, dx_b, dprob_a, dprob_b)
 
 

time: 176 us -> 173 us (0.983)
  other arithmetic: 6.36 us -> 2.33 us
  waiting for transfers between devices: 66.6 us -> 69 us
    unnamed x34 -> x36, local copies, waits for them, and re-layouts: 3.44 us -> 6.23 us
    another operation x5, other arithmetic: 2.47 us -> 0.07 us  [on_device(): far = to_weight_partner(jnp.stack([wanted(v) for v in pre]))]
    slice x3 -> x0, local copies, waits for them, and re-layouts: 2.26 us -> none  [the longest x2 1.26 us: handle(): return (grad_x[None], picked[None, :, wide:wide + 1])]
    broadcast_in_dim x2 -> x0, other arithmetic: 1.77 us -> none  [handle(): return (grad_x[None], picked[None, :, wide:wide + 1])]
    pallas_call x2 -> x4, Pallas kernels: 13.9 us -> 15.3 us  [the longest x2 13.1 us: expert_work(): pl.pallas_call(functools.partial(expert_kernel, which=which), in_specs=[p...]
  transfers between devices with their start and end apart: 22 -> 22, of which waited for: 8 -> 9; matrix products, arithmetic and copies ran while one was open for 7% -> 4% of each run, Pallas kernels for 8% -> 8%
where the time goes in v1:
time: 173 us; the launch traced here: 172 us
  starting transfers between devices  73.9 us (43%)
  waiting for transfers between devices  69 us (40%)
  Pallas kernels  15.3 us (9%)
  local copies, waits for them, and re-layouts  7.23 us (4%)
  matrix products  3.49 us (2%)
  other arithmetic  2.33 us (1%)
    ppermute x16, starting transfers between devices, moved(): return lax.ppermute(value, 'expert', pairs)  42.2 us
    all_to_all x4, waiting for transfers between devices, over_z(): lax.all_to_all(value, 'expert', split_axis=0, concat_axis=0, axis_index_g...  41.2 us
    ppermute x16, waiting for transfers between devices, moved(): return lax.ppermute(value, 'expert', pairs)  27.7 us
    all_to_all x4, starting transfers between devices, over_z(): lax.all_to_all(value, 'expert', split_axis=0, concat_axis=0, axis_index_g...  24.9 us
    pallas_call x2, Pallas kernels, expert_work(): pl.pallas_call(functools.partial(expert_kernel, which=which), in_specs=[p...  13.1 us
    ppermute x2, starting transfers between devices, passed_along(): return lax.ppermute(value, 'section', pairs)  6.87 us
    unnamed x36, local copies, waits for them, and re-layouts  6.23 us
  transfers between devices with their start and end apart: 22, of which 9 were waited for; matrix products, arithmetic and copies ran while one was open for 4% of the time, Pallas kernels for 8%

profile of v1, /device:TPU:24, one launch (start us, length us, event | category | flops | bytes accessed | tf_op | source)
XLA Modules:
  0.0 172.3 jit_solution(9776217191133285121)
XLA Ops:
  0.6 4.4 %collective-permute-start.11 = (bf16[64,3584]{1,0:T(8,128)(2,1)}, bf16[64,3584]{1,0:T(8,128)(2,1)S(1)}, u32[]{:S(2)}, u32[]{:S(2)}) collective-permute-start(bf16[64,3584]{1,0:T(8,128)(2,1)} %bitcast.93), channel_id=1, source_target_pairs={{0,32},{32,64},{64,96},{96,128},{128,160},{160,192},{192,224},{224... | collective-permute-start | bytes 1376264 | tf_op jit(solution)/shard_map/ppermute | solution.py:58
  5.1 3.4 %collective-permute-start.5 = (bf16[128,3584]{1,0:T(8,128)(2,1)}, bf16[128,3584]{1,0:T(8,128)(2,1)}, u32[]{:S(2)}, u32[]{:S(2)}) collective-permute-start(bf16[128,3584]{1,0:T(8,128)(2,1)} %bitcast.61), channel_id=1, source_target_pairs={{0,2},{1,7},{2,0},{3,5},{4,6},{5,3},{6,4},{7,1},{8,10},{9,15},{10,... | collective-permute-start | bytes 2752520 | tf_op jit(solution)/shard_map/ppermute | solution.py:37
  8.5 2.4 %collective-permute-start.6 = (bf16[3584,128]{1,0:T(8,128)(2,1)}, bf16[3584,128]{1,0:T(8,128)(2,1)}, u32[]{:S(2)}, u32[]{:S(2)}) collective-permute-start(bf16[3584,128]{1,0:T(8,128)(2,1)} %bitcast.64), channel_id=1, source_target_pairs={{0,2},{1,7},{2,0},{3,5},{4,6},{5,3},{6,4},{7,1},{8,10},{9,15},{10,... | collective-permute-start | bytes 2752520 | tf_op jit(solution)/shard_map/ppermute | solution.py:37
  10.9 3.4 %collective-permute-start.7 = (bf16[3584,128]{1,0:T(8,128)(2,1)}, bf16[3584,128]{1,0:T(8,128)(2,1)}, u32[]{:S(2)}, u32[]{:S(2)}) collective-permute-start(bf16[3584,128]{1,0:T(8,128)(2,1)} %bitcast.67), channel_id=1, source_target_pairs={{0,2},{1,7},{2,0},{3,5},{4,6},{5,3},{6,4},{7,1},{8,10},{9,15},{10,... | collective-permute-start | bytes 2752520 | tf_op jit(solution)/shard_map/ppermute | solution.py:37
  14.3 2.5 %collective-permute-start = (bf16[64,3584]{1,0:T(8,128)(2,1)}, bf16[64,3584]{1,0:T(8,128)(2,1)S(1)}, u32[]{:S(2)}, u32[]{:S(2)}) collective-permute-start(bf16[64,3584]{1,0:T(8,128)(2,1)} %bitcast.94), channel_id=1, source_target_pairs={{0,480},{32,0},{64,32},{96,64},{128,96},{160,128},{192,160},{224,1... | collective-permute-start | bytes 1376264 | tf_op jit(solution)/shard_map/ppermute | solution.py:58
  16.8 0.9 fusion.1
  17.8 0.8 dynamic-slice_bitcast_fusion.5
  18.6 0.6 copy-done.16
  19.2 1.2 convolution_convert_fusion
  20.4 10.4 %all-to-all-start.2 = ((bf16[4,16,3584]{2,1,0:T(8,128)(2,1)}), bf16[4,16,3584]{2,1,0:T(8,128)(2,1)S(1)}, u32[]{:S(2)}, u32[]{:S(2)}) async-start(bf16[4,16,3584]{2,1,0:T(8,128)(2,1)} %bitcast.35), calls=%async_computation.2 | async-start | bytes 917504 | tf_op jit(solution)/shard_map/all_to_all | solution.py:50
  30.8 0.7 copy-done.17
  31.8 1.2 convolution_convert_fusion.1
  32.9 17.7 %all-to-all-done.2 = bf16[4,16,3584]{2,1,0:T(8,128)(2,1)S(1)} async-done(((bf16[4,16,3584]{2,1,0:T(8,128)(2,1)}), bf16[4,16,3584]{2,1,0:T(8,128)(2,1)S(1)}, u32[]{:S(2)}, u32[]{:S(2)}) %all-to-all-start.2) | async-done | bytes 458784 | tf_op jit(solution)/shard_map/all_to_all | solution.py:50
  50.7 0.8 copy-done.3
  51.4 3.6 %all-to-all-start = ((bf16[4,16,3584]{2,1,0:T(8,128)(2,1)}), bf16[4,16,3584]{2,1,0:T(8,128)(2,1)S(1)}, u32[]{:S(2)}, u32[]{:S(2)}) async-start(bf16[4,16,3584]{2,1,0:T(8,128)(2,1)} %bitcast.90), calls=%async_computation | async-start | bytes 917504 | tf_op jit(solution)/shard_map/all_to_all | solution.py:50
  55.1 1.9 %collective-permute-start.4 = (bf16[4,2,4,2,16,128]{5,4,3,2,1,0:T(8,128)(2,1)S(1)}, bf16[4,2,4,2,16,128]{5,4,3,2,1,0:T(8,128)(2,1)S(1)}, u32[]{:S(2)}, u32[]{:S(2)}) collective-permute-start(bf16[4,2,4,2,16,128]{5,4,3,2,1,0:T(8,128)(2,1)S(1)} %pad_maximum_fusion), channel_id=1, source_target_pairs={{0,2},{1,7},{2,0},{3,5},{4,6},{5,3},{6,4},{7,1},{8,10},{9,15},{10,... | collective-permute-start | bytes 786440 | tf_op jit(solution)/shard_map/ppermute | solution.py:37
  57.1 2.3 %collective-permute-start.12 = (bf16[64,3584]{1,0:T(8,128)(2,1)}, bf16[64,3584]{1,0:T(8,128)(2,1)}, u32[]{:S(2)}, u32[]{:S(2)}) collective-permute-start(bf16[64,3584]{1,0:T(8,128)(2,1)} %bitcast.76), channel_id=1, source_target_pairs={{0,1},{1,0},{2,3},{3,2},{4,5},{5,4},{6,7},{7,6},{8,9},{9,8},{10,11... | collective-permute-start | bytes 1376264 | tf_op jit(solution)/shard_map/ppermute | solution.py:37
  59.4 4.0 %collective-permute-done.4 = bf16[4,2,4,2,16,128]{5,4,3,2,1,0:T(8,128)(2,1)S(1)} collective-permute-done((bf16[4,2,4,2,16,128]{5,4,3,2,1,0:T(8,128)(2,1)S(1)}, bf16[4,2,4,2,16,128]{5,4,3,2,1,0:T(8,128)(2,1)S(1)}, u32[]{:S(2)}, u32[]{:S(2)}) %collective-permute-start.4) | collective-permute-done | bytes 262176 | tf_op jit(solution)/shard_map/ppermute | solution.py:37
  63.4 2.6 %collective-permute-start.13 = (bf16[64,3584]{1,0:T(8,128)(2,1)}, bf16[64,3584]{1,0:T(8,128)(2,1)}, u32[]{:S(2)}, u32[]{:S(2)}) collective-permute-start(bf16[64,3584]{1,0:T(8,128)(2,1)} %bitcast.77), channel_id=1, source_target_pairs={{0,6},{1,3},{2,4},{3,1},{4,2},{5,7},{6,0},{7,5},{8,14},{9,11},{10,... | collective-permute-start | bytes 1376264 | tf_op jit(solution)/shard_map/ppermute | solution.py:37
  66.0 2.8 %collective-permute-start.14 = (bf16[64,3584]{1,0:T(8,128)(2,1)}, bf16[64,3584]{1,0:T(8,128)(2,1)}, u32[]{:S(2)}, u32[]{:S(2)}) collective-permute-start(bf16[64,3584]{1,0:T(8,128)(2,1)} %bitcast.78), channel_id=1, source_target_pairs={{0,3},{1,6},{2,1},{3,4},{4,7},{5,2},{6,5},{7,0},{8,11},{9,14},{10,... | collective-permute-start | bytes 1376264 | tf_op jit(solution)/shard_map/ppermute | solution.py:37
  69.1 3.4 %collective-permute-start.1 = (bf16[64,3584]{1,0:T(8,128)(2,1)S(1)}, bf16[64,3584]{1,0:T(8,128)(2,1)}, u32[]{:S(2)}, u32[]{:S(2)}) collective-permute-start(bf16[64,3584]{1,0:T(8,128)(2,1)S(1)} %bitcast.72), channel_id=1, source_target_pairs={{0,1},{1,0},{2,3},{3,2},{4,5},{5,4},{6,7},{7,6},{8,9},{9,8},{10,11... | collective-permute-start | bytes 1376264 | tf_op jit(solution)/shard_map/ppermute | solution.py:37
  72.6 5.5 %collective-permute-done.13.same = bf16[64,3584]{1,0:T(8,128)(2,1)} collective-permute-done((bf16[64,3584]{1,0:T(8,128)(2,1)}, bf16[64,3584]{1,0:T(8,128)(2,1)}, u32[]{:S(2)}, u32[]{:S(2)}) %collective-permute-start.13) | collective-permute-done | bytes 458784 | tf_op jit(solution)/shard_map/ppermute | solution.py:37
  78.1 2.1 %collective-permute-done.14.cross = bf16[64,3584]{1,0:T(8,128)(2,1)} collective-permute-done((bf16[64,3584]{1,0:T(8,128)(2,1)}, bf16[64,3584]{1,0:T(8,128)(2,1)}, u32[]{:S(2)}, u32[]{:S(2)}) %collective-permute-start.14) | collective-permute-done | bytes 458784 | tf_op jit(solution)/shard_map/ppermute | solution.py:37
  80.2 1.0 copy-done.4
  81.2 0.9 copy-done.8
  82.1 0.9 copy-done.10
  83.0 6.3 %expert_work.3 = (bf16[64,3712]{1,0:T(8,128)(2,1)S(1)}, bf16[64,3712]{1,0:T(8,128)(2,1)S(1)}, bf16[64,3712]{1,0:T(8,128)(2,1)S(1)}, bf16[64,3712]{1,0:T(8,128)(2,1)S(1)}) custom-call(s32[3]{0:T(128)S(1)} %pad_add_fusion.pos, bf16[64,3584]{1,0:T(8,128)(2,1)S(1)} %bitcast.79, bf16[64,3584]{1,0:T(8,128)(2,1)} %collective-permute-done.12.sib, ...), custom_call_target="tpu_custom_call" | custom-call | tf_op jit(solution)/shard_map/expert_work/pallas_call | solution.py:176
  89.4 1.9 %collective-permute-start.15 = (bf16[64,3712]{1,0:T(8,128)(2,1)S(1)}, bf16[64,3712]{1,0:T(8,128)(2,1)S(1)}, u32[]{:S(2)}, u32[]{:S(2)}) collective-permute-start(bf16[64,3712]{1,0:T(8,128)(2,1)S(1)} %get-tuple-element.22), channel_id=1, source_target_pairs={{0,1},{1,0},{2,3},{3,2},{4,5},{5,4},{6,7},{7,6},{8,9},{9,8},{10,11... | collective-permute-start | bytes 1425416 | tf_op jit(solution)/shard_map/ppermute | solution.py:37
  91.3 2.6 %collective-permute-start.16 = (bf16[64,3712]{1,0:T(8,128)(2,1)S(1)}, bf16[64,3712]{1,0:T(8,128)(2,1)S(1)}, u32[]{:S(2)}, u32[]{:S(2)}) collective-permute-start(bf16[64,3712]{1,0:T(8,128)(2,1)S(1)} %get-tuple-element.23), channel_id=1, source_target_pairs={{0,6},{1,3},{2,4},{3,1},{4,2},{5,7},{6,0},{7,5},{8,14},{9,11},{10,... | collective-permute-start | bytes 1425416 | tf_op jit(solution)/shard_map/ppermute | solution.py:37
  93.9 2.0 %collective-permute-start.17 = (bf16[64,3712]{1,0:T(8,128)(2,1)S(1)}, bf16[64,3712]{1,0:T(8,128)(2,1)S(1)}, u32[]{:S(2)}, u32[]{:S(2)}) collective-permute-start(bf16[64,3712]{1,0:T(8,128)(2,1)S(1)} %get-tuple-element.24), channel_id=1, source_target_pairs={{0,7},{1,2},{2,5},{3,0},{4,3},{5,6},{6,1},{7,4},{8,15},{9,10},{10,... | collective-permute-start | bytes 1425416 | tf_op jit(solution)/shard_map/ppermute | solution.py:37
  95.9 4.4 %collective-permute-start.2 = (bf16[64,3584]{1,0:T(8,128)(2,1)S(1)}, bf16[64,3584]{1,0:T(8,128)(2,1)S(1)}, u32[]{:S(2)}, u32[]{:S(2)}) collective-permute-start(bf16[64,3584]{1,0:T(8,128)(2,1)S(1)} %bitcast.73), channel_id=1, source_target_pairs={{0,6},{1,3},{2,4},{3,1},{4,2},{5,7},{6,0},{7,5},{8,14},{9,11},{10,... | collective-permute-start | bytes 1376264 | tf_op jit(solution)/shard_map/ppermute | solution.py:37
  100.4 1.9 %collective-permute-start.3 = (bf16[64,3584]{1,0:T(8,128)(2,1)S(1)}, bf16[64,3584]{1,0:T(8,128)(2,1)S(1)}, u32[]{:S(2)}, u32[]{:S(2)}) collective-permute-start(bf16[64,3584]{1,0:T(8,128)(2,1)S(1)} %bitcast.74), channel_id=1, source_target_pairs={{0,3},{1,6},{2,1},{3,4},{4,7},{5,2},{6,5},{7,0},{8,11},{9,14},{10,... | collective-permute-start | bytes 1376264 | tf_op jit(solution)/shard_map/ppermute | solution.py:37
  102.3 15.6 %collective-permute-done.2.same = bf16[64,3584]{1,0:T(8,128)(2,1)S(1)} collective-permute-done((bf16[64,3584]{1,0:T(8,128)(2,1)S(1)}, bf16[64,3584]{1,0:T(8,128)(2,1)S(1)}, u32[]{:S(2)}, u32[]{:S(2)}) %collective-permute-start.2) | collective-permute-done | bytes 458784 | tf_op jit(solution)/shard_map/ppermute | solution.py:37
  118.0 6.8 %expert_work.2 = (bf16[64,3712]{1,0:T(8,128)(2,1)S(1)}, bf16[64,3712]{1,0:T(8,128)(2,1)}, bf16[64,3712]{1,0:T(8,128)(2,1)}, bf16[64,3712]{1,0:T(8,128)(2,1)}) custom-call(s32[3]{0:T(128)S(1)} %pad_add_fusion.pos, bf16[64,3584]{1,0:T(8,128)(2,1)S(1)} %bitcast.75, bf16[64,3584]{1,0:T(8,128)(2,1)} %collective-permute-done.1.sib, ...), custom_call_target="tpu_custom_call" | custom-call | tf_op jit(solution)/shard_map/expert_work/pallas_call | solution.py:176
  124.8 1.9 %collective-permute-start.10 = (bf16[64,3712]{1,0:T(8,128)(2,1)}, bf16[64,3712]{1,0:T(8,128)(2,1)S(1)}, u32[]{:S(2)}, u32[]{:S(2)}) collective-permute-start(bf16[64,3712]{1,0:T(8,128)(2,1)} %get-tuple-element.19), channel_id=1, source_target_pairs={{0,7},{1,2},{2,5},{3,0},{4,3},{5,6},{6,1},{7,4},{8,15},{9,10},{10,... | collective-permute-start | bytes 1425416 | tf_op jit(solution)/shard_map/ppermute | solution.py:37
  126.8 1.9 %collective-permute-start.8 = (bf16[64,3712]{1,0:T(8,128)(2,1)}, bf16[64,3712]{1,0:T(8,128)(2,1)S(1)}, u32[]{:S(2)}, u32[]{:S(2)}) collective-permute-start(bf16[64,3712]{1,0:T(8,128)(2,1)} %get-tuple-element.17), channel_id=1, source_target_pairs={{0,1},{1,0},{2,3},{3,2},{4,5},{5,4},{6,7},{7,6},{8,9},{9,8},{10,11... | collective-permute-start | bytes 1425416 | tf_op jit(solution)/shard_map/ppermute | solution.py:37
  128.7 3.2 %collective-permute-start.9 = (bf16[64,3712]{1,0:T(8,128)(2,1)}, bf16[64,3712]{1,0:T(8,128)(2,1)S(1)}, u32[]{:S(2)}, u32[]{:S(2)}) collective-permute-start(bf16[64,3712]{1,0:T(8,128)(2,1)} %get-tuple-element.18), channel_id=1, source_target_pairs={{0,6},{1,3},{2,4},{3,1},{4,2},{5,7},{6,0},{7,5},{8,14},{9,11},{10,... | collective-permute-start | bytes 1425416 | tf_op jit(solution)/shard_map/ppermute | solution.py:37
  131.9 1.0 add_convert_fusion
  132.9 7.3 %all-to-all-start.3 = ((bf16[4,16,3712]{2,1,0:T(8,128)(2,1)}), bf16[4,16,3712]{2,1,0:T(8,128)(2,1)S(1)}, u32[]{:S(2)}, u32[]{:S(2)}) async-start(bf16[4,16,3712]{2,1,0:T(8,128)(2,1)} %bitcast.39), calls=%async_computation.3 | async-start | bytes 950272 | tf_op jit(solution)/shard_map/all_to_all | solution.py:50
  140.2 0.5 collective-permute-done.9
  140.7 1.0 add_convert_fusion.1
  141.7 13.2 %all-to-all-done.3 = bf16[4,16,3712]{2,1,0:T(8,128)(2,1)S(1)} async-done(((bf16[4,16,3712]{2,1,0:T(8,128)(2,1)}), bf16[4,16,3712]{2,1,0:T(8,128)(2,1)S(1)}, u32[]{:S(2)}, u32[]{:S(2)}) %all-to-all-start.3) | async-done | bytes 475168 | tf_op jit(solution)/shard_map/all_to_all | solution.py:50
  154.9 3.6 %all-to-all-start.1 = ((bf16[4,16,3712]{2,1,0:T(8,128)(2,1)}), bf16[4,16,3712]{2,1,0:T(8,128)(2,1)S(1)}, u32[]{:S(2)}, u32[]{:S(2)}) async-start(bf16[4,16,3712]{2,1,0:T(8,128)(2,1)} %bitcast.29), calls=%async_computation.1 | async-start | bytes 950272 | tf_op jit(solution)/shard_map/all_to_all | solution.py:50
  158.4 0.7 copy-done.14
  159.2 0.7 copy-done.15
  160.1 1.1 unpack.3
  161.1 10.1 %all-to-all-done.1 = bf16[4,16,3712]{2,1,0:T(8,128)(2,1)S(1)} async-done(((bf16[4,16,3712]{2,1,0:T(8,128)(2,1)}), bf16[4,16,3712]{2,1,0:T(8,128)(2,1)S(1)}, u32[]{:S(2)}, u32[]{:S(2)}) %all-to-all-start.1) | async-done | bytes 475168 | tf_op jit(solution)/shard_map/all_to_all | solution.py:50
  171.2 1.1 unpack.2
  (57 shorter events, 1.1 us)
Async XLA Ops:
  0.6 17.1 %copy-start.11 = (bf16[1,512,128]{2,1,0:T(8,128)(2,1)S(1)}, bf16[1,512,128]{2,1,0:T(8,128)(2,1)}, u32[]{:S(2)}) copy-start(bf16[1,512,128]{2,1,0:T(8,128)(2,1)} %param.13) | copy-start | bytes 393220
  0.6 18.6 %collective-permute-start.11 = (bf16[64,3584]{1,0:T(8,128)(2,1)}, bf16[64,3584]{1,0:T(8,128)(2,1)S(1)}, u32[]{:S(2)}, u32[]{:S(2)}) collective-permute-start(bf16[64,3584]{1,0:T(8,128)(2,1)} %bitcast.93), channel_id=1, source_target_pairs={{0,32},{32,64},{64,96},{96,128},{128,160},{160,192},{192,224},{224... | collective-permute-start | bytes 1376264 | tf_op jit(solution)/shard_map/ppermute | solution.py:58
  5.1 60.9 %collective-permute-start.5 = (bf16[128,3584]{1,0:T(8,128)(2,1)}, bf16[128,3584]{1,0:T(8,128)(2,1)}, u32[]{:S(2)}, u32[]{:S(2)}) collective-permute-start(bf16[128,3584]{1,0:T(8,128)(2,1)} %bitcast.61), channel_id=1, source_target_pairs={{0,2},{1,7},{2,0},{3,5},{4,6},{5,3},{6,4},{7,1},{8,10},{9,15},{10,... | collective-permute-start | bytes 2752520 | tf_op jit(solution)/shard_map/ppermute | solution.py:37
  8.5 60.4 %collective-permute-start.6 = (bf16[3584,128]{1,0:T(8,128)(2,1)}, bf16[3584,128]{1,0:T(8,128)(2,1)}, u32[]{:S(2)}, u32[]{:S(2)}) collective-permute-start(bf16[3584,128]{1,0:T(8,128)(2,1)} %bitcast.64), channel_id=1, source_target_pairs={{0,2},{1,7},{2,0},{3,5},{4,6},{5,3},{6,4},{7,1},{8,10},{9,15},{10,... | collective-permute-start | bytes 2752520 | tf_op jit(solution)/shard_map/ppermute | solution.py:37
  10.9 61.7 %collective-permute-start.7 = (bf16[3584,128]{1,0:T(8,128)(2,1)}, bf16[3584,128]{1,0:T(8,128)(2,1)}, u32[]{:S(2)}, u32[]{:S(2)}) collective-permute-start(bf16[3584,128]{1,0:T(8,128)(2,1)} %bitcast.67), channel_id=1, source_target_pairs={{0,2},{1,7},{2,0},{3,5},{4,6},{5,3},{6,4},{7,1},{8,10},{9,15},{10,... | collective-permute-start | bytes 2752520 | tf_op jit(solution)/shard_map/ppermute | solution.py:37
  14.3 17.4 %collective-permute-start = (bf16[64,3584]{1,0:T(8,128)(2,1)}, bf16[64,3584]{1,0:T(8,128)(2,1)S(1)}, u32[]{:S(2)}, u32[]{:S(2)}) collective-permute-start(bf16[64,3584]{1,0:T(8,128)(2,1)} %bitcast.94), channel_id=1, source_target_pairs={{0,480},{32,0},{64,32},{96,64},{128,96},{160,128},{192,160},{224,1... | collective-permute-start | bytes 1376264 | tf_op jit(solution)/shard_map/ppermute | solution.py:58
  18.6 0.7 copy-start.16
  20.4 11.3 %copy-start.7 = (bf16[1,512,128]{2,1,0:T(8,128)(2,1)S(1)}, bf16[1,512,128]{2,1,0:T(8,128)(2,1)}, u32[]{:S(2)}) copy-start(bf16[1,512,128]{2,1,0:T(8,128)(2,1)} %param.16) | copy-start | bytes 393220
  20.4 11.3 %copy-start.9 = (bf16[1,512,128]{2,1,0:T(8,128)(2,1)S(1)}, bf16[1,512,128]{2,1,0:T(8,128)(2,1)}, u32[]{:S(2)}) copy-start(bf16[1,512,128]{2,1,0:T(8,128)(2,1)} %param.14) | copy-start | bytes 393220
  20.4 30.3 %all-to-all-start.2 = ((bf16[4,16,3584]{2,1,0:T(8,128)(2,1)}), bf16[4,16,3584]{2,1,0:T(8,128)(2,1)S(1)}, u32[]{:S(2)}, u32[]{:S(2)}) async-start(bf16[4,16,3584]{2,1,0:T(8,128)(2,1)} %bitcast.35), calls=%async_computation.2 | async-start | bytes 917504 | tf_op jit(solution)/shard_map/all_to_all | solution.py:50
  30.8 0.7 copy-start.17
  31.8 48.4 %copy-start.2 = (bf16[1,3584,128]{2,1,0:T(8,128)(2,1)S(1)}, bf16[1,3584,128]{2,1,0:T(8,128)(2,1)}, u32[]{:S(2)}) copy-start(bf16[1,3584,128]{2,1,0:T(8,128)(2,1)} %param.24) | copy-start | bytes 2752516
  50.7 0.8 copy-start.3
  51.4 28.8 %copy-start = (bf16[1,128,3584]{2,1,0:T(8,128)(2,1)S(1)}, bf16[1,128,3584]{2,1,0:T(8,128)(2,1)}, u32[]{:S(2)}) copy-start(bf16[1,128,3584]{2,1,0:T(8,128)(2,1)} %param.25) | copy-start | bytes 2752516
  51.4 28.8 %copy-start.1 = (bf16[1,3584,128]{2,1,0:T(8,128)(2,1)S(1)}, bf16[1,3584,128]{2,1,0:T(8,128)(2,1)}, u32[]{:S(2)}) copy-start(bf16[1,3584,128]{2,1,0:T(8,128)(2,1)} %param.23) | copy-start | bytes 2752516
  51.4 17.7 %all-to-all-start = ((bf16[4,16,3584]{2,1,0:T(8,128)(2,1)}), bf16[4,16,3584]{2,1,0:T(8,128)(2,1)S(1)}, u32[]{:S(2)}, u32[]{:S(2)}) async-start(bf16[4,16,3584]{2,1,0:T(8,128)(2,1)} %bitcast.90), calls=%async_computation | async-start | bytes 917504 | tf_op jit(solution)/shard_map/all_to_all | solution.py:50
  55.1 8.3 %collective-permute-start.4 = (bf16[4,2,4,2,16,128]{5,4,3,2,1,0:T(8,128)(2,1)S(1)}, bf16[4,2,4,2,16,128]{5,4,3,2,1,0:T(8,128)(2,1)S(1)}, u32[]{:S(2)}, u32[]{:S(2)}) collective-permute-start(bf16[4,2,4,2,16,128]{5,4,3,2,1,0:T(8,128)(2,1)S(1)} %pad_maximum_fusion), channel_id=1, source_target_pairs={{0,2},{1,7},{2,0},{3,5},{4,6},{5,3},{6,4},{7,1},{8,10},{9,15},{10,... | collective-permute-start | bytes 786440 | tf_op jit(solution)/shard_map/ppermute | solution.py:37
  57.1 15.6 %collective-permute-start.12 = (bf16[64,3584]{1,0:T(8,128)(2,1)}, bf16[64,3584]{1,0:T(8,128)(2,1)}, u32[]{:S(2)}, u32[]{:S(2)}) collective-permute-start(bf16[64,3584]{1,0:T(8,128)(2,1)} %bitcast.76), channel_id=1, source_target_pairs={{0,1},{1,0},{2,3},{3,2},{4,5},{5,4},{6,7},{7,6},{8,9},{9,8},{10,11... | collective-permute-start | bytes 1376264 | tf_op jit(solution)/shard_map/ppermute | solution.py:37
  63.4 14.7 %collective-permute-start.13 = (bf16[64,3584]{1,0:T(8,128)(2,1)}, bf16[64,3584]{1,0:T(8,128)(2,1)}, u32[]{:S(2)}, u32[]{:S(2)}) collective-permute-start(bf16[64,3584]{1,0:T(8,128)(2,1)} %bitcast.77), channel_id=1, source_target_pairs={{0,6},{1,3},{2,4},{3,1},{4,2},{5,7},{6,0},{7,5},{8,14},{9,11},{10,... | collective-permute-start | bytes 1376264 | tf_op jit(solution)/shard_map/ppermute | solution.py:37
  66.0 14.2 %collective-permute-start.14 = (bf16[64,3584]{1,0:T(8,128)(2,1)}, bf16[64,3584]{1,0:T(8,128)(2,1)}, u32[]{:S(2)}, u32[]{:S(2)}) collective-permute-start(bf16[64,3584]{1,0:T(8,128)(2,1)} %bitcast.78), channel_id=1, source_target_pairs={{0,3},{1,6},{2,1},{3,4},{4,7},{5,2},{6,5},{7,0},{8,11},{9,14},{10,... | collective-permute-start | bytes 1376264 | tf_op jit(solution)/shard_map/ppermute | solution.py:37
  69.1 31.2 %collective-permute-start.1 = (bf16[64,3584]{1,0:T(8,128)(2,1)S(1)}, bf16[64,3584]{1,0:T(8,128)(2,1)}, u32[]{:S(2)}, u32[]{:S(2)}) collective-permute-start(bf16[64,3584]{1,0:T(8,128)(2,1)S(1)} %bitcast.72), channel_id=1, source_target_pairs={{0,1},{1,0},{2,3},{3,2},{4,5},{5,4},{6,7},{7,6},{8,9},{9,8},{10,11... | collective-permute-start | bytes 1376264 | tf_op jit(solution)/shard_map/ppermute | solution.py:37
  80.2 1.0 copy-start.4
  81.2 0.9 copy-start.8
  82.1 0.9 copy-start.10
  83.0 34.9 %copy-start.12 = (bf16[1,512,128]{2,1,0:T(8,128)(2,1)S(1)}, bf16[1,512,128]{2,1,0:T(8,128)(2,1)}, u32[]{:S(2)}) copy-start(bf16[1,512,128]{2,1,0:T(8,128)(2,1)} %param.13) | copy-start | bytes 393220
  83.0 34.9 %copy-start.13 = (bf16[1,512,128]{2,1,0:T(8,128)(2,1)S(1)}, bf16[1,512,128]{2,1,0:T(8,128)(2,1)}, u32[]{:S(2)}) copy-start(bf16[1,512,128]{2,1,0:T(8,128)(2,1)} %param.15) | copy-start | bytes 393220
  89.4 39.3 %collective-permute-start.15 = (bf16[64,3712]{1,0:T(8,128)(2,1)S(1)}, bf16[64,3712]{1,0:T(8,128)(2,1)S(1)}, u32[]{:S(2)}, u32[]{:S(2)}) collective-permute-start(bf16[64,3712]{1,0:T(8,128)(2,1)S(1)} %get-tuple-element.22), channel_id=1, source_target_pairs={{0,1},{1,0},{2,3},{3,2},{4,5},{5,4},{6,7},{7,6},{8,9},{9,8},{10,11... | collective-permute-start | bytes 1425416 | tf_op jit(solution)/shard_map/ppermute | solution.py:37
  91.3 40.6 %collective-permute-start.16 = (bf16[64,3712]{1,0:T(8,128)(2,1)S(1)}, bf16[64,3712]{1,0:T(8,128)(2,1)S(1)}, u32[]{:S(2)}, u32[]{:S(2)}) collective-permute-start(bf16[64,3712]{1,0:T(8,128)(2,1)S(1)} %get-tuple-element.23), channel_id=1, source_target_pairs={{0,6},{1,3},{2,4},{3,1},{4,2},{5,7},{6,0},{7,5},{8,14},{9,11},{10,... | collective-permute-start | bytes 1425416 | tf_op jit(solution)/shard_map/ppermute | solution.py:37
  93.9 38.0 %collective-permute-start.17 = (bf16[64,3712]{1,0:T(8,128)(2,1)S(1)}, bf16[64,3712]{1,0:T(8,128)(2,1)S(1)}, u32[]{:S(2)}, u32[]{:S(2)}) collective-permute-start(bf16[64,3712]{1,0:T(8,128)(2,1)S(1)} %get-tuple-element.24), channel_id=1, source_target_pairs={{0,7},{1,2},{2,5},{3,0},{4,3},{5,6},{6,1},{7,4},{8,15},{9,10},{10,... | collective-permute-start | bytes 1425416 | tf_op jit(solution)/shard_map/ppermute | solution.py:37
  95.9 22.0 %collective-permute-start.2 = (bf16[64,3584]{1,0:T(8,128)(2,1)S(1)}, bf16[64,3584]{1,0:T(8,128)(2,1)S(1)}, u32[]{:S(2)}, u32[]{:S(2)}) collective-permute-start(bf16[64,3584]{1,0:T(8,128)(2,1)S(1)} %bitcast.73), channel_id=1, source_target_pairs={{0,6},{1,3},{2,4},{3,1},{4,2},{5,7},{6,0},{7,5},{8,14},{9,11},{10,... | collective-permute-start | bytes 1376264 | tf_op jit(solution)/shard_map/ppermute | solution.py:37
  100.4 17.6 %collective-permute-start.3 = (bf16[64,3584]{1,0:T(8,128)(2,1)S(1)}, bf16[64,3584]{1,0:T(8,128)(2,1)S(1)}, u32[]{:S(2)}, u32[]{:S(2)}) collective-permute-start(bf16[64,3584]{1,0:T(8,128)(2,1)S(1)} %bitcast.74), channel_id=1, source_target_pairs={{0,3},{1,6},{2,1},{3,4},{4,7},{5,2},{6,5},{7,0},{8,11},{9,14},{10,... | collective-permute-start | bytes 1376264 | tf_op jit(solution)/shard_map/ppermute | solution.py:37
  124.8 8.1 %copy-start.5 = (bf16[64,3712]{1,0:T(8,128)(2,1)}, bf16[64,3712]{1,0:T(8,128)(2,1)S(1)}, u32[]{:S(2)}) copy-start(bf16[64,3712]{1,0:T(8,128)(2,1)S(1)} %get-tuple-element.16) | copy-start | bytes 1425412
  124.8 15.4 %collective-permute-start.10 = (bf16[64,3712]{1,0:T(8,128)(2,1)}, bf16[64,3712]{1,0:T(8,128)(2,1)S(1)}, u32[]{:S(2)}, u32[]{:S(2)}) collective-permute-start(bf16[64,3712]{1,0:T(8,128)(2,1)} %get-tuple-element.19), channel_id=1, source_target_pairs={{0,7},{1,2},{2,5},{3,0},{4,3},{5,6},{6,1},{7,4},{8,15},{9,10},{10,... | collective-permute-start | bytes 1425416 | tf_op jit(solution)/shard_map/ppermute | solution.py:37
  126.8 13.4 %collective-permute-start.8 = (bf16[64,3712]{1,0:T(8,128)(2,1)}, bf16[64,3712]{1,0:T(8,128)(2,1)S(1)}, u32[]{:S(2)}, u32[]{:S(2)}) collective-permute-start(bf16[64,3712]{1,0:T(8,128)(2,1)} %get-tuple-element.17), channel_id=1, source_target_pairs={{0,1},{1,0},{2,3},{3,2},{4,5},{5,4},{6,7},{7,6},{8,9},{9,8},{10,11... | collective-permute-start | bytes 1425416 | tf_op jit(solution)/shard_map/ppermute | solution.py:37
  128.7 12.0 %collective-permute-start.9 = (bf16[64,3712]{1,0:T(8,128)(2,1)}, bf16[64,3712]{1,0:T(8,128)(2,1)S(1)}, u32[]{:S(2)}, u32[]{:S(2)}) collective-permute-start(bf16[64,3712]{1,0:T(8,128)(2,1)} %get-tuple-element.18), channel_id=1, source_target_pairs={{0,6},{1,3},{2,4},{3,1},{4,2},{5,7},{6,0},{7,5},{8,14},{9,11},{10,... | collective-permute-start | bytes 1425416 | tf_op jit(solution)/shard_map/ppermute | solution.py:37
  132.9 7.8 %copy-start.6 = (bf16[64,3712]{1,0:T(8,128)(2,1)S(1)}, bf16[64,3712]{1,0:T(8,128)(2,1)}, u32[]{:S(2)}) copy-start(bf16[64,3712]{1,0:T(8,128)(2,1)} %copy-done.5) | copy-start | bytes 1425412
  132.9 21.9 %all-to-all-start.3 = ((bf16[4,16,3712]{2,1,0:T(8,128)(2,1)}), bf16[4,16,3712]{2,1,0:T(8,128)(2,1)S(1)}, u32[]{:S(2)}, u32[]{:S(2)}) async-start(bf16[4,16,3712]{2,1,0:T(8,128)(2,1)} %bitcast.39), calls=%async_computation.3 | async-start | bytes 950272 | tf_op jit(solution)/shard_map/all_to_all | solution.py:50
  154.9 16.4 %all-to-all-start.1 = ((bf16[4,16,3712]{2,1,0:T(8,128)(2,1)}), bf16[4,16,3712]{2,1,0:T(8,128)(2,1)S(1)}, u32[]{:S(2)}, u32[]{:S(2)}) async-start(bf16[4,16,3712]{2,1,0:T(8,128)(2,1)} %bitcast.29), calls=%async_computation.1 | async-start | bytes 950272 | tf_op jit(solution)/shard_map/all_to_all | solution.py:50
  158.4 0.7 copy-start.14
  159.2 0.7 copy-start.15

commit v2 on v0

v2 whole, which is shorter than its diff:
```python
import functools

import jax
import jax.numpy as jnp
from jax import lax
from jax.experimental import pallas as pl
from jax.experimental.pallas import tpu as pltpu
from jax.sharding import PartitionSpec as P

EXPERTS = 4
CAP = 16
NX = 4
NC = 2
PAD = 128
TILE = 512


def place(z, x, c):
    return z * NX * NC + x * NC + c


def weight_partner(x, c):
    return (((x + c) ^ 1) + NX - c) % NX


def token_partner(x, c):
    return weight_partner(x, 1 - c)


def moved(value, rule):
    pairs = []
    for z in range(EXPERTS):
        for x in range(NX):
            for c in range(NC):
                to_x, to_c = rule(x, c)
                pairs.append((place(z, x, c), place(z, to_x, to_c)))
    return lax.ppermute(value, "expert", pairs)


def to_weight_partner(value):
    return moved(value, lambda x, c: (weight_partner(x, c), c))


def to_sibling(value):
    return moved(value, lambda x, c: (x, 1 - c))


def over_z(value):
    columns = [[place(z, x, c) for z in range(EXPERTS)] for x in range(NX) for c in range(NC)]
    return lax.all_to_all(
        value, "expert", split_axis=0, concat_axis=0, axis_index_groups=columns, tiled=True
    )


def along_z(value, dz):
    return lax.ppermute(
        value,
        "expert",
        [
            (place(z, x, c), place((z + dz) % EXPERTS, x, c))
            for z in range(EXPERTS)
            for x in range(NX)
            for c in range(NC)
        ],
    )


def exchange_z(blocks):
    arrived = [blocks[0]]
    for dz in range(1, EXPERTS):
        arrived.append(along_z(blocks[dz], dz))
    return arrived


def passed_along(value, steps):
    count = lax.axis_size("section")
    pairs = [(source, (source + steps) % count) for source in range(count)]
    return lax.ppermute(value, "section", pairs)


def slots_of(route):
    onehot = (route == jnp.arange(EXPERTS, dtype=jnp.int32)[None, :]).astype(jnp.float32)
    size = onehot.shape[0]
    before = jnp.tril(jnp.ones((size, size), jnp.float32), -1)
    rank = jnp.dot(before, onehot)
    slot = jnp.sum(rank * onehot, axis=-1, keepdims=True).astype(jnp.int32)
    return route * CAP + slot


def table(place_of):
    lanes = jnp.arange(EXPERTS * CAP, dtype=jnp.int32)[None, :]
    return (place_of == lanes).astype(jnp.bfloat16)


def nt(a, b):
    return lax.dot_general(a, b, (((1,), (1,)), ((), ())), preferred_element_type=jnp.float32)


def expert_kernel(
    pos, own, sib, same, cross, gate_own, up_own, far,
    wd_own, wd_mate, wg_own, wg_mate, wu_own, wu_mate,
    p_own, p_sib, p_same, p_cross, *, which,
):
    x, c, tp = pos[0], pos[1], pos[2]
    n, wide = own.shape
    dh = None
    for d in range(0, wide, TILE):
        cut = slice(d, d + TILE)
        rows = jnp.concatenate([own[:, cut], sib[:, cut], same[:, cut], cross[:, cut]], axis=0)
        wd = jnp.concatenate([wd_own[:, cut], wd_mate[:, cut]], axis=0)
        term = nt(rows, wd)
        dh = term if dh is None else dh + term

    def saved(near, k):
        blocks = []
        for slot, xs in ((0, x), (1, tp)):
            for cs in (c, 1 - c):
                for z in range(EXPERTS):
                    mine = near[z * NX * NC + xs * NC + cs]
                    away = far[2 * which + k, (slot * EXPERTS + z) * NC + cs]
                    blocks.append(jnp.concatenate([mine, away], axis=-1))
        return jnp.concatenate(blocks, axis=0).astype(jnp.float32)

    gate = saved(gate_own, 0)
    up = saved(up_own, 1)
    sig = jax.nn.sigmoid(gate)
    act = gate * sig
    slope = sig * (1.0 + gate * (1.0 - sig))
    q = jnp.sum(dh * (act * up), axis=-1, keepdims=True)
    dg = (dh * up * slope).astype(jnp.bfloat16)
    du = (dh * act).astype(jnp.bfloat16)
    both = jnp.concatenate([dg, du], axis=-1)
    outs = (p_own, p_sib, p_same, p_cross)
    for d in range(0, wide, TILE):
        cut = slice(d, d + TILE)
        w = jnp.concatenate([wg_own[cut], wg_mate[cut], wu_own[cut], wu_mate[cut]], axis=-1)
        part = nt(both, w).astype(jnp.bfloat16)
        for k, out in enumerate(outs):
            out[:, cut] = part[k * n:(k + 1) * n]
    q = jnp.broadcast_to(q, (q.shape[0], PAD)).astype(jnp.bfloat16)
    for k, out in enumerate(outs):
        out[:, wide:] = q[k * n:(k + 1) * n]


def expert_work(pos, pieces, near, far, weights, which):
    count, wide = pieces[0].shape
    shape = jax.ShapeDtypeStruct((count, wide + PAD), jnp.bfloat16)
    vmem = pl.BlockSpec(memory_space=pltpu.VMEM)
    return pl.pallas_call(
        functools.partial(expert_kernel, which=which),
        in_specs=[pl.BlockSpec(memory_space=pltpu.SMEM)] + [vmem] * 13,
        out_specs=[vmem] * 4,
        out_shape=[shape] * 4,
        compiler_params=pltpu.CompilerParams(vmem_limit_bytes=20 << 20),
        name="expert_work",
    )(pos, *pieces, *near, far, *weights)


def total_kernel(pos, own, sib, same, cross, *outs):
    for k, out in enumerate(outs):
        z = pos[k]
        total = own[z].astype(jnp.float32) + sib[z].astype(jnp.float32)
        total = total + same[z].astype(jnp.float32) + cross[z].astype(jnp.float32)
        out[...] = total.astype(jnp.bfloat16)


def total_blocks(pos, parts):
    wide = parts[0].shape[1]
    parts = [v.reshape(EXPERTS, CAP, wide) for v in parts]
    vmem = pl.BlockSpec(memory_space=pltpu.VMEM)
    return pl.pallas_call(
        total_kernel,
        in_specs=[pl.BlockSpec(memory_space=pltpu.SMEM)] + [vmem] * 4,
        out_specs=[vmem] * EXPERTS,
        out_shape=[jax.ShapeDtypeStruct((CAP, wide), jnp.bfloat16)] * EXPERTS,
        compiler_params=pltpu.CompilerParams(vmem_limit_bytes=8 << 20),
        name="total_blocks",
    )(pos, *parts)


def unpack_kernel(chosen, probs, *refs):
    grad_x, grad_p = refs[-2:]
    wide = grad_x.shape[-1]
    back = jnp.concatenate([ref[...] for ref in refs[:-2]], axis=0)
    picked = jnp.dot(chosen[...], back[:, :wide], preferred_element_type=jnp.float32)
    grad_x[...] = (probs[...] * picked).astype(jnp.bfloat16)
    shares = back[:, wide:].astype(jnp.float32).T.astype(jnp.bfloat16)
    grad_p[...] = nt(shares, chosen[...])[:1]


def unpack(chosen, probs, *blocks):
    count = chosen.shape[0]
    vmem = pl.BlockSpec(memory_space=pltpu.VMEM)
    grad_x, grad_p = pl.pallas_call(
        unpack_kernel,
        in_specs=[vmem] * (2 + len(blocks)),
        out_specs=[vmem] * 2,
        out_shape=[
            jax.ShapeDtypeStruct((count, blocks[0].shape[-1] - PAD), jnp.bfloat16),
            jax.ShapeDtypeStruct((1, count), jnp.float32),
        ],
        compiler_params=pltpu.CompilerParams(vmem_limit_bytes=8 << 20),
        name="unpack",
    )(chosen, probs, *blocks)
    return grad_x[None], grad_p[..., None]


def gather_rows(own):
    same = moved(own, lambda x, c: (token_partner(x, c), c))
    cross = moved(own, lambda x, c: (token_partner(x, 1 - c), 1 - c))
    sib = to_sibling(own)
    return own, sib, same, cross


def reduce_rows(p_own, p_sib, p_same, p_cross):
    same = moved(p_same, lambda x, c: (token_partner(x, c), c))
    cross = moved(p_cross, lambda x, c: (token_partner(x, c), 1 - c))
    sib = to_sibling(p_sib)
    return p_own, sib, same, cross


def total_of(parts):
    total = parts[0].astype(jnp.float32) + parts[1].astype(jnp.float32)
    total = total + parts[2].astype(jnp.float32) + parts[3].astype(jnp.float32)
    return total.astype(jnp.bfloat16)


def on_device(
    pre_gate_a, pre_gate_b, pre_up_a, pre_up_b, grads_a, grads_b,
    route_a, route_b, probs_a, probs_b, w_gate, w_up, w_down,
):
    upper = passed_along(grads_a, -1)
    lower = passed_along(grads_b, 1)
    me = lax.axis_index("expert")
    core = me % NC
    x = (me // NC) % NX
    mate = weight_partner(x, core)
    pos = jnp.stack([x, core, token_partner(x, core)]).astype(jnp.int32)
    pre = [v[0].reshape(-1, CAP, v.shape[-1]) for v in (pre_gate_a, pre_up_a, pre_gate_b, pre_up_b)]

    def wanted(v):
        grid = v.reshape(EXPERTS, NX, NC, CAP, v.shape[-1])
        pair = [lax.dynamic_index_in_dim(grid, k, 1, False) for k in (mate, (x + 2) % NX)]
        return jnp.stack(pair)

    weights = []
    for w in (w_down[0], w_gate[0], w_up[0]):
        weights += [w, to_weight_partner(w)]
    far = to_weight_partner(jnp.stack([wanted(v) for v in pre]))
    far = far.reshape(len(pre), -1, CAP, far.shape[-1])

    home = me // (NX * NC)
    order = jnp.arange(EXPERTS, dtype=jnp.int32)
    ahead = ((home + order) % EXPERTS).astype(jnp.int32)
    wide = upper.shape[-1]

    def partials(own, near, which):
        pieces = gather_rows(own)
        parts = expert_work(pos, pieces, near, far, weights, which)
        return reduce_rows(*parts)

    chosen_a = table(slots_of(route_a[0]))
    send_a = lax.dot_general(
        chosen_a, upper[0], (((0,), (0,)), ((), ())), preferred_element_type=jnp.float32
    ).astype(jnp.bfloat16)
    own_a = over_z(send_a.reshape(EXPERTS, CAP, wide)).reshape(EXPERTS * CAP, wide)
    total_a = total_of(partials(own_a, (pre[0], pre[1]), 0))
    back_a = over_z(total_a.reshape(EXPERTS, CAP, -1)).reshape(EXPERTS * CAP, -1)
    dx_a, dprob_a = unpack(chosen_a, probs_a[0], back_a)

    slot_b = slots_of(route_b[0])
    send_b = lax.dot_general(
        table(slot_b), lower[0], (((0,), (0,)), ((), ())), preferred_element_type=jnp.float32
    ).astype(jnp.bfloat16)
    own_b = over_z(send_b.reshape(EXPERTS, CAP, wide)).reshape(EXPERTS * CAP, wide)
    parts_b = partials(own_b, (pre[2], pre[3]), 1)
    back_b = exchange_z(total_blocks(ahead, parts_b))
    turned = (home - slot_b // CAP) % EXPERTS * CAP + slot_b % CAP
    dx_b, dprob_b = unpack(table(turned), probs_b[0], *back_b)
    return (dx_a, dx_b, dprob_a, dprob_b)


def solution(mesh):
    hidden = P("section", None, "expert")
    tokens = P("section", "expert", None)

    return jax.shard_map(
        on_device,
        mesh=mesh,
        in_specs=(hidden,) * 4 + (tokens,) * 6 + (hidden, hidden, tokens),
        out_specs=(tokens,) * 4,
        check_vma=False,
    )
```

time: 176 us -> 166 us (0.943)
  the two profiles are of different devices: /device:TPU:24 before, /device:TPU:1 now
where the time goes in v2:
time: 166 us; the launch traced here: 165 us
  starting transfers between devices  96.1 us (58%)
  waiting for transfers between devices  35.4 us (21%)
  Pallas kernels  14 us (8%)
  local copies, waits for them, and re-layouts  11.9 us (7%)
  matrix products  3.9 us (2%)
  other arithmetic  2.66 us (2%)
    ppermute x16, starting transfers between devices, moved(): return lax.ppermute(value, 'expert', pairs)  49.4 us
    all_to_all x3, starting transfers between devices, over_z(): lax.all_to_all(value, 'expert', split_axis=0, concat_axis=0, axis_index_g...  22.3 us
    ppermute x16, waiting for transfers between devices, moved(): return lax.ppermute(value, 'expert', pairs)  16.7 us
    ppermute x3, starting transfers between devices, along_z(): lax.ppermute(value, 'expert', [(place(z, x, c), place((z + dz) % EXPERTS,...  14.6 us
    pallas_call x2, Pallas kernels, expert_work(): pl.pallas_call(functools.partial(expert_kernel, which=which), in_specs=[p...  11.1 us
    unnamed x40, local copies, waits for them, and re-layouts  10.9 us
    ppermute x2, starting transfers between devices, passed_along(): return lax.ppermute(value, 'section', pairs)  9.78 us
    ppermute x3, waiting for transfers between devices, along_z(): lax.ppermute(value, 'expert', [(place(z, x, c), place((z + dz) % EXPERTS,...  9.2 us
  transfers between devices with their start and end apart: 24, of which 7 were waited for; matrix products, arithmetic and copies ran while one was open for 5% of the time, Pallas kernels for 8%

profile of v2, /device:TPU:1, one launch (start us, length us, event | category | flops | bytes accessed | tf_op | source)
XLA Modules:
  0.0 165.2 jit_solution(15874034614569595893)
XLA Ops:
  0.6 5.0 %collective-permute-start.11 = (bf16[1,64,3584]{2,1,0:T(8,128)(2,1)}, bf16[1,64,3584]{2,1,0:T(8,128)(2,1)}, u32[]{:S(2)}, u32[]{:S(2)}) collective-permute-start(bf16[1,64,3584]{2,1,0:T(8,128)(2,1)} %param.18), channel_id=1, source_target_pairs={{0,32},{32,64},{64,96},{96,128},{128,160},{160,192},{192,224},{224... | collective-permute-start | bytes 1376264 | tf_op jit(solution)/shard_map/ppermute | solution.py:78
  5.6 4.4 %collective-permute-start.5 = (bf16[128,3584]{1,0:T(8,128)(2,1)}, bf16[128,3584]{1,0:T(8,128)(2,1)S(1)}, u32[]{:S(2)}, u32[]{:S(2)}) collective-permute-start(bf16[128,3584]{1,0:T(8,128)(2,1)} %bitcast.66), channel_id=1, source_target_pairs={{0,2},{1,7},{2,0},{3,5},{4,6},{5,3},{6,4},{7,1},{8,10},{9,15},{10,... | collective-permute-start | bytes 2752520 | tf_op jit(solution)/shard_map/ppermute | solution.py:37
  10.0 2.1 %collective-permute-start.6 = (bf16[3584,128]{1,0:T(8,128)(2,1)}, bf16[3584,128]{1,0:T(8,128)(2,1)}, u32[]{:S(2)}, u32[]{:S(2)}) collective-permute-start(bf16[3584,128]{1,0:T(8,128)(2,1)} %bitcast.69), channel_id=1, source_target_pairs={{0,2},{1,7},{2,0},{3,5},{4,6},{5,3},{6,4},{7,1},{8,10},{9,15},{10,... | collective-permute-start | bytes 2752520 | tf_op jit(solution)/shard_map/ppermute | solution.py:37
  12.1 4.4 %collective-permute-start.7 = (bf16[3584,128]{1,0:T(8,128)(2,1)}, bf16[3584,128]{1,0:T(8,128)(2,1)}, u32[]{:S(2)}, u32[]{:S(2)}) collective-permute-start(bf16[3584,128]{1,0:T(8,128)(2,1)} %bitcast.72), channel_id=1, source_target_pairs={{0,2},{1,7},{2,0},{3,5},{4,6},{5,3},{6,4},{7,1},{8,10},{9,15},{10,... | collective-permute-start | bytes 2752520 | tf_op jit(solution)/shard_map/ppermute | solution.py:37
  16.5 4.8 %collective-permute-start = (bf16[1,64,3584]{2,1,0:T(8,128)(2,1)}, bf16[1,64,3584]{2,1,0:T(8,128)(2,1)S(1)}, u32[]{:S(2)}, u32[]{:S(2)}) collective-permute-start(bf16[1,64,3584]{2,1,0:T(8,128)(2,1)} %param.17), channel_id=1, source_target_pairs={{0,480},{32,0},{64,32},{96,64},{128,96},{160,128},{192,160},{224,1... | collective-permute-start | bytes 1376264 | tf_op jit(solution)/shard_map/ppermute | solution.py:78
  21.5 0.8 dynamic-slice_bitcast_fusion.5
  23.3 6.7 %collective-permute-done = bf16[1,64,3584]{2,1,0:T(8,128)(2,1)S(1)} collective-permute-done((bf16[1,64,3584]{2,1,0:T(8,128)(2,1)}, bf16[1,64,3584]{2,1,0:T(8,128)(2,1)S(1)}, u32[]{:S(2)}, u32[]{:S(2)}) %collective-permute-start) | collective-permute-done | bytes 458784 | tf_op jit(solution)/shard_map/ppermute | solution.py:78
  30.0 1.2 convolution_convert_fusion.1
  31.1 10.6 %all-to-all-start = ((bf16[4,16,3584]{2,1,0:T(8,128)(2,1)}), bf16[4,16,3584]{2,1,0:T(8,128)(2,1)S(1)}, u32[]{:S(2)}, u32[]{:S(2)}) async-start(bf16[4,16,3584]{2,1,0:T(8,128)(2,1)} %bitcast.6), calls=%async_computation | async-start | bytes 917504 | tf_op jit(solution)/shard_map/all_to_all | solution.py:50
  41.9 2.1 %collective-permute-start.4 = (bf16[4,2,4,2,16,128]{5,4,3,2,1,0:T(8,128)(2,1)S(1)}, bf16[4,2,4,2,16,128]{5,4,3,2,1,0:T(8,128)(2,1)S(1)}, u32[]{:S(2)}, u32[]{:S(2)}) collective-permute-start(bf16[4,2,4,2,16,128]{5,4,3,2,1,0:T(8,128)(2,1)S(1)} %pad_maximum_fusion), channel_id=1, source_target_pairs={{0,2},{1,7},{2,0},{3,5},{4,6},{5,3},{6,4},{7,1},{8,10},{9,15},{10,... | collective-permute-start | bytes 786440 | tf_op jit(solution)/shard_map/ppermute | solution.py:37
  44.2 6.2 %collective-permute-done.4 = bf16[4,2,4,2,16,128]{5,4,3,2,1,0:T(8,128)(2,1)S(1)} collective-permute-done((bf16[4,2,4,2,16,128]{5,4,3,2,1,0:T(8,128)(2,1)S(1)}, bf16[4,2,4,2,16,128]{5,4,3,2,1,0:T(8,128)(2,1)S(1)}, u32[]{:S(2)}, u32[]{:S(2)}) %collective-permute-start.4) | collective-permute-done | bytes 262176 | tf_op jit(solution)/shard_map/ppermute | solution.py:37
  50.5 2.8 %all-to-all-done = bf16[4,16,3584]{2,1,0:T(8,128)(2,1)S(1)} async-done(((bf16[4,16,3584]{2,1,0:T(8,128)(2,1)}), bf16[4,16,3584]{2,1,0:T(8,128)(2,1)S(1)}, u32[]{:S(2)}, u32[]{:S(2)}) %all-to-all-start) | async-done | bytes 458784 | tf_op jit(solution)/shard_map/all_to_all | solution.py:50
  53.3 4.0 %collective-permute-start.1 = (bf16[64,3584]{1,0:T(8,128)(2,1)S(1)}, bf16[64,3584]{1,0:T(8,128)(2,1)}, u32[]{:S(2)}, u32[]{:S(2)}) collective-permute-start(bf16[64,3584]{1,0:T(8,128)(2,1)S(1)} %bitcast.76), channel_id=1, source_target_pairs={{0,1},{1,0},{2,3},{3,2},{4,5},{5,4},{6,7},{7,6},{8,9},{9,8},{10,11... | collective-permute-start | bytes 1376264 | tf_op jit(solution)/shard_map/ppermute | solution.py:37
  57.3 2.2 %collective-permute-start.2 = (bf16[64,3584]{1,0:T(8,128)(2,1)S(1)}, bf16[64,3584]{1,0:T(8,128)(2,1)}, u32[]{:S(2)}, u32[]{:S(2)}) collective-permute-start(bf16[64,3584]{1,0:T(8,128)(2,1)S(1)} %bitcast.77), channel_id=1, source_target_pairs={{0,6},{1,3},{2,4},{3,1},{4,2},{5,7},{6,0},{7,5},{8,14},{9,11},{10,... | collective-permute-start | bytes 1376264 | tf_op jit(solution)/shard_map/ppermute | solution.py:37
  59.5 0.9 copy-done.3
  60.4 4.4 %collective-permute-start.3 = (bf16[64,3584]{1,0:T(8,128)(2,1)S(1)}, bf16[64,3584]{1,0:T(8,128)(2,1)}, u32[]{:S(2)}, u32[]{:S(2)}) collective-permute-start(bf16[64,3584]{1,0:T(8,128)(2,1)S(1)} %bitcast.78), channel_id=1, source_target_pairs={{0,3},{1,6},{2,1},{3,4},{4,7},{5,2},{6,5},{7,0},{8,11},{9,14},{10,... | collective-permute-start | bytes 1376264 | tf_op jit(solution)/shard_map/ppermute | solution.py:37
  64.9 2.3 %convolution_convert_fusion = bf16[64,3584]{1,0:T(8,128)(2,1)} fusion(bf16[1,64,3584]{2,1,0:T(8,128)(2,1)} %collective-permute-done.11, s32[64]{0:T(128)S(1)} %get-tuple-element.37), kind=kOutput, calls=%fused_computation | convolution fusion | flops 29593600 | bytes 917760 | tf_op jit(solution)/shard_map/dot_general | solution.py:272
  67.2 5.1 %all-to-all-start.2 = ((bf16[4,16,3584]{2,1,0:T(8,128)(2,1)}), bf16[4,16,3584]{2,1,0:T(8,128)(2,1)}, u32[]{:S(2)}, u32[]{:S(2)}) async-start(bf16[4,16,3584]{2,1,0:T(8,128)(2,1)} %bitcast.95), calls=%async_computation.2 | async-start | bytes 917504 | tf_op jit(solution)/shard_map/all_to_all | solution.py:50
  72.5 1.2 copy-done.4
  73.6 0.9 copy-done.10
  74.5 0.9 copy-done.11
  75.4 5.5 %expert_work.2 = (bf16[64,3712]{1,0:T(8,128)(2,1)S(1)}, bf16[64,3712]{1,0:T(8,128)(2,1)}, bf16[64,3712]{1,0:T(8,128)(2,1)}, bf16[64,3712]{1,0:T(8,128)(2,1)}) custom-call(s32[3]{0:T(128)S(1)} %pad_add_fusion.pos, bf16[64,3584]{1,0:T(8,128)(2,1)S(1)} %bitcast.79, bf16[64,3584]{1,0:T(8,128)(2,1)} %collective-permute-done.1.sib, ...), custom_call_target="tpu_custom_call" | custom-call | tf_op jit(solution)/shard_map/expert_work/pallas_call | solution.py:149
  81.7 2.3 %collective-permute-start.10 = (bf16[64,3712]{1,0:T(8,128)(2,1)}, bf16[64,3712]{1,0:T(8,128)(2,1)S(1)}, u32[]{:S(2)}, u32[]{:S(2)}) collective-permute-start(bf16[64,3712]{1,0:T(8,128)(2,1)} %get-tuple-element.23), channel_id=1, source_target_pairs={{0,7},{1,2},{2,5},{3,0},{4,3},{5,6},{6,1},{7,4},{8,15},{9,10},{10,... | collective-permute-start | bytes 1425416 | tf_op jit(solution)/shard_map/ppermute | solution.py:37
  84.0 2.9 %collective-permute-start.8 = (bf16[64,3712]{1,0:T(8,128)(2,1)}, bf16[64,3712]{1,0:T(8,128)(2,1)}, u32[]{:S(2)}, u32[]{:S(2)}) collective-permute-start(bf16[64,3712]{1,0:T(8,128)(2,1)} %get-tuple-element.21), channel_id=1, source_target_pairs={{0,1},{1,0},{2,3},{3,2},{4,5},{5,4},{6,7},{7,6},{8,9},{9,8},{10,11... | collective-permute-start | bytes 1425416 | tf_op jit(solution)/shard_map/ppermute | solution.py:37
  87.0 3.3 %collective-permute-start.9 = (bf16[64,3712]{1,0:T(8,128)(2,1)}, bf16[64,3712]{1,0:T(8,128)(2,1)}, u32[]{:S(2)}, u32[]{:S(2)}) collective-permute-start(bf16[64,3712]{1,0:T(8,128)(2,1)} %get-tuple-element.22), channel_id=1, source_target_pairs={{0,6},{1,3},{2,4},{3,1},{4,2},{5,7},{6,0},{7,5},{8,14},{9,11},{10,... | collective-permute-start | bytes 1425416 | tf_op jit(solution)/shard_map/ppermute | solution.py:37
  90.3 2.5 %collective-permute-start.12 = (bf16[64,3584]{1,0:T(8,128)(2,1)}, bf16[64,3584]{1,0:T(8,128)(2,1)}, u32[]{:S(2)}, u32[]{:S(2)}) collective-permute-start(bf16[64,3584]{1,0:T(8,128)(2,1)} %bitcast.37.own), channel_id=1, source_target_pairs={{0,1},{1,0},{2,3},{3,2},{4,5},{5,4},{6,7},{7,6},{8,9},{9,8},{10,11... | collective-permute-start | bytes 1376264 | tf_op jit(solution)/shard_map/ppermute | solution.py:37
  92.8 3.1 %collective-permute-start.13 = (bf16[64,3584]{1,0:T(8,128)(2,1)}, bf16[64,3584]{1,0:T(8,128)(2,1)}, u32[]{:S(2)}, u32[]{:S(2)}) collective-permute-start(bf16[64,3584]{1,0:T(8,128)(2,1)} %bitcast.37.own), channel_id=1, source_target_pairs={{0,6},{1,3},{2,4},{3,1},{4,2},{5,7},{6,0},{7,5},{8,14},{9,11},{10,... | collective-permute-start | bytes 1376264 | tf_op jit(solution)/shard_map/ppermute | solution.py:37
  95.9 3.5 %collective-permute-start.14 = (bf16[64,3584]{1,0:T(8,128)(2,1)}, bf16[64,3584]{1,0:T(8,128)(2,1)}, u32[]{:S(2)}, u32[]{:S(2)}) collective-permute-start(bf16[64,3584]{1,0:T(8,128)(2,1)} %bitcast.37.own), channel_id=1, source_target_pairs={{0,3},{1,6},{2,1},{3,4},{4,7},{5,2},{6,5},{7,0},{8,11},{9,14},{10,... | collective-permute-start | bytes 1376264 | tf_op jit(solution)/shard_map/ppermute | solution.py:37
  99.5 2.3 %add_convert_fusion = bf16[64,3712]{1,0:T(8,128)(2,1)} fusion(bf16[64,3712]{1,0:T(8,128)(2,1)S(1)} %collective-permute-done.10, bf16[64,3712]{1,0:T(8,128)(2,1)} %collective-permute-done.9, bf16[64,3712]{1,0:T(8,128)(2,1)} %collective-permute-done.8, bf16[64,3712]{1,0:T(8,128)(2,1)} %copy-done.6), kind=kLoop, calls=%fused_computation.6 | loop fusion | flops 1900544 | bytes 2375680 | tf_op jit(solution)/shard_map/convert_element_type | solution.py:225
  101.8 6.6 %all-to-all-start.1 = ((bf16[4,16,3712]{2,1,0:T(8,128)(2,1)}), bf16[4,16,3712]{2,1,0:T(8,128)(2,1)S(1)}, u32[]{:S(2)}, u32[]{:S(2)}) async-start(bf16[4,16,3712]{2,1,0:T(8,128)(2,1)} %bitcast.94), calls=%async_computation.1 | async-start | bytes 950272 | tf_op jit(solution)/shard_map/all_to_all | solution.py:50
  108.4 1.2 copy-done.5
  109.6 0.9 copy-done.13
  110.5 0.9 copy-done.15
  111.4 5.6 %expert_work.3 = (bf16[64,3712]{1,0:T(8,128)(2,1)S(1)}, bf16[64,3712]{1,0:T(8,128)(2,1)}, bf16[64,3712]{1,0:T(8,128)(2,1)}, bf16[64,3712]{1,0:T(8,128)(2,1)}) custom-call(s32[3]{0:T(128)S(1)} %pad_add_fusion.pos, bf16[64,3584]{1,0:T(8,128)(2,1)} %bitcast.37.own, bf16[64,3584]{1,0:T(8,128)(2,1)} %collective-permute-done.12.sib, ...), custom_call_target="tpu_custom_call" | custom-call | tf_op jit(solution)/shard_map/expert_work/pallas_call | solution.py:149
  117.1 0.8 copy-done.7
  117.9 3.1 %collective-permute-start.15 = (bf16[64,3712]{1,0:T(8,128)(2,1)}, bf16[64,3712]{1,0:T(8,128)(2,1)S(1)}, u32[]{:S(2)}, u32[]{:S(2)}) collective-permute-start(bf16[64,3712]{1,0:T(8,128)(2,1)} %get-tuple-element.26), channel_id=1, source_target_pairs={{0,1},{1,0},{2,3},{3,2},{4,5},{5,4},{6,7},{7,6},{8,9},{9,8},{10,11... | collective-permute-start | bytes 1425416 | tf_op jit(solution)/shard_map/ppermute | solution.py:37
  120.9 1.9 %collective-permute-start.16 = (bf16[64,3712]{1,0:T(8,128)(2,1)}, bf16[64,3712]{1,0:T(8,128)(2,1)S(1)}, u32[]{:S(2)}, u32[]{:S(2)}) collective-permute-start(bf16[64,3712]{1,0:T(8,128)(2,1)} %get-tuple-element.27), channel_id=1, source_target_pairs={{0,6},{1,3},{2,4},{3,1},{4,2},{5,7},{6,0},{7,5},{8,14},{9,11},{10,... | collective-permute-start | bytes 1425416 | tf_op jit(solution)/shard_map/ppermute | solution.py:37
  122.9 3.0 %collective-permute-start.17 = (bf16[64,3712]{1,0:T(8,128)(2,1)}, bf16[64,3712]{1,0:T(8,128)(2,1)S(1)}, u32[]{:S(2)}, u32[]{:S(2)}) collective-permute-start(bf16[64,3712]{1,0:T(8,128)(2,1)} %get-tuple-element.28), channel_id=1, source_target_pairs={{0,7},{1,2},{2,5},{3,0},{4,3},{5,6},{6,1},{7,4},{8,15},{9,10},{10,... | collective-permute-start | bytes 1425416 | tf_op jit(solution)/shard_map/ppermute | solution.py:37
  126.9 4.0 %collective-permute-done.16 = bf16[64,3712]{1,0:T(8,128)(2,1)S(1)} collective-permute-done((bf16[64,3712]{1,0:T(8,128)(2,1)}, bf16[64,3712]{1,0:T(8,128)(2,1)S(1)}, u32[]{:S(2)}, u32[]{:S(2)}) %collective-permute-start.16) | collective-permute-done | bytes 475168 | tf_op jit(solution)/shard_map/ppermute | solution.py:37
  130.8 6.5 %collective-permute-done.17 = bf16[64,3712]{1,0:T(8,128)(2,1)S(1)} collective-permute-done((bf16[64,3712]{1,0:T(8,128)(2,1)}, bf16[64,3712]{1,0:T(8,128)(2,1)S(1)}, u32[]{:S(2)}, u32[]{:S(2)}) %collective-permute-start.17) | collective-permute-done | bytes 475168 | tf_op jit(solution)/shard_map/ppermute | solution.py:37
  137.3 1.0 copy-done.8
  139.1 4.2 %collective-permute-start.18 = (bf16[16,3712]{1,0:T(8,128)(2,1)S(1)}, bf16[16,3712]{1,0:T(8,128)(2,1)S(1)}, u32[]{:S(2)}, u32[]{:S(2)}) collective-permute-start(bf16[16,3712]{1,0:T(8,128)(2,1)S(1)} %get-tuple-element.30), channel_id=1, source_target_pairs={{0,8},{1,9},{2,10},{3,11},{4,12},{5,13},{6,14},{7,15},{8,16},{9,17... | collective-permute-start | bytes 356360 | tf_op jit(solution)/shard_map/ppermute | solution.py:56
  143.4 5.4 %collective-permute-start.19 = (bf16[16,3712]{1,0:T(8,128)(2,1)S(1)}, bf16[16,3712]{1,0:T(8,128)(2,1)S(1)}, u32[]{:S(2)}, u32[]{:S(2)}) collective-permute-start(bf16[16,3712]{1,0:T(8,128)(2,1)S(1)} %get-tuple-element.31), channel_id=1, source_target_pairs={{0,16},{1,17},{2,18},{3,19},{4,20},{5,21},{6,22},{7,23},{8,24},{9,... | collective-permute-start | bytes 356360 | tf_op jit(solution)/shard_map/ppermute | solution.py:56
  148.7 5.0 %collective-permute-start.20 = (bf16[16,3712]{1,0:T(8,128)(2,1)S(1)}, bf16[16,3712]{1,0:T(8,128)(2,1)S(1)}, u32[]{:S(2)}, u32[]{:S(2)}) collective-permute-start(bf16[16,3712]{1,0:T(8,128)(2,1)S(1)} %get-tuple-element.32), channel_id=1, source_target_pairs={{0,24},{1,25},{2,26},{3,27},{4,28},{5,29},{6,30},{7,31},{8,0},{9,1... | collective-permute-start | bytes 356360 | tf_op jit(solution)/shard_map/ppermute | solution.py:56
  153.9 2.7 %collective-permute-done.19.refs_2_ = bf16[16,3712]{1,0:T(8,128)(2,1)S(1)} collective-permute-done((bf16[16,3712]{1,0:T(8,128)(2,1)S(1)}, bf16[16,3712]{1,0:T(8,128)(2,1)S(1)}, u32[]{:S(2)}, u32[]{:S(2)}) %collective-permute-start.19) | collective-permute-done | bytes 118816 | tf_op jit(solution)/shard_map/ppermute | solution.py:56
  156.6 6.5 %collective-permute-done.20.refs_3_ = bf16[16,3712]{1,0:T(8,128)(2,1)S(1)} collective-permute-done((bf16[16,3712]{1,0:T(8,128)(2,1)S(1)}, bf16[16,3712]{1,0:T(8,128)(2,1)S(1)}, u32[]{:S(2)}, u32[]{:S(2)}) %collective-permute-start.20) | collective-permute-done | bytes 118816 | tf_op jit(solution)/shard_map/ppermute | solution.py:56
  163.1 1.1 unpack.3
  164.1 1.1 unpack.2
  (66 shorter events, 3.9 us)
Async XLA Ops:
  0.6 20.8 %copy-start.9 = (bf16[1,512,128]{2,1,0:T(8,128)(2,1)S(1)}, bf16[1,512,128]{2,1,0:T(8,128)(2,1)}, u32[]{:S(2)}) copy-start(bf16[1,512,128]{2,1,0:T(8,128)(2,1)} %param.13) | copy-start | bytes 393220
  0.6 56.6 %collective-permute-start.11 = (bf16[1,64,3584]{2,1,0:T(8,128)(2,1)}, bf16[1,64,3584]{2,1,0:T(8,128)(2,1)}, u32[]{:S(2)}, u32[]{:S(2)}) collective-permute-start(bf16[1,64,3584]{2,1,0:T(8,128)(2,1)} %param.18), channel_id=1, source_target_pairs={{0,32},{32,64},{64,96},{96,128},{128,160},{160,192},{192,224},{224... | collective-permute-start | bytes 1376264 | tf_op jit(solution)/shard_map/ppermute | solution.py:78
  5.6 53.9 %collective-permute-start.5 = (bf16[128,3584]{1,0:T(8,128)(2,1)}, bf16[128,3584]{1,0:T(8,128)(2,1)S(1)}, u32[]{:S(2)}, u32[]{:S(2)}) collective-permute-start(bf16[128,3584]{1,0:T(8,128)(2,1)} %bitcast.66), channel_id=1, source_target_pairs={{0,2},{1,7},{2,0},{3,5},{4,6},{5,3},{6,4},{7,1},{8,10},{9,15},{10,... | collective-permute-start | bytes 2752520 | tf_op jit(solution)/shard_map/ppermute | solution.py:37
  10.0 62.4 %collective-permute-start.6 = (bf16[3584,128]{1,0:T(8,128)(2,1)}, bf16[3584,128]{1,0:T(8,128)(2,1)}, u32[]{:S(2)}, u32[]{:S(2)}) collective-permute-start(bf16[3584,128]{1,0:T(8,128)(2,1)} %bitcast.69), channel_id=1, source_target_pairs={{0,2},{1,7},{2,0},{3,5},{4,6},{5,3},{6,4},{7,1},{8,10},{9,15},{10,... | collective-permute-start | bytes 2752520 | tf_op jit(solution)/shard_map/ppermute | solution.py:37
  12.1 60.3 %collective-permute-start.7 = (bf16[3584,128]{1,0:T(8,128)(2,1)}, bf16[3584,128]{1,0:T(8,128)(2,1)}, u32[]{:S(2)}, u32[]{:S(2)}) collective-permute-start(bf16[3584,128]{1,0:T(8,128)(2,1)} %bitcast.72), channel_id=1, source_target_pairs={{0,2},{1,7},{2,0},{3,5},{4,6},{5,3},{6,4},{7,1},{8,10},{9,15},{10,... | collective-permute-start | bytes 2752520 | tf_op jit(solution)/shard_map/ppermute | solution.py:37
  16.5 13.5 %collective-permute-start = (bf16[1,64,3584]{2,1,0:T(8,128)(2,1)}, bf16[1,64,3584]{2,1,0:T(8,128)(2,1)S(1)}, u32[]{:S(2)}, u32[]{:S(2)}) collective-permute-start(bf16[1,64,3584]{2,1,0:T(8,128)(2,1)} %param.17), channel_id=1, source_target_pairs={{0,480},{32,0},{64,32},{96,64},{128,96},{160,128},{192,160},{224,1... | collective-permute-start | bytes 1376264 | tf_op jit(solution)/shard_map/ppermute | solution.py:78
  21.5 0.9 copy-start.19
  21.5 1.1 copy-start.14
  22.3 0.9 copy-start.12
  31.1 22.1 %all-to-all-start = ((bf16[4,16,3584]{2,1,0:T(8,128)(2,1)}), bf16[4,16,3584]{2,1,0:T(8,128)(2,1)S(1)}, u32[]{:S(2)}, u32[]{:S(2)}) async-start(bf16[4,16,3584]{2,1,0:T(8,128)(2,1)} %bitcast.6), calls=%async_computation | async-start | bytes 917504 | tf_op jit(solution)/shard_map/all_to_all | solution.py:50
  41.8 2.2 %copy-start.18 = (s32[1,64,1]{1,2,0:T(1,128)S(1)}, s32[1,64,1]{1,2,0:T(1,128)}, u32[]{:S(2)}) copy-start(s32[1,64,1]{1,2,0:T(1,128)} %param.20) | copy-start | bytes 772
  41.8 30.6 %copy-start.2 = (bf16[1,3584,128]{2,1,0:T(8,128)(2,1)S(1)}, bf16[1,3584,128]{2,1,0:T(8,128)(2,1)}, u32[]{:S(2)}) copy-start(bf16[1,3584,128]{2,1,0:T(8,128)(2,1)} %param.24) | copy-start | bytes 2752516
  41.9 8.6 %collective-permute-start.4 = (bf16[4,2,4,2,16,128]{5,4,3,2,1,0:T(8,128)(2,1)S(1)}, bf16[4,2,4,2,16,128]{5,4,3,2,1,0:T(8,128)(2,1)S(1)}, u32[]{:S(2)}, u32[]{:S(2)}) collective-permute-start(bf16[4,2,4,2,16,128]{5,4,3,2,1,0:T(8,128)(2,1)S(1)} %pad_maximum_fusion), channel_id=1, source_target_pairs={{0,2},{1,7},{2,0},{3,5},{4,6},{5,3},{6,4},{7,1},{8,10},{9,15},{10,... | collective-permute-start | bytes 786440 | tf_op jit(solution)/shard_map/ppermute | solution.py:37
  53.3 19.1 %collective-permute-start.1 = (bf16[64,3584]{1,0:T(8,128)(2,1)S(1)}, bf16[64,3584]{1,0:T(8,128)(2,1)}, u32[]{:S(2)}, u32[]{:S(2)}) collective-permute-start(bf16[64,3584]{1,0:T(8,128)(2,1)S(1)} %bitcast.76), channel_id=1, source_target_pairs={{0,1},{1,0},{2,3},{3,2},{4,5},{5,4},{6,7},{7,6},{8,9},{9,8},{10,11... | collective-permute-start | bytes 1376264 | tf_op jit(solution)/shard_map/ppermute | solution.py:37
  57.3 15.1 %collective-permute-start.2 = (bf16[64,3584]{1,0:T(8,128)(2,1)S(1)}, bf16[64,3584]{1,0:T(8,128)(2,1)}, u32[]{:S(2)}, u32[]{:S(2)}) collective-permute-start(bf16[64,3584]{1,0:T(8,128)(2,1)S(1)} %bitcast.77), channel_id=1, source_target_pairs={{0,6},{1,3},{2,4},{3,1},{4,2},{5,7},{6,0},{7,5},{8,14},{9,11},{10,... | collective-permute-start | bytes 1376264 | tf_op jit(solution)/shard_map/ppermute | solution.py:37
  59.5 0.9 copy-start.3
  60.4 12.0 %collective-permute-start.3 = (bf16[64,3584]{1,0:T(8,128)(2,1)S(1)}, bf16[64,3584]{1,0:T(8,128)(2,1)}, u32[]{:S(2)}, u32[]{:S(2)}) collective-permute-start(bf16[64,3584]{1,0:T(8,128)(2,1)S(1)} %bitcast.78), channel_id=1, source_target_pairs={{0,3},{1,6},{2,1},{3,4},{4,7},{5,2},{6,5},{7,0},{8,11},{9,14},{10,... | collective-permute-start | bytes 1376264 | tf_op jit(solution)/shard_map/ppermute | solution.py:37
  64.9 7.5 %copy-start = (bf16[1,128,3584]{2,1,0:T(8,128)(2,1)S(1)}, bf16[1,128,3584]{2,1,0:T(8,128)(2,1)}, u32[]{:S(2)}) copy-start(bf16[1,128,3584]{2,1,0:T(8,128)(2,1)} %param.25) | copy-start | bytes 2752516
  64.9 7.5 %copy-start.1 = (bf16[1,3584,128]{2,1,0:T(8,128)(2,1)S(1)}, bf16[1,3584,128]{2,1,0:T(8,128)(2,1)}, u32[]{:S(2)}) copy-start(bf16[1,3584,128]{2,1,0:T(8,128)(2,1)} %param.23) | copy-start | bytes 2752516
  67.2 23.0 %all-to-all-start.2 = ((bf16[4,16,3584]{2,1,0:T(8,128)(2,1)}), bf16[4,16,3584]{2,1,0:T(8,128)(2,1)}, u32[]{:S(2)}, u32[]{:S(2)}) async-start(bf16[4,16,3584]{2,1,0:T(8,128)(2,1)} %bitcast.95), calls=%async_computation.2 | async-start | bytes 917504 | tf_op jit(solution)/shard_map/all_to_all | solution.py:50
  72.5 1.2 copy-start.4
  73.6 0.9 copy-start.10
  74.5 0.9 copy-start.11
  80.9 0.8 copy-start.6
  81.7 14.2 %collective-permute-start.10 = (bf16[64,3712]{1,0:T(8,128)(2,1)}, bf16[64,3712]{1,0:T(8,128)(2,1)S(1)}, u32[]{:S(2)}, u32[]{:S(2)}) collective-permute-start(bf16[64,3712]{1,0:T(8,128)(2,1)} %get-tuple-element.23), channel_id=1, source_target_pairs={{0,7},{1,2},{2,5},{3,0},{4,3},{5,6},{6,1},{7,4},{8,15},{9,10},{10,... | collective-permute-start | bytes 1425416 | tf_op jit(solution)/shard_map/ppermute | solution.py:37
  84.0 15.5 %collective-permute-start.8 = (bf16[64,3712]{1,0:T(8,128)(2,1)}, bf16[64,3712]{1,0:T(8,128)(2,1)}, u32[]{:S(2)}, u32[]{:S(2)}) collective-permute-start(bf16[64,3712]{1,0:T(8,128)(2,1)} %get-tuple-element.21), channel_id=1, source_target_pairs={{0,1},{1,0},{2,3},{3,2},{4,5},{5,4},{6,7},{7,6},{8,9},{9,8},{10,11... | collective-permute-start | bytes 1425416 | tf_op jit(solution)/shard_map/ppermute | solution.py:37
  87.0 12.5 %collective-permute-start.9 = (bf16[64,3712]{1,0:T(8,128)(2,1)}, bf16[64,3712]{1,0:T(8,128)(2,1)}, u32[]{:S(2)}, u32[]{:S(2)}) collective-permute-start(bf16[64,3712]{1,0:T(8,128)(2,1)} %get-tuple-element.22), channel_id=1, source_target_pairs={{0,6},{1,3},{2,4},{3,1},{4,2},{5,7},{6,0},{7,5},{8,14},{9,11},{10,... | collective-permute-start | bytes 1425416 | tf_op jit(solution)/shard_map/ppermute | solution.py:37
  90.3 18.2 %collective-permute-start.12 = (bf16[64,3584]{1,0:T(8,128)(2,1)}, bf16[64,3584]{1,0:T(8,128)(2,1)}, u32[]{:S(2)}, u32[]{:S(2)}) collective-permute-start(bf16[64,3584]{1,0:T(8,128)(2,1)} %bitcast.37.own), channel_id=1, source_target_pairs={{0,1},{1,0},{2,3},{3,2},{4,5},{5,4},{6,7},{7,6},{8,9},{9,8},{10,11... | collective-permute-start | bytes 1376264 | tf_op jit(solution)/shard_map/ppermute | solution.py:37
  92.8 15.6 %collective-permute-start.13 = (bf16[64,3584]{1,0:T(8,128)(2,1)}, bf16[64,3584]{1,0:T(8,128)(2,1)}, u32[]{:S(2)}, u32[]{:S(2)}) collective-permute-start(bf16[64,3584]{1,0:T(8,128)(2,1)} %bitcast.37.own), channel_id=1, source_target_pairs={{0,6},{1,3},{2,4},{3,1},{4,2},{5,7},{6,0},{7,5},{8,14},{9,11},{10,... | collective-permute-start | bytes 1376264 | tf_op jit(solution)/shard_map/ppermute | solution.py:37
  95.9 12.5 %collective-permute-start.14 = (bf16[64,3584]{1,0:T(8,128)(2,1)}, bf16[64,3584]{1,0:T(8,128)(2,1)}, u32[]{:S(2)}, u32[]{:S(2)}) collective-permute-start(bf16[64,3584]{1,0:T(8,128)(2,1)} %bitcast.37.own), channel_id=1, source_target_pairs={{0,3},{1,6},{2,1},{3,4},{4,7},{5,2},{6,5},{7,0},{8,11},{9,14},{10,... | collective-permute-start | bytes 1376264 | tf_op jit(solution)/shard_map/ppermute | solution.py:37
  101.8 62.3 %all-to-all-start.1 = ((bf16[4,16,3712]{2,1,0:T(8,128)(2,1)}), bf16[4,16,3712]{2,1,0:T(8,128)(2,1)S(1)}, u32[]{:S(2)}, u32[]{:S(2)}) async-start(bf16[4,16,3712]{2,1,0:T(8,128)(2,1)} %bitcast.94), calls=%async_computation.1 | async-start | bytes 950272 | tf_op jit(solution)/shard_map/all_to_all | solution.py:50
  108.4 1.2 copy-start.5
  109.6 0.9 copy-start.13
  110.5 0.9 copy-start.15
  117.1 0.8 copy-start.7
  117.9 9.0 %collective-permute-start.15 = (bf16[64,3712]{1,0:T(8,128)(2,1)}, bf16[64,3712]{1,0:T(8,128)(2,1)S(1)}, u32[]{:S(2)}, u32[]{:S(2)}) collective-permute-start(bf16[64,3712]{1,0:T(8,128)(2,1)} %get-tuple-element.26), channel_id=1, source_target_pairs={{0,1},{1,0},{2,3},{3,2},{4,5},{5,4},{6,7},{7,6},{8,9},{9,8},{10,11... | collective-permute-start | bytes 1425416 | tf_op jit(solution)/shard_map/ppermute | solution.py:37
  120.9 9.9 %collective-permute-start.16 = (bf16[64,3712]{1,0:T(8,128)(2,1)}, bf16[64,3712]{1,0:T(8,128)(2,1)S(1)}, u32[]{:S(2)}, u32[]{:S(2)}) collective-permute-start(bf16[64,3712]{1,0:T(8,128)(2,1)} %get-tuple-element.27), channel_id=1, source_target_pairs={{0,6},{1,3},{2,4},{3,1},{4,2},{5,7},{6,0},{7,5},{8,14},{9,11},{10,... | collective-permute-start | bytes 1425416 | tf_op jit(solution)/shard_map/ppermute | solution.py:37
  122.9 3.1 %copy-start.16 = (f32[1,64,1]{1,2,0:T(1,128)S(1)}, f32[1,64,1]{1,2,0:T(1,128)}, u32[]{:S(2)}) copy-start(f32[1,64,1]{1,2,0:T(1,128)} %param.22) | copy-start | bytes 772
  122.9 14.4 %collective-permute-start.17 = (bf16[64,3712]{1,0:T(8,128)(2,1)}, bf16[64,3712]{1,0:T(8,128)(2,1)S(1)}, u32[]{:S(2)}, u32[]{:S(2)}) collective-permute-start(bf16[64,3712]{1,0:T(8,128)(2,1)} %get-tuple-element.28), channel_id=1, source_target_pairs={{0,7},{1,2},{2,5},{3,0},{4,3},{5,6},{6,1},{7,4},{8,15},{9,10},{10,... | collective-permute-start | bytes 1425416 | tf_op jit(solution)/shard_map/ppermute | solution.py:37
  126.0 0.7 copy-start.17
  137.3 1.0 copy-start.8
  139.1 14.7 %collective-permute-start.18 = (bf16[16,3712]{1,0:T(8,128)(2,1)S(1)}, bf16[16,3712]{1,0:T(8,128)(2,1)S(1)}, u32[]{:S(2)}, u32[]{:S(2)}) collective-permute-start(bf16[16,3712]{1,0:T(8,128)(2,1)S(1)} %get-tuple-element.30), channel_id=1, source_target_pairs={{0,8},{1,9},{2,10},{3,11},{4,12},{5,13},{6,14},{7,15},{8,16},{9,17... | collective-permute-start | bytes 356360 | tf_op jit(solution)/shard_map/ppermute | solution.py:56
  143.4 13.2 %collective-permute-start.19 = (bf16[16,3712]{1,0:T(8,128)(2,1)S(1)}, bf16[16,3712]{1,0:T(8,128)(2,1)S(1)}, u32[]{:S(2)}, u32[]{:S(2)}) collective-permute-start(bf16[16,3712]{1,0:T(8,128)(2,1)S(1)} %get-tuple-element.31), channel_id=1, source_target_pairs={{0,16},{1,17},{2,18},{3,19},{4,20},{5,21},{6,22},{7,23},{8,24},{9,... | collective-permute-start | bytes 356360 | tf_op jit(solution)/shard_map/ppermute | solution.py:56
  148.7 14.3 %collective-permute-start.20 = (bf16[16,3712]{1,0:T(8,128)(2,1)S(1)}, bf16[16,3712]{1,0:T(8,128)(2,1)S(1)}, u32[]{:S(2)}, u32[]{:S(2)}) collective-permute-start(bf16[16,3712]{1,0:T(8,128)(2,1)S(1)} %get-tuple-element.32), channel_id=1, source_target_pairs={{0,24},{1,25},{2,26},{3,27},{4,28},{5,29},{6,30},{7,31},{8,0},{9,1... | collective-permute-start | bytes 356360 | tf_op jit(solution)/shard_map/ppermute | solution.py:56

commit v3 on v2

--- a/solution.py
+++ b/solution.py
@@ -97,12 +97,18 @@
 
 
 def expert_kernel(
-    pos, own, sib, same, cross, gate_own, up_own, far,
+    pos, near_all, far_all, own, sib, same, cross,
     wd_own, wd_mate, wg_own, wg_mate, wu_own, wu_mate,
-    p_own, p_sib, p_same, p_cross, *, which,
+    p_own, p_sib, p_same, p_cross, near, far, arrived, *, which,
 ):
     x, c, tp = pos[0], pos[1], pos[2]
     n, wide = own.shape
+    loads = [
+        pltpu.make_async_copy(ref.at[pl.ds(2 * which, 2)], buf, arrived.at[k])
+        for k, (ref, buf) in enumerate(((near_all, near), (far_all, far)))
+    ]
+    for load in loads:
+        load.start()
     dh = None
     for d in range(0, wide, TILE):
         cut = slice(d, d + TILE)
@@ -111,18 +117,21 @@
         term = nt(rows, wd)
         dh = term if dh is None else dh + term
 
-    def saved(near, k):
+    for load in loads:
+        load.wait()
+
+    def saved(k):
         blocks = []
         for slot, xs in ((0, x), (1, tp)):
             for cs in (c, 1 - c):
                 for z in range(EXPERTS):
-                    mine = near[z * NX * NC + xs * NC + cs]
-                    away = far[2 * which + k, (slot * EXPERTS + z) * NC + cs]
+                    mine = near[k, z * NX * NC + xs * NC + cs]
+                    away = far[k, (slot * EXPERTS + z) * NC + cs]
                     blocks.append(jnp.concatenate([mine, away], axis=-1))
         return jnp.concatenate(blocks, axis=0).astype(jnp.float32)
 
-    gate = saved(gate_own, 0)
-    up = saved(up_own, 1)
+    gate = saved(0)
+    up = saved(1)
     sig = jax.nn.sigmoid(gate)
     act = gate * sig
     slope = sig * (1.0 + gate * (1.0 - sig))
@@ -148,12 +157,19 @@
     vmem = pl.BlockSpec(memory_space=pltpu.VMEM)
     return pl.pallas_call(
         functools.partial(expert_kernel, which=which),
-        in_specs=[pl.BlockSpec(memory_space=pltpu.SMEM)] + [vmem] * 13,
+        in_specs=[pl.BlockSpec(memory_space=pltpu.SMEM)]
+        + [pl.BlockSpec(memory_space=pl.ANY)] * 2
+        + [vmem] * 10,
         out_specs=[vmem] * 4,
         out_shape=[shape] * 4,
+        scratch_shapes=[
+            pltpu.VMEM((2,) + near.shape[1:], near.dtype),
+            pltpu.VMEM((2,) + far.shape[1:], far.dtype),
+            pltpu.SemaphoreType.DMA((2,)),
+        ],
         compiler_params=pltpu.CompilerParams(vmem_limit_bytes=20 << 20),
         name="expert_work",
-    )(pos, *pieces, *near, far, *weights)
+    )(pos, near, far, *pieces, *weights)
 
 
 def total_kernel(pos, own, sib, same, cross, *outs):
@@ -254,7 +270,9 @@
     ahead = ((home + order) % EXPERTS).astype(jnp.int32)
     wide = upper.shape[-1]
 
-    def partials(own, near, which):
+    near = jnp.stack(pre)
+
+    def partials(own, which):
         pieces = gather_rows(own)
         parts = expert_work(pos, pieces, near, far, weights, which)
         return reduce_rows(*parts)
@@ -264,7 +282,7 @@
         chosen_a, upper[0], (((0,), (0,)), ((), ())), preferred_element_type=jnp.float32
     ).astype(jnp.bfloat16)
     own_a = over_z(send_a.reshape(EXPERTS, CAP, wide)).reshape(EXPERTS * CAP, wide)
-    total_a = total_of(partials(own_a, (pre[0], pre[1]), 0))
+    total_a = total_of(partials(own_a, 0))
     back_a = over_z(total_a.reshape(EXPERTS, CAP, -1)).reshape(EXPERTS * CAP, -1)
     dx_a, dprob_a = unpack(chosen_a, probs_a[0], back_a)
 
@@ -273,7 +291,7 @@
         table(slot_b), lower[0], (((0,), (0,)), ((), ())), preferred_element_type=jnp.float32
     ).astype(jnp.bfloat16)
     own_b = over_z(send_b.reshape(EXPERTS, CAP, wide)).reshape(EXPERTS * CAP, wide)
-    parts_b = partials(own_b, (pre[2], pre[3]), 1)
+    parts_b = partials(own_b, 1)
     back_b = exchange_z(total_blocks(ahead, parts_b))
     turned = (home - slot_b // CAP) % EXPERTS * CAP + slot_b % CAP
     dx_b, dprob_b = unpack(table(turned), probs_b[0], *back_b)

time: 166 us -> 165 us (level)
  local copies, waits for them, and re-layouts: 11.9 us -> 7.3 us
  waiting for transfers between devices: 35.4 us -> 37.3 us
  Pallas kernels: 14 us -> 15.7 us
    unnamed x40 -> x32, local copies, waits for them, and re-layouts: 10.9 us -> 6.27 us
  transfers between devices with their start and end apart: 24 -> 24, of which waited for: 7 -> 9; matrix products, arithmetic and copies ran while one was open for 5% -> 5% of each run, Pallas kernels for 8% -> 8%
where the time goes in v3:
time: 165 us; the launch traced here: 164 us
  starting transfers between devices  95.2 us (58%)
  waiting for transfers between devices  37.3 us (23%)
  Pallas kernels  15.7 us (10%)
  local copies, waits for them, and re-layouts  7.3 us (4%)
  other arithmetic  3.98 us (2%)
  matrix products  2.75 us (2%)
    ppermute x16, starting transfers between devices, moved(): return lax.ppermute(value, 'expert', pairs)  50.4 us
    all_to_all x3, starting transfers between devices, over_z(): lax.all_to_all(value, 'expert', split_axis=0, concat_axis=0, axis_index_g...  21.4 us
    ppermute x16, waiting for transfers between devices, moved(): return lax.ppermute(value, 'expert', pairs)  17.5 us
    ppermute x3, starting transfers between devices, along_z(): lax.ppermute(value, 'expert', [(place(z, x, c), place((z + dz) % EXPERTS,...  13.6 us
    pallas_call x2, Pallas kernels, expert_work(): pl.pallas_call(functools.partial(expert_kernel, which=which), in_specs=[p...  11.8 us
    ppermute x3, waiting for transfers between devices, along_z(): lax.ppermute(value, 'expert', [(place(z, x, c), place((z + dz) % EXPERTS,...  10.2 us
    ppermute x2, starting transfers between devices, passed_along(): return lax.ppermute(value, 'section', pairs)  9.77 us
    ppermute x2, waiting for transfers between devices, passed_along(): return lax.ppermute(value, 'section', pairs)  6.72 us
  transfers between devices with their start and end apart: 24, of which 9 were waited for; matrix products, arithmetic and copies ran while one was open for 5% of the time, Pallas kernels for 8%

profile of v3, /device:TPU:1, one launch (start us, length us, event | category | flops | bytes accessed | tf_op | source)
XLA Modules:
  0.0 163.6 jit_solution(4072892664053705187)
XLA Ops:
  0.6 4.9 %collective-permute-start.11 = (bf16[1,64,3584]{2,1,0:T(8,128)(2,1)}, bf16[1,64,3584]{2,1,0:T(8,128)(2,1)S(1)}, u32[]{:S(2)}, u32[]{:S(2)}) collective-permute-start(bf16[1,64,3584]{2,1,0:T(8,128)(2,1)} %param.18), channel_id=1, source_target_pairs={{0,32},{32,64},{64,96},{96,128},{128,160},{160,192},{192,224},{224... | collective-permute-start | bytes 1376264 | tf_op jit(solution)/shard_map/ppermute | solution.py:78
  5.6 4.4 %collective-permute-start.5 = (bf16[128,3584]{1,0:T(8,128)(2,1)}, bf16[128,3584]{1,0:T(8,128)(2,1)S(1)}, u32[]{:S(2)}, u32[]{:S(2)}) collective-permute-start(bf16[128,3584]{1,0:T(8,128)(2,1)} %bitcast.66), channel_id=1, source_target_pairs={{0,2},{1,7},{2,0},{3,5},{4,6},{5,3},{6,4},{7,1},{8,10},{9,15},{10,... | collective-permute-start | bytes 2752520 | tf_op jit(solution)/shard_map/ppermute | solution.py:37
  10.0 2.1 %collective-permute-start.6 = (bf16[3584,128]{1,0:T(8,128)(2,1)}, bf16[3584,128]{1,0:T(8,128)(2,1)}, u32[]{:S(2)}, u32[]{:S(2)}) collective-permute-start(bf16[3584,128]{1,0:T(8,128)(2,1)} %bitcast.69), channel_id=1, source_target_pairs={{0,2},{1,7},{2,0},{3,5},{4,6},{5,3},{6,4},{7,1},{8,10},{9,15},{10,... | collective-permute-start | bytes 2752520 | tf_op jit(solution)/shard_map/ppermute | solution.py:37
  12.1 4.4 %collective-permute-start.7 = (bf16[3584,128]{1,0:T(8,128)(2,1)}, bf16[3584,128]{1,0:T(8,128)(2,1)}, u32[]{:S(2)}, u32[]{:S(2)}) collective-permute-start(bf16[3584,128]{1,0:T(8,128)(2,1)} %bitcast.72), channel_id=1, source_target_pairs={{0,2},{1,7},{2,0},{3,5},{4,6},{5,3},{6,4},{7,1},{8,10},{9,15},{10,... | collective-permute-start | bytes 2752520 | tf_op jit(solution)/shard_map/ppermute | solution.py:37
  16.5 4.8 %collective-permute-start.1 = (bf16[1,64,3584]{2,1,0:T(8,128)(2,1)}, bf16[1,64,3584]{2,1,0:T(8,128)(2,1)S(1)}, u32[]{:S(2)}, u32[]{:S(2)}) collective-permute-start(bf16[1,64,3584]{2,1,0:T(8,128)(2,1)} %param.17), channel_id=1, source_target_pairs={{0,480},{32,0},{64,32},{96,64},{128,96},{160,128},{192,160},{224,1... | collective-permute-start | bytes 1376264 | tf_op jit(solution)/shard_map/ppermute | solution.py:78
  21.5 0.8 dynamic-slice_bitcast_fusion.5
  22.6 0.7 copy-done.9
  23.3 6.7 %collective-permute-done.1 = bf16[1,64,3584]{2,1,0:T(8,128)(2,1)S(1)} collective-permute-done((bf16[1,64,3584]{2,1,0:T(8,128)(2,1)}, bf16[1,64,3584]{2,1,0:T(8,128)(2,1)S(1)}, u32[]{:S(2)}, u32[]{:S(2)}) %collective-permute-start.1) | collective-permute-done | bytes 458784 | tf_op jit(solution)/shard_map/ppermute | solution.py:78
  30.0 1.2 convolution_convert_fusion.1
  31.1 10.6 %all-to-all-start = ((bf16[4,16,3584]{2,1,0:T(8,128)(2,1)}), bf16[4,16,3584]{2,1,0:T(8,128)(2,1)}, u32[]{:S(2)}, u32[]{:S(2)}) async-start(bf16[4,16,3584]{2,1,0:T(8,128)(2,1)} %bitcast.27), calls=%async_computation | async-start | bytes 917504 | tf_op jit(solution)/shard_map/all_to_all | solution.py:50
  41.9 2.0 %collective-permute-start = (bf16[4,2,4,2,16,128]{5,4,3,2,1,0:T(8,128)(2,1)S(1)}, bf16[4,2,4,2,16,128]{5,4,3,2,1,0:T(8,128)(2,1)S(1)}, u32[]{:S(2)}, u32[]{:S(2)}) collective-permute-start(bf16[4,2,4,2,16,128]{5,4,3,2,1,0:T(8,128)(2,1)S(1)} %pad_maximum_fusion.1), channel_id=1, source_target_pairs={{0,2},{1,7},{2,0},{3,5},{4,6},{5,3},{6,4},{7,1},{8,10},{9,15},{10,... | collective-permute-start | bytes 786440 | tf_op jit(solution)/shard_map/ppermute | solution.py:37
  44.1 6.3 %collective-permute-done = bf16[4,2,4,2,16,128]{5,4,3,2,1,0:T(8,128)(2,1)S(1)} collective-permute-done((bf16[4,2,4,2,16,128]{5,4,3,2,1,0:T(8,128)(2,1)S(1)}, bf16[4,2,4,2,16,128]{5,4,3,2,1,0:T(8,128)(2,1)S(1)}, u32[]{:S(2)}, u32[]{:S(2)}) %collective-permute-start) | collective-permute-done | bytes 262176 | tf_op jit(solution)/shard_map/ppermute | solution.py:37
  50.4 2.9 %all-to-all-done = bf16[4,16,3584]{2,1,0:T(8,128)(2,1)} async-done(((bf16[4,16,3584]{2,1,0:T(8,128)(2,1)}), bf16[4,16,3584]{2,1,0:T(8,128)(2,1)}, u32[]{:S(2)}, u32[]{:S(2)}) %all-to-all-start) | async-done | bytes 458784 | tf_op jit(solution)/shard_map/all_to_all | solution.py:50
  53.4 4.0 %collective-permute-start.2 = (bf16[64,3584]{1,0:T(8,128)(2,1)}, bf16[64,3584]{1,0:T(8,128)(2,1)}, u32[]{:S(2)}, u32[]{:S(2)}) collective-permute-start(bf16[64,3584]{1,0:T(8,128)(2,1)} %bitcast.28.own), channel_id=1, source_target_pairs={{0,1},{1,0},{2,3},{3,2},{4,5},{5,4},{6,7},{7,6},{8,9},{9,8},{10,11... | collective-permute-start | bytes 1376264 | tf_op jit(solution)/shard_map/ppermute | solution.py:37
  57.4 2.2 %collective-permute-start.3 = (bf16[64,3584]{1,0:T(8,128)(2,1)}, bf16[64,3584]{1,0:T(8,128)(2,1)}, u32[]{:S(2)}, u32[]{:S(2)}) collective-permute-start(bf16[64,3584]{1,0:T(8,128)(2,1)} %bitcast.28.own), channel_id=1, source_target_pairs={{0,6},{1,3},{2,4},{3,1},{4,2},{5,7},{6,0},{7,5},{8,14},{9,11},{10,... | collective-permute-start | bytes 1376264 | tf_op jit(solution)/shard_map/ppermute | solution.py:37
  59.6 4.5 %collective-permute-start.4 = (bf16[64,3584]{1,0:T(8,128)(2,1)}, bf16[64,3584]{1,0:T(8,128)(2,1)}, u32[]{:S(2)}, u32[]{:S(2)}) collective-permute-start(bf16[64,3584]{1,0:T(8,128)(2,1)} %bitcast.28.own), channel_id=1, source_target_pairs={{0,3},{1,6},{2,1},{3,4},{4,7},{5,2},{6,5},{7,0},{8,11},{9,14},{10,... | collective-permute-start | bytes 1376264 | tf_op jit(solution)/shard_map/ppermute | solution.py:37
  64.1 1.2 convolution_convert_fusion
  65.2 5.2 %all-to-all-start.2 = ((bf16[4,16,3584]{2,1,0:T(8,128)(2,1)}), bf16[4,16,3584]{2,1,0:T(8,128)(2,1)}, u32[]{:S(2)}, u32[]{:S(2)}) async-start(bf16[4,16,3584]{2,1,0:T(8,128)(2,1)} %bitcast.38), calls=%async_computation.2 | async-start | bytes 917504 | tf_op jit(solution)/shard_map/all_to_all | solution.py:50
  70.5 1.2 pad_maximum_fusion.near_all
  72.1 1.2 copy-done.4
  73.3 5.9 %expert_work.2 = (bf16[64,3712]{1,0:T(8,128)(2,1)S(1)}, bf16[64,3712]{1,0:T(8,128)(2,1)}, bf16[64,3712]{1,0:T(8,128)(2,1)}, bf16[64,3712]{1,0:T(8,128)(2,1)}) custom-call(s32[3]{0:T(128)S(1)} %pad_add_fusion.pos, bf16[4,32,16,128]{3,2,1,0:T(8,128)(2,1)S(1)} %pad_maximum_fusion.near_all, bf16[4,16,16,128]{3,2,1,0:T(8,128)(2,1)S(1)} %bitcast.75, ...), custom_call_target="tpu_custom_call" | custom-call | tf_op jit(solution)/shard_map/expert_work/pallas_call | solution.py:158
  79.2 0.8 copy-done.6
  80.0 3.0 %collective-permute-start.10 = (bf16[64,3712]{1,0:T(8,128)(2,1)}, bf16[64,3712]{1,0:T(8,128)(2,1)}, u32[]{:S(2)}, u32[]{:S(2)}) collective-permute-start(bf16[64,3712]{1,0:T(8,128)(2,1)} %get-tuple-element.23), channel_id=1, source_target_pairs={{0,7},{1,2},{2,5},{3,0},{4,3},{5,6},{6,1},{7,4},{8,15},{9,10},{10,... | collective-permute-start | bytes 1425416 | tf_op jit(solution)/shard_map/ppermute | solution.py:37
  83.0 2.9 %collective-permute-start.8 = (bf16[64,3712]{1,0:T(8,128)(2,1)}, bf16[64,3712]{1,0:T(8,128)(2,1)}, u32[]{:S(2)}, u32[]{:S(2)}) collective-permute-start(bf16[64,3712]{1,0:T(8,128)(2,1)} %get-tuple-element.21), channel_id=1, source_target_pairs={{0,1},{1,0},{2,3},{3,2},{4,5},{5,4},{6,7},{7,6},{8,9},{9,8},{10,11... | collective-permute-start | bytes 1425416 | tf_op jit(solution)/shard_map/ppermute | solution.py:37
  85.9 3.3 %collective-permute-start.9 = (bf16[64,3712]{1,0:T(8,128)(2,1)}, bf16[64,3712]{1,0:T(8,128)(2,1)}, u32[]{:S(2)}, u32[]{:S(2)}) collective-permute-start(bf16[64,3712]{1,0:T(8,128)(2,1)} %get-tuple-element.22), channel_id=1, source_target_pairs={{0,6},{1,3},{2,4},{3,1},{4,2},{5,7},{6,0},{7,5},{8,14},{9,11},{10,... | collective-permute-start | bytes 1425416 | tf_op jit(solution)/shard_map/ppermute | solution.py:37
  89.2 2.5 %collective-permute-start.12 = (bf16[64,3584]{1,0:T(8,128)(2,1)}, bf16[64,3584]{1,0:T(8,128)(2,1)}, u32[]{:S(2)}, u32[]{:S(2)}) collective-permute-start(bf16[64,3584]{1,0:T(8,128)(2,1)} %bitcast.39.own), channel_id=1, source_target_pairs={{0,1},{1,0},{2,3},{3,2},{4,5},{5,4},{6,7},{7,6},{8,9},{9,8},{10,11... | collective-permute-start | bytes 1376264 | tf_op jit(solution)/shard_map/ppermute | solution.py:37
  91.7 3.1 %collective-permute-start.13 = (bf16[64,3584]{1,0:T(8,128)(2,1)}, bf16[64,3584]{1,0:T(8,128)(2,1)}, u32[]{:S(2)}, u32[]{:S(2)}) collective-permute-start(bf16[64,3584]{1,0:T(8,128)(2,1)} %bitcast.39.own), channel_id=1, source_target_pairs={{0,6},{1,3},{2,4},{3,1},{4,2},{5,7},{6,0},{7,5},{8,14},{9,11},{10,... | collective-permute-start | bytes 1376264 | tf_op jit(solution)/shard_map/ppermute | solution.py:37
  94.9 3.5 %collective-permute-start.14 = (bf16[64,3584]{1,0:T(8,128)(2,1)}, bf16[64,3584]{1,0:T(8,128)(2,1)}, u32[]{:S(2)}, u32[]{:S(2)}) collective-permute-start(bf16[64,3584]{1,0:T(8,128)(2,1)} %bitcast.39.own), channel_id=1, source_target_pairs={{0,3},{1,6},{2,1},{3,4},{4,7},{5,2},{6,5},{7,0},{8,11},{9,14},{10,... | collective-permute-start | bytes 1376264 | tf_op jit(solution)/shard_map/ppermute | solution.py:37
  98.4 2.5 %add_convert_fusion = bf16[64,3712]{1,0:T(8,128)(2,1)} fusion(bf16[64,3712]{1,0:T(8,128)(2,1)} %collective-permute-done.10, bf16[64,3712]{1,0:T(8,128)(2,1)} %collective-permute-done.9, bf16[64,3712]{1,0:T(8,128)(2,1)} %collective-permute-done.8, bf16[64,3712]{1,0:T(8,128)(2,1)} %copy-done.6), kind=kLoop, calls=%fused_computation.6 | loop fusion | flops 1900544 | bytes 2375680 | tf_op jit(solution)/shard_map/convert_element_type | solution.py:241
  100.9 5.6 %all-to-all-start.1 = ((bf16[4,16,3712]{2,1,0:T(8,128)(2,1)}), bf16[4,16,3712]{2,1,0:T(8,128)(2,1)}, u32[]{:S(2)}, u32[]{:S(2)}) async-start(bf16[4,16,3712]{2,1,0:T(8,128)(2,1)} %bitcast.81), calls=%async_computation.1 | async-start | bytes 950272 | tf_op jit(solution)/shard_map/all_to_all | solution.py:50
  106.9 1.2 copy-done.5
  108.1 5.9 %expert_work.3 = (bf16[64,3712]{1,0:T(8,128)(2,1)S(1)}, bf16[64,3712]{1,0:T(8,128)(2,1)}, bf16[64,3712]{1,0:T(8,128)(2,1)}, bf16[64,3712]{1,0:T(8,128)(2,1)}) custom-call(s32[3]{0:T(128)S(1)} %pad_add_fusion.pos, bf16[4,32,16,128]{3,2,1,0:T(8,128)(2,1)S(1)} %pad_maximum_fusion.near_all, bf16[4,16,16,128]{3,2,1,0:T(8,128)(2,1)S(1)} %bitcast.76, ...), custom_call_target="tpu_custom_call" | custom-call | tf_op jit(solution)/shard_map/expert_work/pallas_call | solution.py:158
  114.0 0.7 copy-done.7
  114.7 3.6 %collective-permute-start.15 = (bf16[64,3712]{1,0:T(8,128)(2,1)}, bf16[64,3712]{1,0:T(8,128)(2,1)S(1)}, u32[]{:S(2)}, u32[]{:S(2)}) collective-permute-start(bf16[64,3712]{1,0:T(8,128)(2,1)} %get-tuple-element.26), channel_id=1, source_target_pairs={{0,1},{1,0},{2,3},{3,2},{4,5},{5,4},{6,7},{7,6},{8,9},{9,8},{10,11... | collective-permute-start | bytes 1425416 | tf_op jit(solution)/shard_map/ppermute | solution.py:37
  118.3 1.9 %collective-permute-start.16 = (bf16[64,3712]{1,0:T(8,128)(2,1)}, bf16[64,3712]{1,0:T(8,128)(2,1)S(1)}, u32[]{:S(2)}, u32[]{:S(2)}) collective-permute-start(bf16[64,3712]{1,0:T(8,128)(2,1)} %get-tuple-element.27), channel_id=1, source_target_pairs={{0,6},{1,3},{2,4},{3,1},{4,2},{5,7},{6,0},{7,5},{8,14},{9,11},{10,... | collective-permute-start | bytes 1425416 | tf_op jit(solution)/shard_map/ppermute | solution.py:37
  120.3 3.0 %collective-permute-start.17 = (bf16[64,3712]{1,0:T(8,128)(2,1)}, bf16[64,3712]{1,0:T(8,128)(2,1)S(1)}, u32[]{:S(2)}, u32[]{:S(2)}) collective-permute-start(bf16[64,3712]{1,0:T(8,128)(2,1)} %get-tuple-element.28), channel_id=1, source_target_pairs={{0,7},{1,2},{2,5},{3,0},{4,3},{5,6},{6,1},{7,4},{8,15},{9,10},{10,... | collective-permute-start | bytes 1425416 | tf_op jit(solution)/shard_map/ppermute | solution.py:37
  123.4 0.7 copy-done.13
  124.3 4.0 %collective-permute-done.16 = bf16[64,3712]{1,0:T(8,128)(2,1)S(1)} collective-permute-done((bf16[64,3712]{1,0:T(8,128)(2,1)}, bf16[64,3712]{1,0:T(8,128)(2,1)S(1)}, u32[]{:S(2)}, u32[]{:S(2)}) %collective-permute-start.16) | collective-permute-done | bytes 475168 | tf_op jit(solution)/shard_map/ppermute | solution.py:37
  128.2 6.5 %collective-permute-done.17 = bf16[64,3712]{1,0:T(8,128)(2,1)S(1)} collective-permute-done((bf16[64,3712]{1,0:T(8,128)(2,1)}, bf16[64,3712]{1,0:T(8,128)(2,1)S(1)}, u32[]{:S(2)}, u32[]{:S(2)}) %collective-permute-start.17) | collective-permute-done | bytes 475168 | tf_op jit(solution)/shard_map/ppermute | solution.py:37
  134.7 1.0 copy-done.8
  135.7 0.8 total_blocks.1
  136.5 4.0 %collective-permute-start.18 = (bf16[16,3712]{1,0:T(8,128)(2,1)S(1)}, bf16[16,3712]{1,0:T(8,128)(2,1)S(1)}, u32[]{:S(2)}, u32[]{:S(2)}) collective-permute-start(bf16[16,3712]{1,0:T(8,128)(2,1)S(1)} %get-tuple-element.30), channel_id=1, source_target_pairs={{0,8},{1,9},{2,10},{3,11},{4,12},{5,13},{6,14},{7,15},{8,16},{9,17... | collective-permute-start | bytes 356360 | tf_op jit(solution)/shard_map/ppermute | solution.py:56
  140.6 5.5 %collective-permute-start.19 = (bf16[16,3712]{1,0:T(8,128)(2,1)S(1)}, bf16[16,3712]{1,0:T(8,128)(2,1)S(1)}, u32[]{:S(2)}, u32[]{:S(2)}) collective-permute-start(bf16[16,3712]{1,0:T(8,128)(2,1)S(1)} %get-tuple-element.31), channel_id=1, source_target_pairs={{0,16},{1,17},{2,18},{3,19},{4,20},{5,21},{6,22},{7,23},{8,24},{9,... | collective-permute-start | bytes 356360 | tf_op jit(solution)/shard_map/ppermute | solution.py:56
  146.1 4.1 %collective-permute-start.20 = (bf16[16,3712]{1,0:T(8,128)(2,1)S(1)}, bf16[16,3712]{1,0:T(8,128)(2,1)S(1)}, u32[]{:S(2)}, u32[]{:S(2)}) collective-permute-start(bf16[16,3712]{1,0:T(8,128)(2,1)S(1)} %get-tuple-element.32), channel_id=1, source_target_pairs={{0,24},{1,25},{2,26},{3,27},{4,28},{5,29},{6,30},{7,31},{8,0},{9,1... | collective-permute-start | bytes 356360 | tf_op jit(solution)/shard_map/ppermute | solution.py:56
  150.3 4.1 %collective-permute-done.19.refs_2_ = bf16[16,3712]{1,0:T(8,128)(2,1)S(1)} collective-permute-done((bf16[16,3712]{1,0:T(8,128)(2,1)S(1)}, bf16[16,3712]{1,0:T(8,128)(2,1)S(1)}, u32[]{:S(2)}, u32[]{:S(2)}) %collective-permute-start.19) | collective-permute-done | bytes 118816 | tf_op jit(solution)/shard_map/ppermute | solution.py:56
  154.3 6.1 %collective-permute-done.20.refs_3_ = bf16[16,3712]{1,0:T(8,128)(2,1)S(1)} collective-permute-done((bf16[16,3712]{1,0:T(8,128)(2,1)S(1)}, bf16[16,3712]{1,0:T(8,128)(2,1)S(1)}, u32[]{:S(2)}, u32[]{:S(2)}) %collective-permute-start.20) | collective-permute-done | bytes 118816 | tf_op jit(solution)/shard_map/ppermute | solution.py:56
  160.4 1.1 unpack.3
  161.5 2.1 %unpack.2 = (bf16[64,3584]{1,0:T(8,128)(2,1)}, f32[1,64]{1,0:T(1,128)}) custom-call(bf16[64,64]{1,0:T(8,128)(2,1)S(1)} %fusion.6.chosen, f32[64,1]{1,0:T(8,128)S(1)} %copy.17.probs, bf16[64,3712]{1,0:T(8,128)(2,1)} %bitcast.33.refs_0_), custom_call_target="tpu_custom_call" | custom-call | tf_op jit(solution)/shard_map/unpack/pallas_call | solution.py:210
  (59 shorter events, 1.8 us)
Async XLA Ops:
  0.6 20.8 %copy-start.11 = (bf16[1,512,128]{2,1,0:T(8,128)(2,1)S(1)}, bf16[1,512,128]{2,1,0:T(8,128)(2,1)}, u32[]{:S(2)}) copy-start(bf16[1,512,128]{2,1,0:T(8,128)(2,1)} %param.15) | copy-start | bytes 393220
  0.6 56.7 %collective-permute-start.11 = (bf16[1,64,3584]{2,1,0:T(8,128)(2,1)}, bf16[1,64,3584]{2,1,0:T(8,128)(2,1)S(1)}, u32[]{:S(2)}, u32[]{:S(2)}) collective-permute-start(bf16[1,64,3584]{2,1,0:T(8,128)(2,1)} %param.18), channel_id=1, source_target_pairs={{0,32},{32,64},{64,96},{96,128},{128,160},{160,192},{192,224},{224... | collective-permute-start | bytes 1376264 | tf_op jit(solution)/shard_map/ppermute | solution.py:78
  5.6 54.0 %collective-permute-start.5 = (bf16[128,3584]{1,0:T(8,128)(2,1)}, bf16[128,3584]{1,0:T(8,128)(2,1)S(1)}, u32[]{:S(2)}, u32[]{:S(2)}) collective-permute-start(bf16[128,3584]{1,0:T(8,128)(2,1)} %bitcast.66), channel_id=1, source_target_pairs={{0,2},{1,7},{2,0},{3,5},{4,6},{5,3},{6,4},{7,1},{8,10},{9,15},{10,... | collective-permute-start | bytes 2752520 | tf_op jit(solution)/shard_map/ppermute | solution.py:37
  10.0 61.7 %collective-permute-start.6 = (bf16[3584,128]{1,0:T(8,128)(2,1)}, bf16[3584,128]{1,0:T(8,128)(2,1)}, u32[]{:S(2)}, u32[]{:S(2)}) collective-permute-start(bf16[3584,128]{1,0:T(8,128)(2,1)} %bitcast.69), channel_id=1, source_target_pairs={{0,2},{1,7},{2,0},{3,5},{4,6},{5,3},{6,4},{7,1},{8,10},{9,15},{10,... | collective-permute-start | bytes 2752520 | tf_op jit(solution)/shard_map/ppermute | solution.py:37
  12.1 59.6 %collective-permute-start.7 = (bf16[3584,128]{1,0:T(8,128)(2,1)}, bf16[3584,128]{1,0:T(8,128)(2,1)}, u32[]{:S(2)}, u32[]{:S(2)}) collective-permute-start(bf16[3584,128]{1,0:T(8,128)(2,1)} %bitcast.72), channel_id=1, source_target_pairs={{0,2},{1,7},{2,0},{3,5},{4,6},{5,3},{6,4},{7,1},{8,10},{9,15},{10,... | collective-permute-start | bytes 2752520 | tf_op jit(solution)/shard_map/ppermute | solution.py:37
  16.5 13.5 %collective-permute-start.1 = (bf16[1,64,3584]{2,1,0:T(8,128)(2,1)}, bf16[1,64,3584]{2,1,0:T(8,128)(2,1)S(1)}, u32[]{:S(2)}, u32[]{:S(2)}) collective-permute-start(bf16[1,64,3584]{2,1,0:T(8,128)(2,1)} %param.17), channel_id=1, source_target_pairs={{0,480},{32,0},{64,32},{96,64},{128,96},{160,128},{192,160},{224,1... | collective-permute-start | bytes 1376264 | tf_op jit(solution)/shard_map/ppermute | solution.py:78
  21.5 0.9 copy-start.15
  21.5 1.1 copy-start.10
  22.3 0.9 copy-start.9
  31.1 22.2 %all-to-all-start = ((bf16[4,16,3584]{2,1,0:T(8,128)(2,1)}), bf16[4,16,3584]{2,1,0:T(8,128)(2,1)}, u32[]{:S(2)}, u32[]{:S(2)}) async-start(bf16[4,16,3584]{2,1,0:T(8,128)(2,1)} %bitcast.27), calls=%async_computation | async-start | bytes 917504 | tf_op jit(solution)/shard_map/all_to_all | solution.py:50
  41.9 2.0 %copy-start.14 = (s32[1,64,1]{1,2,0:T(1,128)S(1)}, s32[1,64,1]{1,2,0:T(1,128)}, u32[]{:S(2)}) copy-start(s32[1,64,1]{1,2,0:T(1,128)} %param.20) | copy-start | bytes 772
  41.9 8.6 %collective-permute-start = (bf16[4,2,4,2,16,128]{5,4,3,2,1,0:T(8,128)(2,1)S(1)}, bf16[4,2,4,2,16,128]{5,4,3,2,1,0:T(8,128)(2,1)S(1)}, u32[]{:S(2)}, u32[]{:S(2)}) collective-permute-start(bf16[4,2,4,2,16,128]{5,4,3,2,1,0:T(8,128)(2,1)S(1)} %pad_maximum_fusion.1), channel_id=1, source_target_pairs={{0,2},{1,7},{2,0},{3,5},{4,6},{5,3},{6,4},{7,1},{8,10},{9,15},{10,... | collective-permute-start | bytes 786440 | tf_op jit(solution)/shard_map/ppermute | solution.py:37
  53.4 18.3 %collective-permute-start.2 = (bf16[64,3584]{1,0:T(8,128)(2,1)}, bf16[64,3584]{1,0:T(8,128)(2,1)}, u32[]{:S(2)}, u32[]{:S(2)}) collective-permute-start(bf16[64,3584]{1,0:T(8,128)(2,1)} %bitcast.28.own), channel_id=1, source_target_pairs={{0,1},{1,0},{2,3},{3,2},{4,5},{5,4},{6,7},{7,6},{8,9},{9,8},{10,11... | collective-permute-start | bytes 1376264 | tf_op jit(solution)/shard_map/ppermute | solution.py:37
  57.4 14.4 %collective-permute-start.3 = (bf16[64,3584]{1,0:T(8,128)(2,1)}, bf16[64,3584]{1,0:T(8,128)(2,1)}, u32[]{:S(2)}, u32[]{:S(2)}) collective-permute-start(bf16[64,3584]{1,0:T(8,128)(2,1)} %bitcast.28.own), channel_id=1, source_target_pairs={{0,6},{1,3},{2,4},{3,1},{4,2},{5,7},{6,0},{7,5},{8,14},{9,11},{10,... | collective-permute-start | bytes 1376264 | tf_op jit(solution)/shard_map/ppermute | solution.py:37
  59.6 5.6 %copy-start.3 = (bf16[128,3584]{1,0:T(8,128)(2,1)}, bf16[128,3584]{1,0:T(8,128)(2,1)S(1)}, u32[]{:S(2)}) copy-start(bf16[128,3584]{1,0:T(8,128)(2,1)S(1)} %collective-permute-done.5.wd_mate) | copy-start | bytes 2752516
  59.6 12.5 %collective-permute-start.4 = (bf16[64,3584]{1,0:T(8,128)(2,1)}, bf16[64,3584]{1,0:T(8,128)(2,1)}, u32[]{:S(2)}, u32[]{:S(2)}) collective-permute-start(bf16[64,3584]{1,0:T(8,128)(2,1)} %bitcast.28.own), channel_id=1, source_target_pairs={{0,3},{1,6},{2,1},{3,4},{4,7},{5,2},{6,5},{7,0},{8,11},{9,14},{10,... | collective-permute-start | bytes 1376264 | tf_op jit(solution)/shard_map/ppermute | solution.py:37
  64.1 8.0 %copy-start.2 = (bf16[1,3584,128]{2,1,0:T(8,128)(2,1)S(1)}, bf16[1,3584,128]{2,1,0:T(8,128)(2,1)}, u32[]{:S(2)}) copy-start(bf16[1,3584,128]{2,1,0:T(8,128)(2,1)} %param.24) | copy-start | bytes 2752516
  65.2 6.9 %copy-start = (bf16[1,128,3584]{2,1,0:T(8,128)(2,1)S(1)}, bf16[1,128,3584]{2,1,0:T(8,128)(2,1)}, u32[]{:S(2)}) copy-start(bf16[1,128,3584]{2,1,0:T(8,128)(2,1)} %param.25) | copy-start | bytes 2752516
  65.2 6.9 %copy-start.1 = (bf16[1,3584,128]{2,1,0:T(8,128)(2,1)S(1)}, bf16[1,3584,128]{2,1,0:T(8,128)(2,1)}, u32[]{:S(2)}) copy-start(bf16[1,3584,128]{2,1,0:T(8,128)(2,1)} %param.23) | copy-start | bytes 2752516
  65.2 23.9 %all-to-all-start.2 = ((bf16[4,16,3584]{2,1,0:T(8,128)(2,1)}), bf16[4,16,3584]{2,1,0:T(8,128)(2,1)}, u32[]{:S(2)}, u32[]{:S(2)}) async-start(bf16[4,16,3584]{2,1,0:T(8,128)(2,1)} %bitcast.38), calls=%async_computation.2 | async-start | bytes 917504 | tf_op jit(solution)/shard_map/all_to_all | solution.py:50
  72.1 1.2 copy-start.4
  79.2 0.8 copy-start.6
  80.0 14.9 %collective-permute-start.10 = (bf16[64,3712]{1,0:T(8,128)(2,1)}, bf16[64,3712]{1,0:T(8,128)(2,1)}, u32[]{:S(2)}, u32[]{:S(2)}) collective-permute-start(bf16[64,3712]{1,0:T(8,128)(2,1)} %get-tuple-element.23), channel_id=1, source_target_pairs={{0,7},{1,2},{2,5},{3,0},{4,3},{5,6},{6,1},{7,4},{8,15},{9,10},{10,... | collective-permute-start | bytes 1425416 | tf_op jit(solution)/shard_map/ppermute | solution.py:37
  83.0 15.5 %collective-permute-start.8 = (bf16[64,3712]{1,0:T(8,128)(2,1)}, bf16[64,3712]{1,0:T(8,128)(2,1)}, u32[]{:S(2)}, u32[]{:S(2)}) collective-permute-start(bf16[64,3712]{1,0:T(8,128)(2,1)} %get-tuple-element.21), channel_id=1, source_target_pairs={{0,1},{1,0},{2,3},{3,2},{4,5},{5,4},{6,7},{7,6},{8,9},{9,8},{10,11... | collective-permute-start | bytes 1425416 | tf_op jit(solution)/shard_map/ppermute | solution.py:37
  85.9 12.5 %collective-permute-start.9 = (bf16[64,3712]{1,0:T(8,128)(2,1)}, bf16[64,3712]{1,0:T(8,128)(2,1)}, u32[]{:S(2)}, u32[]{:S(2)}) collective-permute-start(bf16[64,3712]{1,0:T(8,128)(2,1)} %get-tuple-element.22), channel_id=1, source_target_pairs={{0,6},{1,3},{2,4},{3,1},{4,2},{5,7},{6,0},{7,5},{8,14},{9,11},{10,... | collective-permute-start | bytes 1425416 | tf_op jit(solution)/shard_map/ppermute | solution.py:37
  89.2 17.3 %collective-permute-start.12 = (bf16[64,3584]{1,0:T(8,128)(2,1)}, bf16[64,3584]{1,0:T(8,128)(2,1)}, u32[]{:S(2)}, u32[]{:S(2)}) collective-permute-start(bf16[64,3584]{1,0:T(8,128)(2,1)} %bitcast.39.own), channel_id=1, source_target_pairs={{0,1},{1,0},{2,3},{3,2},{4,5},{5,4},{6,7},{7,6},{8,9},{9,8},{10,11... | collective-permute-start | bytes 1376264 | tf_op jit(solution)/shard_map/ppermute | solution.py:37
  91.7 14.8 %collective-permute-start.13 = (bf16[64,3584]{1,0:T(8,128)(2,1)}, bf16[64,3584]{1,0:T(8,128)(2,1)}, u32[]{:S(2)}, u32[]{:S(2)}) collective-permute-start(bf16[64,3584]{1,0:T(8,128)(2,1)} %bitcast.39.own), channel_id=1, source_target_pairs={{0,6},{1,3},{2,4},{3,1},{4,2},{5,7},{6,0},{7,5},{8,14},{9,11},{10,... | collective-permute-start | bytes 1376264 | tf_op jit(solution)/shard_map/ppermute | solution.py:37
  94.9 12.0 %collective-permute-start.14 = (bf16[64,3584]{1,0:T(8,128)(2,1)}, bf16[64,3584]{1,0:T(8,128)(2,1)}, u32[]{:S(2)}, u32[]{:S(2)}) collective-permute-start(bf16[64,3584]{1,0:T(8,128)(2,1)} %bitcast.39.own), channel_id=1, source_target_pairs={{0,3},{1,6},{2,1},{3,4},{4,7},{5,2},{6,5},{7,0},{8,11},{9,14},{10,... | collective-permute-start | bytes 1376264 | tf_op jit(solution)/shard_map/ppermute | solution.py:37
  100.9 60.6 %all-to-all-start.1 = ((bf16[4,16,3712]{2,1,0:T(8,128)(2,1)}), bf16[4,16,3712]{2,1,0:T(8,128)(2,1)}, u32[]{:S(2)}, u32[]{:S(2)}) async-start(bf16[4,16,3712]{2,1,0:T(8,128)(2,1)} %bitcast.81), calls=%async_computation.1 | async-start | bytes 950272 | tf_op jit(solution)/shard_map/all_to_all | solution.py:50
  106.9 1.2 copy-start.5
  114.0 0.8 copy-start.7
  114.7 9.5 %collective-permute-start.15 = (bf16[64,3712]{1,0:T(8,128)(2,1)}, bf16[64,3712]{1,0:T(8,128)(2,1)S(1)}, u32[]{:S(2)}, u32[]{:S(2)}) collective-permute-start(bf16[64,3712]{1,0:T(8,128)(2,1)} %get-tuple-element.26), channel_id=1, source_target_pairs={{0,1},{1,0},{2,3},{3,2},{4,5},{5,4},{6,7},{7,6},{8,9},{9,8},{10,11... | collective-permute-start | bytes 1425416 | tf_op jit(solution)/shard_map/ppermute | solution.py:37
  118.3 9.9 %collective-permute-start.16 = (bf16[64,3712]{1,0:T(8,128)(2,1)}, bf16[64,3712]{1,0:T(8,128)(2,1)S(1)}, u32[]{:S(2)}, u32[]{:S(2)}) collective-permute-start(bf16[64,3712]{1,0:T(8,128)(2,1)} %get-tuple-element.27), channel_id=1, source_target_pairs={{0,6},{1,3},{2,4},{3,1},{4,2},{5,7},{6,0},{7,5},{8,14},{9,11},{10,... | collective-permute-start | bytes 1425416 | tf_op jit(solution)/shard_map/ppermute | solution.py:37
  120.3 3.1 %copy-start.12 = (f32[1,64,1]{1,2,0:T(1,128)S(1)}, f32[1,64,1]{1,2,0:T(1,128)}, u32[]{:S(2)}) copy-start(f32[1,64,1]{1,2,0:T(1,128)} %param.22) | copy-start | bytes 772
  120.3 14.4 %collective-permute-start.17 = (bf16[64,3712]{1,0:T(8,128)(2,1)}, bf16[64,3712]{1,0:T(8,128)(2,1)S(1)}, u32[]{:S(2)}, u32[]{:S(2)}) collective-permute-start(bf16[64,3712]{1,0:T(8,128)(2,1)} %get-tuple-element.28), channel_id=1, source_target_pairs={{0,7},{1,2},{2,5},{3,0},{4,3},{5,6},{6,1},{7,4},{8,15},{9,10},{10,... | collective-permute-start | bytes 1425416 | tf_op jit(solution)/shard_map/ppermute | solution.py:37
  123.4 0.7 copy-start.13
  134.7 1.0 copy-start.8
  136.5 13.7 %collective-permute-start.18 = (bf16[16,3712]{1,0:T(8,128)(2,1)S(1)}, bf16[16,3712]{1,0:T(8,128)(2,1)S(1)}, u32[]{:S(2)}, u32[]{:S(2)}) collective-permute-start(bf16[16,3712]{1,0:T(8,128)(2,1)S(1)} %get-tuple-element.30), channel_id=1, source_target_pairs={{0,8},{1,9},{2,10},{3,11},{4,12},{5,13},{6,14},{7,15},{8,16},{9,17... | collective-permute-start | bytes 356360 | tf_op jit(solution)/shard_map/ppermute | solution.py:56
  140.6 13.8 %collective-permute-start.19 = (bf16[16,3712]{1,0:T(8,128)(2,1)S(1)}, bf16[16,3712]{1,0:T(8,128)(2,1)S(1)}, u32[]{:S(2)}, u32[]{:S(2)}) collective-permute-start(bf16[16,3712]{1,0:T(8,128)(2,1)S(1)} %get-tuple-element.31), channel_id=1, source_target_pairs={{0,16},{1,17},{2,18},{3,19},{4,20},{5,21},{6,22},{7,23},{8,24},{9,... | collective-permute-start | bytes 356360 | tf_op jit(solution)/shard_map/ppermute | solution.py:56
  146.1 14.3 %collective-permute-start.20 = (bf16[16,3712]{1,0:T(8,128)(2,1)S(1)}, bf16[16,3712]{1,0:T(8,128)(2,1)S(1)}, u32[]{:S(2)}, u32[]{:S(2)}) collective-permute-start(bf16[16,3712]{1,0:T(8,128)(2,1)S(1)} %get-tuple-element.32), channel_id=1, source_target_pairs={{0,24},{1,25},{2,26},{3,27},{4,28},{5,29},{6,30},{7,31},{8,0},{9,1... | collective-permute-start | bytes 356360 | tf_op jit(solution)/shard_map/ppermute | solution.py:56

commit v4 on v3

--- a/solution.py
+++ b/solution.py
@@ -97,9 +97,9 @@
 
 
 def expert_kernel(
-    pos, near_all, far_all, own, sib, same, cross,
-    wd_own, wd_mate, wg_own, wg_mate, wu_own, wu_mate,
-    p_own, p_sib, p_same, p_cross, near, far, arrived, *, which,
+    pos, near_all, far_all, wg_away, wu_away, own, sib, same, cross,
+    wd_own, wd_mate, wg_own, wu_own,
+    p_own, p_sib, p_same, p_cross, near, far, wg_mate, wu_mate, arrived, *, which,
 ):
     x, c, tp = pos[0], pos[1], pos[2]
     n, wide = own.shape
@@ -107,7 +107,11 @@
         pltpu.make_async_copy(ref.at[pl.ds(2 * which, 2)], buf, arrived.at[k])
         for k, (ref, buf) in enumerate(((near_all, near), (far_all, far)))
     ]
-    for load in loads:
+    later = [
+        pltpu.make_async_copy(wg_away, wg_mate, arrived.at[2]),
+        pltpu.make_async_copy(wu_away, wu_mate, arrived.at[3]),
+    ]
+    for load in loads + later:
         load.start()
     dh = None
     for d in range(0, wide, TILE):
@@ -139,6 +143,8 @@
     dg = (dh * up * slope).astype(jnp.bfloat16)
     du = (dh * act).astype(jnp.bfloat16)
     both = jnp.concatenate([dg, du], axis=-1)
+    for load in later:
+        load.wait()
     outs = (p_own, p_sib, p_same, p_cross)
     for d in range(0, wide, TILE):
         cut = slice(d, d + TILE)
@@ -153,23 +159,26 @@
 
 def expert_work(pos, pieces, near, far, weights, which):
     count, wide = pieces[0].shape
+    wd, wd_mate, wg, wg_mate, wu, wu_mate = weights
     shape = jax.ShapeDtypeStruct((count, wide + PAD), jnp.bfloat16)
     vmem = pl.BlockSpec(memory_space=pltpu.VMEM)
     return pl.pallas_call(
         functools.partial(expert_kernel, which=which),
         in_specs=[pl.BlockSpec(memory_space=pltpu.SMEM)]
-        + [pl.BlockSpec(memory_space=pl.ANY)] * 2
-        + [vmem] * 10,
+        + [pl.BlockSpec(memory_space=pl.ANY)] * 4
+        + [vmem] * 8,
         out_specs=[vmem] * 4,
         out_shape=[shape] * 4,
         scratch_shapes=[
             pltpu.VMEM((2,) + near.shape[1:], near.dtype),
             pltpu.VMEM((2,) + far.shape[1:], far.dtype),
-            pltpu.SemaphoreType.DMA((2,)),
+            pltpu.VMEM(wg_mate.shape, wg_mate.dtype),
+            pltpu.VMEM(wu_mate.shape, wu_mate.dtype),
+            pltpu.SemaphoreType.DMA((4,)),
         ],
         compiler_params=pltpu.CompilerParams(vmem_limit_bytes=20 << 20),
         name="expert_work",
-    )(pos, near, far, *pieces, *weights)
+    )(pos, near, far, wg_mate, wu_mate, *pieces, wd, wd_mate, wg, wu)
 
 
 def total_kernel(pos, own, sib, same, cross, *outs):

time: 165 us -> 167 us (1.012)
  Pallas kernels: 15.7 us -> 17.5 us
    pallas_call x2, Pallas kernels: 11.8 us -> 13.6 us  [expert_work(): pl.pallas_call(functools.partial(expert_kernel, which=which), in_specs=[p...]
  transfers between devices with their start and end apart: 24 -> 24, of which waited for: 9 -> 9; matrix products, arithmetic and copies ran while one was open for 5% -> 5% of each run, Pallas kernels for 8% -> 9%
where the time goes in v4:
time: 167 us; the launch traced here: 165 us
  starting transfers between devices  95.2 us (57%)
  waiting for transfers between devices  37.3 us (22%)
  Pallas kernels  17.5 us (10%)
  local copies, waits for them, and re-layouts  7.3 us (4%)
  other arithmetic  3.98 us (2%)
  matrix products  2.75 us (2%)
    ppermute x16, starting transfers between devices, moved(): return lax.ppermute(value, 'expert', pairs)  50.4 us
    all_to_all x3, starting transfers between devices, over_z(): lax.all_to_all(value, 'expert', split_axis=0, concat_axis=0, axis_index_g...  21.4 us
    ppermute x16, waiting for transfers between devices, moved(): return lax.ppermute(value, 'expert', pairs)  17.5 us
    ppermute x3, starting transfers between devices, along_z(): lax.ppermute(value, 'expert', [(place(z, x, c), place((z + dz) % EXPERTS,...  13.6 us
    pallas_call x2, Pallas kernels, expert_work(): pl.pallas_call(functools.partial(expert_kernel, which=which), in_specs=[p...  13.6 us
    ppermute x3, waiting for transfers between devices, along_z(): lax.ppermute(value, 'expert', [(place(z, x, c), place((z + dz) % EXPERTS,...  10.2 us
    ppermute x2, starting transfers between devices, passed_along(): return lax.ppermute(value, 'section', pairs)  9.77 us
    ppermute x2, waiting for transfers between devices, passed_along(): return lax.ppermute(value, 'section', pairs)  6.72 us
  transfers between devices with their start and end apart: 24, of which 9 were waited for; matrix products, arithmetic and copies ran while one was open for 5% of the time, Pallas kernels for 9%

profile of v4, /device:TPU:1, one launch (start us, length us, event | category | flops | bytes accessed | tf_op | source)
XLA Modules:
  0.0 165.3 jit_solution(17166965818024707600)
XLA Ops:
  0.6 4.9 %collective-permute-start.11 = (bf16[1,64,3584]{2,1,0:T(8,128)(2,1)}, bf16[1,64,3584]{2,1,0:T(8,128)(2,1)S(1)}, u32[]{:S(2)}, u32[]{:S(2)}) collective-permute-start(bf16[1,64,3584]{2,1,0:T(8,128)(2,1)} %param.18), channel_id=1, source_target_pairs={{0,32},{32,64},{64,96},{96,128},{128,160},{160,192},{192,224},{224... | collective-permute-start | bytes 1376264 | tf_op jit(solution)/shard_map/ppermute | solution.py:78
  5.6 4.4 %collective-permute-start.1 = (bf16[3584,128]{1,0:T(8,128)(2,1)}, bf16[3584,128]{1,0:T(8,128)(2,1)S(1)}, u32[]{:S(2)}, u32[]{:S(2)}) collective-permute-start(bf16[3584,128]{1,0:T(8,128)(2,1)} %bitcast.66), channel_id=1, source_target_pairs={{0,2},{1,7},{2,0},{3,5},{4,6},{5,3},{6,4},{7,1},{8,10},{9,15},{10,... | collective-permute-start | bytes 2752520 | tf_op jit(solution)/shard_map/ppermute | solution.py:37
  10.0 2.1 %collective-permute-start.2 = (bf16[3584,128]{1,0:T(8,128)(2,1)}, bf16[3584,128]{1,0:T(8,128)(2,1)}, u32[]{:S(2)}, u32[]{:S(2)}) collective-permute-start(bf16[3584,128]{1,0:T(8,128)(2,1)} %bitcast.69), channel_id=1, source_target_pairs={{0,2},{1,7},{2,0},{3,5},{4,6},{5,3},{6,4},{7,1},{8,10},{9,15},{10,... | collective-permute-start | bytes 2752520 | tf_op jit(solution)/shard_map/ppermute | solution.py:37
  12.1 4.4 %collective-permute-start.7 = (bf16[128,3584]{1,0:T(8,128)(2,1)}, bf16[128,3584]{1,0:T(8,128)(2,1)}, u32[]{:S(2)}, u32[]{:S(2)}) collective-permute-start(bf16[128,3584]{1,0:T(8,128)(2,1)} %bitcast.72), channel_id=1, source_target_pairs={{0,2},{1,7},{2,0},{3,5},{4,6},{5,3},{6,4},{7,1},{8,10},{9,15},{10,... | collective-permute-start | bytes 2752520 | tf_op jit(solution)/shard_map/ppermute | solution.py:37
  16.5 4.8 %collective-permute-start.3 = (bf16[1,64,3584]{2,1,0:T(8,128)(2,1)}, bf16[1,64,3584]{2,1,0:T(8,128)(2,1)S(1)}, u32[]{:S(2)}, u32[]{:S(2)}) collective-permute-start(bf16[1,64,3584]{2,1,0:T(8,128)(2,1)} %param.17), channel_id=1, source_target_pairs={{0,480},{32,0},{64,32},{96,64},{128,96},{160,128},{192,160},{224,1... | collective-permute-start | bytes 1376264 | tf_op jit(solution)/shard_map/ppermute | solution.py:78
  21.5 0.8 dynamic-slice_bitcast_fusion.5
  22.6 0.7 copy-done.9
  23.3 6.7 %collective-permute-done.3 = bf16[1,64,3584]{2,1,0:T(8,128)(2,1)S(1)} collective-permute-done((bf16[1,64,3584]{2,1,0:T(8,128)(2,1)}, bf16[1,64,3584]{2,1,0:T(8,128)(2,1)S(1)}, u32[]{:S(2)}, u32[]{:S(2)}) %collective-permute-start.3) | collective-permute-done | bytes 458784 | tf_op jit(solution)/shard_map/ppermute | solution.py:78
  30.0 1.2 convolution_convert_fusion.1
  31.1 10.6 %all-to-all-start = ((bf16[4,16,3584]{2,1,0:T(8,128)(2,1)}), bf16[4,16,3584]{2,1,0:T(8,128)(2,1)}, u32[]{:S(2)}, u32[]{:S(2)}) async-start(bf16[4,16,3584]{2,1,0:T(8,128)(2,1)} %bitcast.29), calls=%async_computation | async-start | bytes 917504 | tf_op jit(solution)/shard_map/all_to_all | solution.py:50
  41.9 2.0 %collective-permute-start = (bf16[4,2,4,2,16,128]{5,4,3,2,1,0:T(8,128)(2,1)S(1)}, bf16[4,2,4,2,16,128]{5,4,3,2,1,0:T(8,128)(2,1)S(1)}, u32[]{:S(2)}, u32[]{:S(2)}) collective-permute-start(bf16[4,2,4,2,16,128]{5,4,3,2,1,0:T(8,128)(2,1)S(1)} %pad_maximum_fusion.1), channel_id=1, source_target_pairs={{0,2},{1,7},{2,0},{3,5},{4,6},{5,3},{6,4},{7,1},{8,10},{9,15},{10,... | collective-permute-start | bytes 786440 | tf_op jit(solution)/shard_map/ppermute | solution.py:37
  44.1 6.3 %collective-permute-done = bf16[4,2,4,2,16,128]{5,4,3,2,1,0:T(8,128)(2,1)S(1)} collective-permute-done((bf16[4,2,4,2,16,128]{5,4,3,2,1,0:T(8,128)(2,1)S(1)}, bf16[4,2,4,2,16,128]{5,4,3,2,1,0:T(8,128)(2,1)S(1)}, u32[]{:S(2)}, u32[]{:S(2)}) %collective-permute-start) | collective-permute-done | bytes 262176 | tf_op jit(solution)/shard_map/ppermute | solution.py:37
  50.4 2.9 %all-to-all-done = bf16[4,16,3584]{2,1,0:T(8,128)(2,1)} async-done(((bf16[4,16,3584]{2,1,0:T(8,128)(2,1)}), bf16[4,16,3584]{2,1,0:T(8,128)(2,1)}, u32[]{:S(2)}, u32[]{:S(2)}) %all-to-all-start) | async-done | bytes 458784 | tf_op jit(solution)/shard_map/all_to_all | solution.py:50
  53.4 4.0 %collective-permute-start.4 = (bf16[64,3584]{1,0:T(8,128)(2,1)}, bf16[64,3584]{1,0:T(8,128)(2,1)}, u32[]{:S(2)}, u32[]{:S(2)}) collective-permute-start(bf16[64,3584]{1,0:T(8,128)(2,1)} %bitcast.30.own), channel_id=1, source_target_pairs={{0,1},{1,0},{2,3},{3,2},{4,5},{5,4},{6,7},{7,6},{8,9},{9,8},{10,11... | collective-permute-start | bytes 1376264 | tf_op jit(solution)/shard_map/ppermute | solution.py:37
  57.4 2.2 %collective-permute-start.5 = (bf16[64,3584]{1,0:T(8,128)(2,1)}, bf16[64,3584]{1,0:T(8,128)(2,1)}, u32[]{:S(2)}, u32[]{:S(2)}) collective-permute-start(bf16[64,3584]{1,0:T(8,128)(2,1)} %bitcast.30.own), channel_id=1, source_target_pairs={{0,6},{1,3},{2,4},{3,1},{4,2},{5,7},{6,0},{7,5},{8,14},{9,11},{10,... | collective-permute-start | bytes 1376264 | tf_op jit(solution)/shard_map/ppermute | solution.py:37
  59.6 4.5 %collective-permute-start.6 = (bf16[64,3584]{1,0:T(8,128)(2,1)}, bf16[64,3584]{1,0:T(8,128)(2,1)}, u32[]{:S(2)}, u32[]{:S(2)}) collective-permute-start(bf16[64,3584]{1,0:T(8,128)(2,1)} %bitcast.30.own), channel_id=1, source_target_pairs={{0,3},{1,6},{2,1},{3,4},{4,7},{5,2},{6,5},{7,0},{8,11},{9,14},{10,... | collective-permute-start | bytes 1376264 | tf_op jit(solution)/shard_map/ppermute | solution.py:37
  64.1 1.2 convolution_convert_fusion
  65.2 5.2 %all-to-all-start.2 = ((bf16[4,16,3584]{2,1,0:T(8,128)(2,1)}), bf16[4,16,3584]{2,1,0:T(8,128)(2,1)}, u32[]{:S(2)}, u32[]{:S(2)}) async-start(bf16[4,16,3584]{2,1,0:T(8,128)(2,1)} %bitcast.38), calls=%async_computation.2 | async-start | bytes 917504 | tf_op jit(solution)/shard_map/all_to_all | solution.py:50
  70.5 1.2 pad_maximum_fusion.near_all
  72.1 1.2 copy-done.4
  73.3 6.8 %expert_work.2 = (bf16[64,3712]{1,0:T(8,128)(2,1)S(1)}, bf16[64,3712]{1,0:T(8,128)(2,1)}, bf16[64,3712]{1,0:T(8,128)(2,1)}, bf16[64,3712]{1,0:T(8,128)(2,1)}) custom-call(s32[3]{0:T(128)S(1)} %pad_add_fusion.pos, bf16[4,32,16,128]{3,2,1,0:T(8,128)(2,1)S(1)} %pad_maximum_fusion.near_all, bf16[4,16,16,128]{3,2,1,0:T(8,128)(2,1)S(1)} %bitcast.75, ...), custom_call_target="tpu_custom_call" | custom-call | tf_op jit(solution)/shard_map/expert_work/pallas_call | solution.py:165
  80.1 0.8 copy-done.6
  80.9 3.0 %collective-permute-start.10 = (bf16[64,3712]{1,0:T(8,128)(2,1)}, bf16[64,3712]{1,0:T(8,128)(2,1)}, u32[]{:S(2)}, u32[]{:S(2)}) collective-permute-start(bf16[64,3712]{1,0:T(8,128)(2,1)} %get-tuple-element.23), channel_id=1, source_target_pairs={{0,7},{1,2},{2,5},{3,0},{4,3},{5,6},{6,1},{7,4},{8,15},{9,10},{10,... | collective-permute-start | bytes 1425416 | tf_op jit(solution)/shard_map/ppermute | solution.py:37
  83.8 2.9 %collective-permute-start.8 = (bf16[64,3712]{1,0:T(8,128)(2,1)}, bf16[64,3712]{1,0:T(8,128)(2,1)}, u32[]{:S(2)}, u32[]{:S(2)}) collective-permute-start(bf16[64,3712]{1,0:T(8,128)(2,1)} %get-tuple-element.21), channel_id=1, source_target_pairs={{0,1},{1,0},{2,3},{3,2},{4,5},{5,4},{6,7},{7,6},{8,9},{9,8},{10,11... | collective-permute-start | bytes 1425416 | tf_op jit(solution)/shard_map/ppermute | solution.py:37
  86.8 3.3 %collective-permute-start.9 = (bf16[64,3712]{1,0:T(8,128)(2,1)}, bf16[64,3712]{1,0:T(8,128)(2,1)}, u32[]{:S(2)}, u32[]{:S(2)}) collective-permute-start(bf16[64,3712]{1,0:T(8,128)(2,1)} %get-tuple-element.22), channel_id=1, source_target_pairs={{0,6},{1,3},{2,4},{3,1},{4,2},{5,7},{6,0},{7,5},{8,14},{9,11},{10,... | collective-permute-start | bytes 1425416 | tf_op jit(solution)/shard_map/ppermute | solution.py:37
  90.1 2.5 %collective-permute-start.12 = (bf16[64,3584]{1,0:T(8,128)(2,1)}, bf16[64,3584]{1,0:T(8,128)(2,1)}, u32[]{:S(2)}, u32[]{:S(2)}) collective-permute-start(bf16[64,3584]{1,0:T(8,128)(2,1)} %bitcast.39.own), channel_id=1, source_target_pairs={{0,1},{1,0},{2,3},{3,2},{4,5},{5,4},{6,7},{7,6},{8,9},{9,8},{10,11... | collective-permute-start | bytes 1376264 | tf_op jit(solution)/shard_map/ppermute | solution.py:37
  92.6 3.1 %collective-permute-start.13 = (bf16[64,3584]{1,0:T(8,128)(2,1)}, bf16[64,3584]{1,0:T(8,128)(2,1)}, u32[]{:S(2)}, u32[]{:S(2)}) collective-permute-start(bf16[64,3584]{1,0:T(8,128)(2,1)} %bitcast.39.own), channel_id=1, source_target_pairs={{0,6},{1,3},{2,4},{3,1},{4,2},{5,7},{6,0},{7,5},{8,14},{9,11},{10,... | collective-permute-start | bytes 1376264 | tf_op jit(solution)/shard_map/ppermute | solution.py:37
  95.8 3.5 %collective-permute-start.14 = (bf16[64,3584]{1,0:T(8,128)(2,1)}, bf16[64,3584]{1,0:T(8,128)(2,1)}, u32[]{:S(2)}, u32[]{:S(2)}) collective-permute-start(bf16[64,3584]{1,0:T(8,128)(2,1)} %bitcast.39.own), channel_id=1, source_target_pairs={{0,3},{1,6},{2,1},{3,4},{4,7},{5,2},{6,5},{7,0},{8,11},{9,14},{10,... | collective-permute-start | bytes 1376264 | tf_op jit(solution)/shard_map/ppermute | solution.py:37
  99.3 2.5 %add_convert_fusion = bf16[64,3712]{1,0:T(8,128)(2,1)} fusion(bf16[64,3712]{1,0:T(8,128)(2,1)} %collective-permute-done.10, bf16[64,3712]{1,0:T(8,128)(2,1)} %collective-permute-done.9, bf16[64,3712]{1,0:T(8,128)(2,1)} %collective-permute-done.8, bf16[64,3712]{1,0:T(8,128)(2,1)} %copy-done.6), kind=kLoop, calls=%fused_computation.6 | loop fusion | flops 1900544 | bytes 2375680 | tf_op jit(solution)/shard_map/convert_element_type | solution.py:250
  101.8 5.6 %all-to-all-start.1 = ((bf16[4,16,3712]{2,1,0:T(8,128)(2,1)}), bf16[4,16,3712]{2,1,0:T(8,128)(2,1)}, u32[]{:S(2)}, u32[]{:S(2)}) async-start(bf16[4,16,3712]{2,1,0:T(8,128)(2,1)} %bitcast.81), calls=%async_computation.1 | async-start | bytes 950272 | tf_op jit(solution)/shard_map/all_to_all | solution.py:50
  107.7 1.2 copy-done.5
  108.9 6.8 %expert_work.3 = (bf16[64,3712]{1,0:T(8,128)(2,1)S(1)}, bf16[64,3712]{1,0:T(8,128)(2,1)}, bf16[64,3712]{1,0:T(8,128)(2,1)}, bf16[64,3712]{1,0:T(8,128)(2,1)}) custom-call(s32[3]{0:T(128)S(1)} %pad_add_fusion.pos, bf16[4,32,16,128]{3,2,1,0:T(8,128)(2,1)S(1)} %pad_maximum_fusion.near_all, bf16[4,16,16,128]{3,2,1,0:T(8,128)(2,1)S(1)} %bitcast.76, ...), custom_call_target="tpu_custom_call" | custom-call | tf_op jit(solution)/shard_map/expert_work/pallas_call | solution.py:165
  115.7 0.7 copy-done.7
  116.5 3.6 %collective-permute-start.15 = (bf16[64,3712]{1,0:T(8,128)(2,1)}, bf16[64,3712]{1,0:T(8,128)(2,1)S(1)}, u32[]{:S(2)}, u32[]{:S(2)}) collective-permute-start(bf16[64,3712]{1,0:T(8,128)(2,1)} %get-tuple-element.26), channel_id=1, source_target_pairs={{0,1},{1,0},{2,3},{3,2},{4,5},{5,4},{6,7},{7,6},{8,9},{9,8},{10,11... | collective-permute-start | bytes 1425416 | tf_op jit(solution)/shard_map/ppermute | solution.py:37
  120.1 1.9 %collective-permute-start.16 = (bf16[64,3712]{1,0:T(8,128)(2,1)}, bf16[64,3712]{1,0:T(8,128)(2,1)S(1)}, u32[]{:S(2)}, u32[]{:S(2)}) collective-permute-start(bf16[64,3712]{1,0:T(8,128)(2,1)} %get-tuple-element.27), channel_id=1, source_target_pairs={{0,6},{1,3},{2,4},{3,1},{4,2},{5,7},{6,0},{7,5},{8,14},{9,11},{10,... | collective-permute-start | bytes 1425416 | tf_op jit(solution)/shard_map/ppermute | solution.py:37
  122.0 3.0 %collective-permute-start.17 = (bf16[64,3712]{1,0:T(8,128)(2,1)}, bf16[64,3712]{1,0:T(8,128)(2,1)S(1)}, u32[]{:S(2)}, u32[]{:S(2)}) collective-permute-start(bf16[64,3712]{1,0:T(8,128)(2,1)} %get-tuple-element.28), channel_id=1, source_target_pairs={{0,7},{1,2},{2,5},{3,0},{4,3},{5,6},{6,1},{7,4},{8,15},{9,10},{10,... | collective-permute-start | bytes 1425416 | tf_op jit(solution)/shard_map/ppermute | solution.py:37
  125.2 0.7 copy-done.13
  126.0 4.0 %collective-permute-done.16 = bf16[64,3712]{1,0:T(8,128)(2,1)S(1)} collective-permute-done((bf16[64,3712]{1,0:T(8,128)(2,1)}, bf16[64,3712]{1,0:T(8,128)(2,1)S(1)}, u32[]{:S(2)}, u32[]{:S(2)}) %collective-permute-start.16) | collective-permute-done | bytes 475168 | tf_op jit(solution)/shard_map/ppermute | solution.py:37
  130.0 6.5 %collective-permute-done.17 = bf16[64,3712]{1,0:T(8,128)(2,1)S(1)} collective-permute-done((bf16[64,3712]{1,0:T(8,128)(2,1)}, bf16[64,3712]{1,0:T(8,128)(2,1)S(1)}, u32[]{:S(2)}, u32[]{:S(2)}) %collective-permute-start.17) | collective-permute-done | bytes 475168 | tf_op jit(solution)/shard_map/ppermute | solution.py:37
  136.4 1.0 copy-done.8
  137.5 0.8 total_blocks.1
  138.3 4.0 %collective-permute-start.18 = (bf16[16,3712]{1,0:T(8,128)(2,1)S(1)}, bf16[16,3712]{1,0:T(8,128)(2,1)S(1)}, u32[]{:S(2)}, u32[]{:S(2)}) collective-permute-start(bf16[16,3712]{1,0:T(8,128)(2,1)S(1)} %get-tuple-element.30), channel_id=1, source_target_pairs={{0,8},{1,9},{2,10},{3,11},{4,12},{5,13},{6,14},{7,15},{8,16},{9,17... | collective-permute-start | bytes 356360 | tf_op jit(solution)/shard_map/ppermute | solution.py:56
  142.3 5.5 %collective-permute-start.19 = (bf16[16,3712]{1,0:T(8,128)(2,1)S(1)}, bf16[16,3712]{1,0:T(8,128)(2,1)S(1)}, u32[]{:S(2)}, u32[]{:S(2)}) collective-permute-start(bf16[16,3712]{1,0:T(8,128)(2,1)S(1)} %get-tuple-element.31), channel_id=1, source_target_pairs={{0,16},{1,17},{2,18},{3,19},{4,20},{5,21},{6,22},{7,23},{8,24},{9,... | collective-permute-start | bytes 356360 | tf_op jit(solution)/shard_map/ppermute | solution.py:56
  147.9 4.1 %collective-permute-start.20 = (bf16[16,3712]{1,0:T(8,128)(2,1)S(1)}, bf16[16,3712]{1,0:T(8,128)(2,1)S(1)}, u32[]{:S(2)}, u32[]{:S(2)}) collective-permute-start(bf16[16,3712]{1,0:T(8,128)(2,1)S(1)} %get-tuple-element.32), channel_id=1, source_target_pairs={{0,24},{1,25},{2,26},{3,27},{4,28},{5,29},{6,30},{7,31},{8,0},{9,1... | collective-permute-start | bytes 356360 | tf_op jit(solution)/shard_map/ppermute | solution.py:56
  152.0 4.1 %collective-permute-done.19.refs_2_ = bf16[16,3712]{1,0:T(8,128)(2,1)S(1)} collective-permute-done((bf16[16,3712]{1,0:T(8,128)(2,1)S(1)}, bf16[16,3712]{1,0:T(8,128)(2,1)S(1)}, u32[]{:S(2)}, u32[]{:S(2)}) %collective-permute-start.19) | collective-permute-done | bytes 118816 | tf_op jit(solution)/shard_map/ppermute | solution.py:56
  156.1 6.1 %collective-permute-done.20.refs_3_ = bf16[16,3712]{1,0:T(8,128)(2,1)S(1)} collective-permute-done((bf16[16,3712]{1,0:T(8,128)(2,1)S(1)}, bf16[16,3712]{1,0:T(8,128)(2,1)S(1)}, u32[]{:S(2)}, u32[]{:S(2)}) %collective-permute-start.20) | collective-permute-done | bytes 118816 | tf_op jit(solution)/shard_map/ppermute | solution.py:56
  162.2 1.1 unpack.3
  163.2 2.1 %unpack.2 = (bf16[64,3584]{1,0:T(8,128)(2,1)}, f32[1,64]{1,0:T(1,128)}) custom-call(bf16[64,64]{1,0:T(8,128)(2,1)S(1)} %fusion.6.chosen, f32[64,1]{1,0:T(8,128)S(1)} %copy.17.probs, bf16[64,3712]{1,0:T(8,128)(2,1)} %bitcast.33.refs_0_), custom_call_target="tpu_custom_call" | custom-call | tf_op jit(solution)/shard_map/unpack/pallas_call | solution.py:219
  (59 shorter events, 1.8 us)
Async XLA Ops:
  0.6 20.8 %copy-start.11 = (bf16[1,512,128]{2,1,0:T(8,128)(2,1)S(1)}, bf16[1,512,128]{2,1,0:T(8,128)(2,1)}, u32[]{:S(2)}) copy-start(bf16[1,512,128]{2,1,0:T(8,128)(2,1)} %param.15) | copy-start | bytes 393220
  0.6 56.7 %collective-permute-start.11 = (bf16[1,64,3584]{2,1,0:T(8,128)(2,1)}, bf16[1,64,3584]{2,1,0:T(8,128)(2,1)S(1)}, u32[]{:S(2)}, u32[]{:S(2)}) collective-permute-start(bf16[1,64,3584]{2,1,0:T(8,128)(2,1)} %param.18), channel_id=1, source_target_pairs={{0,32},{32,64},{64,96},{96,128},{128,160},{160,192},{192,224},{224... | collective-permute-start | bytes 1376264 | tf_op jit(solution)/shard_map/ppermute | solution.py:78
  5.6 54.0 %collective-permute-start.1 = (bf16[3584,128]{1,0:T(8,128)(2,1)}, bf16[3584,128]{1,0:T(8,128)(2,1)S(1)}, u32[]{:S(2)}, u32[]{:S(2)}) collective-permute-start(bf16[3584,128]{1,0:T(8,128)(2,1)} %bitcast.66), channel_id=1, source_target_pairs={{0,2},{1,7},{2,0},{3,5},{4,6},{5,3},{6,4},{7,1},{8,10},{9,15},{10,... | collective-permute-start | bytes 2752520 | tf_op jit(solution)/shard_map/ppermute | solution.py:37
  10.0 61.7 %collective-permute-start.2 = (bf16[3584,128]{1,0:T(8,128)(2,1)}, bf16[3584,128]{1,0:T(8,128)(2,1)}, u32[]{:S(2)}, u32[]{:S(2)}) collective-permute-start(bf16[3584,128]{1,0:T(8,128)(2,1)} %bitcast.69), channel_id=1, source_target_pairs={{0,2},{1,7},{2,0},{3,5},{4,6},{5,3},{6,4},{7,1},{8,10},{9,15},{10,... | collective-permute-start | bytes 2752520 | tf_op jit(solution)/shard_map/ppermute | solution.py:37
  12.1 59.6 %collective-permute-start.7 = (bf16[128,3584]{1,0:T(8,128)(2,1)}, bf16[128,3584]{1,0:T(8,128)(2,1)}, u32[]{:S(2)}, u32[]{:S(2)}) collective-permute-start(bf16[128,3584]{1,0:T(8,128)(2,1)} %bitcast.72), channel_id=1, source_target_pairs={{0,2},{1,7},{2,0},{3,5},{4,6},{5,3},{6,4},{7,1},{8,10},{9,15},{10,... | collective-permute-start | bytes 2752520 | tf_op jit(solution)/shard_map/ppermute | solution.py:37
  16.5 13.5 %collective-permute-start.3 = (bf16[1,64,3584]{2,1,0:T(8,128)(2,1)}, bf16[1,64,3584]{2,1,0:T(8,128)(2,1)S(1)}, u32[]{:S(2)}, u32[]{:S(2)}) collective-permute-start(bf16[1,64,3584]{2,1,0:T(8,128)(2,1)} %param.17), channel_id=1, source_target_pairs={{0,480},{32,0},{64,32},{96,64},{128,96},{160,128},{192,160},{224,1... | collective-permute-start | bytes 1376264 | tf_op jit(solution)/shard_map/ppermute | solution.py:78
  21.5 0.9 copy-start.15
  21.5 1.1 copy-start.10
  22.3 0.9 copy-start.9
  31.1 22.2 %all-to-all-start = ((bf16[4,16,3584]{2,1,0:T(8,128)(2,1)}), bf16[4,16,3584]{2,1,0:T(8,128)(2,1)}, u32[]{:S(2)}, u32[]{:S(2)}) async-start(bf16[4,16,3584]{2,1,0:T(8,128)(2,1)} %bitcast.29), calls=%async_computation | async-start | bytes 917504 | tf_op jit(solution)/shard_map/all_to_all | solution.py:50
  41.9 2.0 %copy-start.14 = (s32[1,64,1]{1,2,0:T(1,128)S(1)}, s32[1,64,1]{1,2,0:T(1,128)}, u32[]{:S(2)}) copy-start(s32[1,64,1]{1,2,0:T(1,128)} %param.20) | copy-start | bytes 772
  41.9 8.6 %collective-permute-start = (bf16[4,2,4,2,16,128]{5,4,3,2,1,0:T(8,128)(2,1)S(1)}, bf16[4,2,4,2,16,128]{5,4,3,2,1,0:T(8,128)(2,1)S(1)}, u32[]{:S(2)}, u32[]{:S(2)}) collective-permute-start(bf16[4,2,4,2,16,128]{5,4,3,2,1,0:T(8,128)(2,1)S(1)} %pad_maximum_fusion.1), channel_id=1, source_target_pairs={{0,2},{1,7},{2,0},{3,5},{4,6},{5,3},{6,4},{7,1},{8,10},{9,15},{10,... | collective-permute-start | bytes 786440 | tf_op jit(solution)/shard_map/ppermute | solution.py:37
  53.4 18.3 %collective-permute-start.4 = (bf16[64,3584]{1,0:T(8,128)(2,1)}, bf16[64,3584]{1,0:T(8,128)(2,1)}, u32[]{:S(2)}, u32[]{:S(2)}) collective-permute-start(bf16[64,3584]{1,0:T(8,128)(2,1)} %bitcast.30.own), channel_id=1, source_target_pairs={{0,1},{1,0},{2,3},{3,2},{4,5},{5,4},{6,7},{7,6},{8,9},{9,8},{10,11... | collective-permute-start | bytes 1376264 | tf_op jit(solution)/shard_map/ppermute | solution.py:37
  57.4 14.4 %collective-permute-start.5 = (bf16[64,3584]{1,0:T(8,128)(2,1)}, bf16[64,3584]{1,0:T(8,128)(2,1)}, u32[]{:S(2)}, u32[]{:S(2)}) collective-permute-start(bf16[64,3584]{1,0:T(8,128)(2,1)} %bitcast.30.own), channel_id=1, source_target_pairs={{0,6},{1,3},{2,4},{3,1},{4,2},{5,7},{6,0},{7,5},{8,14},{9,11},{10,... | collective-permute-start | bytes 1376264 | tf_op jit(solution)/shard_map/ppermute | solution.py:37
  59.6 5.6 %copy-start.3 = (bf16[3584,128]{1,0:T(8,128)(2,1)}, bf16[3584,128]{1,0:T(8,128)(2,1)S(1)}, u32[]{:S(2)}) copy-start(bf16[3584,128]{1,0:T(8,128)(2,1)S(1)} %collective-permute-done.1.wg_away) | copy-start | bytes 2752516
  59.6 12.5 %collective-permute-start.6 = (bf16[64,3584]{1,0:T(8,128)(2,1)}, bf16[64,3584]{1,0:T(8,128)(2,1)}, u32[]{:S(2)}, u32[]{:S(2)}) collective-permute-start(bf16[64,3584]{1,0:T(8,128)(2,1)} %bitcast.30.own), channel_id=1, source_target_pairs={{0,3},{1,6},{2,1},{3,4},{4,7},{5,2},{6,5},{7,0},{8,11},{9,14},{10,... | collective-permute-start | bytes 1376264 | tf_op jit(solution)/shard_map/ppermute | solution.py:37
  64.1 8.0 %copy-start.2 = (bf16[1,128,3584]{2,1,0:T(8,128)(2,1)S(1)}, bf16[1,128,3584]{2,1,0:T(8,128)(2,1)}, u32[]{:S(2)}) copy-start(bf16[1,128,3584]{2,1,0:T(8,128)(2,1)} %param.25) | copy-start | bytes 2752516
  65.2 6.9 %copy-start = (bf16[1,3584,128]{2,1,0:T(8,128)(2,1)S(1)}, bf16[1,3584,128]{2,1,0:T(8,128)(2,1)}, u32[]{:S(2)}) copy-start(bf16[1,3584,128]{2,1,0:T(8,128)(2,1)} %param.23) | copy-start | bytes 2752516
  65.2 6.9 %copy-start.1 = (bf16[1,3584,128]{2,1,0:T(8,128)(2,1)S(1)}, bf16[1,3584,128]{2,1,0:T(8,128)(2,1)}, u32[]{:S(2)}) copy-start(bf16[1,3584,128]{2,1,0:T(8,128)(2,1)} %param.24) | copy-start | bytes 2752516
  65.2 24.8 %all-to-all-start.2 = ((bf16[4,16,3584]{2,1,0:T(8,128)(2,1)}), bf16[4,16,3584]{2,1,0:T(8,128)(2,1)}, u32[]{:S(2)}, u32[]{:S(2)}) async-start(bf16[4,16,3584]{2,1,0:T(8,128)(2,1)} %bitcast.38), calls=%async_computation.2 | async-start | bytes 917504 | tf_op jit(solution)/shard_map/all_to_all | solution.py:50
  72.1 1.2 copy-start.4
  80.1 0.8 copy-start.6
  80.9 14.9 %collective-permute-start.10 = (bf16[64,3712]{1,0:T(8,128)(2,1)}, bf16[64,3712]{1,0:T(8,128)(2,1)}, u32[]{:S(2)}, u32[]{:S(2)}) collective-permute-start(bf16[64,3712]{1,0:T(8,128)(2,1)} %get-tuple-element.23), channel_id=1, source_target_pairs={{0,7},{1,2},{2,5},{3,0},{4,3},{5,6},{6,1},{7,4},{8,15},{9,10},{10,... | collective-permute-start | bytes 1425416 | tf_op jit(solution)/shard_map/ppermute | solution.py:37
  83.8 15.5 %collective-permute-start.8 = (bf16[64,3712]{1,0:T(8,128)(2,1)}, bf16[64,3712]{1,0:T(8,128)(2,1)}, u32[]{:S(2)}, u32[]{:S(2)}) collective-permute-start(bf16[64,3712]{1,0:T(8,128)(2,1)} %get-tuple-element.21), channel_id=1, source_target_pairs={{0,1},{1,0},{2,3},{3,2},{4,5},{5,4},{6,7},{7,6},{8,9},{9,8},{10,11... | collective-permute-start | bytes 1425416 | tf_op jit(solution)/shard_map/ppermute | solution.py:37
  86.8 12.5 %collective-permute-start.9 = (bf16[64,3712]{1,0:T(8,128)(2,1)}, bf16[64,3712]{1,0:T(8,128)(2,1)}, u32[]{:S(2)}, u32[]{:S(2)}) collective-permute-start(bf16[64,3712]{1,0:T(8,128)(2,1)} %get-tuple-element.22), channel_id=1, source_target_pairs={{0,6},{1,3},{2,4},{3,1},{4,2},{5,7},{6,0},{7,5},{8,14},{9,11},{10,... | collective-permute-start | bytes 1425416 | tf_op jit(solution)/shard_map/ppermute | solution.py:37
  90.1 17.3 %collective-permute-start.12 = (bf16[64,3584]{1,0:T(8,128)(2,1)}, bf16[64,3584]{1,0:T(8,128)(2,1)}, u32[]{:S(2)}, u32[]{:S(2)}) collective-permute-start(bf16[64,3584]{1,0:T(8,128)(2,1)} %bitcast.39.own), channel_id=1, source_target_pairs={{0,1},{1,0},{2,3},{3,2},{4,5},{5,4},{6,7},{7,6},{8,9},{9,8},{10,11... | collective-permute-start | bytes 1376264 | tf_op jit(solution)/shard_map/ppermute | solution.py:37
  92.6 14.8 %collective-permute-start.13 = (bf16[64,3584]{1,0:T(8,128)(2,1)}, bf16[64,3584]{1,0:T(8,128)(2,1)}, u32[]{:S(2)}, u32[]{:S(2)}) collective-permute-start(bf16[64,3584]{1,0:T(8,128)(2,1)} %bitcast.39.own), channel_id=1, source_target_pairs={{0,6},{1,3},{2,4},{3,1},{4,2},{5,7},{6,0},{7,5},{8,14},{9,11},{10,... | collective-permute-start | bytes 1376264 | tf_op jit(solution)/shard_map/ppermute | solution.py:37
  95.8 12.0 %collective-permute-start.14 = (bf16[64,3584]{1,0:T(8,128)(2,1)}, bf16[64,3584]{1,0:T(8,128)(2,1)}, u32[]{:S(2)}, u32[]{:S(2)}) collective-permute-start(bf16[64,3584]{1,0:T(8,128)(2,1)} %bitcast.39.own), channel_id=1, source_target_pairs={{0,3},{1,6},{2,1},{3,4},{4,7},{5,2},{6,5},{7,0},{8,11},{9,14},{10,... | collective-permute-start | bytes 1376264 | tf_op jit(solution)/shard_map/ppermute | solution.py:37
  101.8 61.4 %all-to-all-start.1 = ((bf16[4,16,3712]{2,1,0:T(8,128)(2,1)}), bf16[4,16,3712]{2,1,0:T(8,128)(2,1)}, u32[]{:S(2)}, u32[]{:S(2)}) async-start(bf16[4,16,3712]{2,1,0:T(8,128)(2,1)} %bitcast.81), calls=%async_computation.1 | async-start | bytes 950272 | tf_op jit(solution)/shard_map/all_to_all | solution.py:50
  107.7 1.2 copy-start.5
  115.7 0.8 copy-start.7
  116.5 9.5 %collective-permute-start.15 = (bf16[64,3712]{1,0:T(8,128)(2,1)}, bf16[64,3712]{1,0:T(8,128)(2,1)S(1)}, u32[]{:S(2)}, u32[]{:S(2)}) collective-permute-start(bf16[64,3712]{1,0:T(8,128)(2,1)} %get-tuple-element.26), channel_id=1, source_target_pairs={{0,1},{1,0},{2,3},{3,2},{4,5},{5,4},{6,7},{7,6},{8,9},{9,8},{10,11... | collective-permute-start | bytes 1425416 | tf_op jit(solution)/shard_map/ppermute | solution.py:37
  120.1 9.9 %collective-permute-start.16 = (bf16[64,3712]{1,0:T(8,128)(2,1)}, bf16[64,3712]{1,0:T(8,128)(2,1)S(1)}, u32[]{:S(2)}, u32[]{:S(2)}) collective-permute-start(bf16[64,3712]{1,0:T(8,128)(2,1)} %get-tuple-element.27), channel_id=1, source_target_pairs={{0,6},{1,3},{2,4},{3,1},{4,2},{5,7},{6,0},{7,5},{8,14},{9,11},{10,... | collective-permute-start | bytes 1425416 | tf_op jit(solution)/shard_map/ppermute | solution.py:37
  122.0 3.1 %copy-start.12 = (f32[1,64,1]{1,2,0:T(1,128)S(1)}, f32[1,64,1]{1,2,0:T(1,128)}, u32[]{:S(2)}) copy-start(f32[1,64,1]{1,2,0:T(1,128)} %param.22) | copy-start | bytes 772
  122.0 14.4 %collective-permute-start.17 = (bf16[64,3712]{1,0:T(8,128)(2,1)}, bf16[64,3712]{1,0:T(8,128)(2,1)S(1)}, u32[]{:S(2)}, u32[]{:S(2)}) collective-permute-start(bf16[64,3712]{1,0:T(8,128)(2,1)} %get-tuple-element.28), channel_id=1, source_target_pairs={{0,7},{1,2},{2,5},{3,0},{4,3},{5,6},{6,1},{7,4},{8,15},{9,10},{10,... | collective-permute-start | bytes 1425416 | tf_op jit(solution)/shard_map/ppermute | solution.py:37
  125.2 0.7 copy-start.13
  136.4 1.0 copy-start.8
  138.3 13.7 %collective-permute-start.18 = (bf16[16,3712]{1,0:T(8,128)(2,1)S(1)}, bf16[16,3712]{1,0:T(8,128)(2,1)S(1)}, u32[]{:S(2)}, u32[]{:S(2)}) collective-permute-start(bf16[16,3712]{1,0:T(8,128)(2,1)S(1)} %get-tuple-element.30), channel_id=1, source_target_pairs={{0,8},{1,9},{2,10},{3,11},{4,12},{5,13},{6,14},{7,15},{8,16},{9,17... | collective-permute-start | bytes 356360 | tf_op jit(solution)/shard_map/ppermute | solution.py:56
  142.3 13.8 %collective-permute-start.19 = (bf16[16,3712]{1,0:T(8,128)(2,1)S(1)}, bf16[16,3712]{1,0:T(8,128)(2,1)S(1)}, u32[]{:S(2)}, u32[]{:S(2)}) collective-permute-start(bf16[16,3712]{1,0:T(8,128)(2,1)S(1)} %get-tuple-element.31), channel_id=1, source_target_pairs={{0,16},{1,17},{2,18},{3,19},{4,20},{5,21},{6,22},{7,23},{8,24},{9,... | collective-permute-start | bytes 356360 | tf_op jit(solution)/shard_map/ppermute | solution.py:56
  147.9 14.3 %collective-permute-start.20 = (bf16[16,3712]{1,0:T(8,128)(2,1)S(1)}, bf16[16,3712]{1,0:T(8,128)(2,1)S(1)}, u32[]{:S(2)}, u32[]{:S(2)}) collective-permute-start(bf16[16,3712]{1,0:T(8,128)(2,1)S(1)} %get-tuple-element.32), channel_id=1, source_target_pairs={{0,24},{1,25},{2,26},{3,27},{4,28},{5,29},{6,30},{7,31},{8,0},{9,1... | collective-permute-start | bytes 356360 | tf_op jit(solution)/shard_map/ppermute | solution.py:56
